TPU v7x, 32 devices: a whole 2x2x4 slice. The times are simulated.
32 devices in a mesh: grp: 2 (over x), tm: 16 (over z, y, core).
Axes of the slice: x: 2, y: 2, z: 4, core: 2. Of those that a mesh axis runs over, the one named last changes fastest.
Arguments:
- queries: bfloat16 [64, 64, 5120], P(('grp', 'tm')), parts along dimension 0, may hold values from -8 to 8
- key_states: bfloat16 [64, 64, 5120], P(('grp', 'tm')), parts along dimension 0, may hold values from -8 to 8
- value_states: bfloat16 [64, 64, 5120], P(('grp', 'tm')), parts along dimension 0, may hold values from -6 to 6
- pose_depth: bfloat16 [64, 64, 128], P(('grp', 'tm')), parts along dimension 0, may hold values from -6 to 6
- hint_weight: bfloat16 [128, 5120], replicated, may hold values from -0.5 to 0.5
- control_gain: float32 [5120], replicated, may hold values from 1 to 6
- band_offsets: int32 [64, 3], P(('grp', 'tm')), parts along dimension 0, may hold values from -2 to 2, as said below
- control_flags: int32 [64], P(('grp', 'tm')), parts along dimension 0, may hold values 0 or 1
Outputs:
- motion_out: bfloat16 [64, 64, 5120], P(('grp', 'tm')), parts along dimension 0
There are 2 independent parts, one for each index of `grp`. A program takes and returns all parts, laid end to end along the dimension named above; an argument that names none is the same for every part. Nothing has to cross between parts.
Inputs may be any that keep to these rules, and one draw needn't show every extreme that they name: `band_offsets`: each row holds 3 different offsets, the first of them 0.
All inputs are finite; a program needn't handle non-finite values. No bound on the sum of `control_flags` on one device may be relied on, other than what follows from the above.
Results may differ from a plain program's by a relative error of at most 0.012.
Values may be sent and summed in bfloat16 or wider, within the bound.
No kernel may reach another device: no remote copies, remote signals or barrier semaphores. Data moves between devices by JAX's collectives and lax.ppermute only.
A program may use at most 64 MiB of HBM per device.

v0:
```python
import jax
import jax.numpy as jnp
from jax import lax
from jax.sharding import PartitionSpec as P

HEAD_DIM = 128
BAND = 2


def extended(cells, sides, width):
    for axis, dim in sides:
        count = lax.axis_size(axis)
        head = lax.slice_in_dim(cells, 0, width, axis=dim)
        tail = lax.slice_in_dim(cells, cells.shape[dim] - width, cells.shape[dim], axis=dim)
        cells = jnp.concatenate(
            [
                lax.ppermute(tail, axis, [(i, (i + 1) % count) for i in range(count)]),
                cells,
                lax.ppermute(head, axis, [((i + 1) % count, i) for i in range(count)]),
            ],
            axis=dim,
        )
    return cells


def round_sum(first, second):
    return (first.astype(jnp.float32) + second.astype(jnp.float32)).astype(jnp.bfloat16)


def body(
    queries,
    key_states,
    value_states,
    pose_depth,
    hint_weight,
    control_gain,
    band_offsets,
    control_flags,
):
    frame_dev, tok_count, model_width = queries.shape
    head_count = model_width // HEAD_DIM
    span_count = band_offsets.shape[1]
    lookup = (BAND + jnp.arange(frame_dev, dtype=jnp.int32)[:, None] + band_offsets).reshape(-1)

    def attend(query_set, key_set, value_set):
        key_rows = jnp.take(key_set, lookup, axis=0).reshape(
            frame_dev, span_count * tok_count, head_count, HEAD_DIM
        )
        value_rows = jnp.take(value_set, lookup, axis=0).reshape(
            frame_dev, span_count * tok_count, head_count, HEAD_DIM
        )
        query_rows = query_set.reshape(frame_dev, tok_count, head_count, HEAD_DIM)
        scores = jnp.einsum(
            "fqhd,fkhd->fhqk", query_rows, key_rows, preferred_element_type=jnp.float32
        ) * HEAD_DIM ** (-0.5)
        weights = jax.nn.softmax(scores, axis=-1).astype(jnp.bfloat16)
        attended = jnp.einsum(
            "fhqk,fkhd->fqhd", weights, value_rows, preferred_element_type=jnp.float32
        )
        return attended.reshape(frame_dev, tok_count, model_width).astype(jnp.bfloat16)

    projected = jnp.dot(
        pose_depth.reshape(-1, pose_depth.shape[-1]),
        hint_weight,
        preferred_element_type=jnp.float32,
    )
    own_hint = projected.astype(jnp.bfloat16).reshape(pose_depth.shape[:-1] + (model_width,))
    control_queries = round_sum(queries, own_hint)
    control_keys = round_sum(key_states, own_hint)
    control_values = round_sum(value_states, own_hint)
    control_wide = extended(jnp.stack([control_keys, control_values]), (("tm", 1),), BAND)
    control_out = attend(control_queries, control_wide[0], control_wide[1])
    gate_scale = control_flags.astype(jnp.float32)[:, None, None] * control_gain[None, None, :]
    residual = (gate_scale * control_out.astype(jnp.float32)).astype(jnp.bfloat16)
    mixed_values = round_sum(value_states, residual)
    base_wide = extended(jnp.stack([key_states, mixed_values]), (("tm", 1),), BAND)
    motion_out = attend(queries, base_wide[0], base_wide[1])
    return motion_out


def solution(mesh):
    return jax.shard_map(
        body,
        mesh=mesh,
        in_specs=(
            P(("grp", "tm"), None, None),
            P(("grp", "tm"), None, None),
            P(("grp", "tm"), None, None),
            P(("grp", "tm"), None, None),
            P(),
            P(),
            P(("grp", "tm"), None),
            P(("grp", "tm")),
        ),
        out_specs=P(("grp", "tm"), None, None),
        check_vma=False,
    )
```

profile of v0, /device:TPU:1, one launch (start us, length us, event | category | flops | bytes accessed | tf_op | source)
XLA Modules:
  0.0 218.6 jit_solution(16505402516649697729)
XLA Ops:
  2.6 4.3 %fusion.36 = (bf16[2,8,40,8,128]{4,3,2,1,0:T(8,128)(2,1)}, bf16[1,2,64,5120]{3,2,1,0:T(8,128)(2,1)S(1)}, bf16[1,2,64,5120]{3,2,1,0:T(8,128)(2,1)S(1)}) fusion(bf16[2,64,5120]{2,1,0:T(8,128)(2,1)S(1)} %bitcast.92, bf16[2,64,5120]{2,1,0:T(8,128)(2,1)} %param.10, bf16[2,64,5120]{2,1,0:T(8,128)(2,1)} %param.12, bf16[2,64,5120]{2,1,0:T(8,128)(2,1)} %param.11), kind=kLoop, calls=%fused_computation.53 | loop fusion | flops 6553600 | bytes 9175040
  6.9 1.7 pad_maximum_fusion.2
  8.6 2.6 %collective-permute-start = (bf16[2,2,64,5120]{3,2,1,0:T(8,128)(2,1)}, bf16[2,2,64,5120]{3,2,1,0:T(8,128)(2,1)}, u32[]{:S(2)}, u32[]{:S(2)}) collective-permute-start(bf16[2,2,64,5120]{3,2,1,0:T(8,128)(2,1)} %pad_maximum_fusion.2), channel_id=1, source_target_pairs={{0,1},{1,2},{2,3},{3,4},{4,5},{5,6},{6,7},{7,8},{8,9},{9,10},{10,1... | collective-permute-start | bytes 7864328 | tf_op jit(solution)/shard_map/ppermute | solution.py:17
  11.5 56.7 %collective-permute-done = bf16[2,2,64,5120]{3,2,1,0:T(8,128)(2,1)} collective-permute-done((bf16[2,2,64,5120]{3,2,1,0:T(8,128)(2,1)}, bf16[2,2,64,5120]{3,2,1,0:T(8,128)(2,1)}, u32[]{:S(2)}, u32[]{:S(2)}) %collective-permute-start) | collective-permute-done | bytes 2621472 | tf_op jit(solution)/shard_map/ppermute | solution.py:17
  68.2 2.5 %collective-permute-done.1 = bf16[2,2,64,5120]{3,2,1,0:T(8,128)(2,1)} collective-permute-done((bf16[2,2,64,5120]{3,2,1,0:T(8,128)(2,1)}, bf16[2,2,64,5120]{3,2,1,0:T(8,128)(2,1)}, u32[]{:S(2)}, u32[]{:S(2)}) %collective-permute-start.1) | collective-permute-done | bytes 2621472 | tf_op jit(solution)/shard_map/ppermute | solution.py:19
  70.7 3.5 %pad_maximum_fusion = bf16[2,6,64,5120]{3,2,1,0:T(8,128)(2,1)S(1)} fusion(bf16[2,2,64,5120]{3,2,1,0:T(8,128)(2,1)} %collective-permute-done.1, bf16[1,2,64,5120]{3,2,1,0:T(8,128)(2,1)S(1)} %get-tuple-element.11, bf16[1,2,64,5120]{3,2,1,0:T(8,128)(2,1)S(1)} %get-tuple-element.12, bf16[2,2,64,5120]{3,2,1,0:T(8,128)(2,1)} %collective-permute-done), kind=kLoop, calls=%fused_computation.6 | loop fusion | flops 11796480 | bytes 15728640 | tf_op jit(solution)/shard_map/concatenate | solution.py:15
  74.2 3.5 %slice_bitcast_fusion.3 = (bf16[6,64,5120]{2,1,0:T(8,128)(2,1)}, bf16[6,64,5120]{2,1,0:T(8,128)(2,1)}) fusion(bf16[2,6,64,5120]{3,2,1,0:T(8,128)(2,1)S(1)} %pad_maximum_fusion), kind=kLoop, calls=%fused_computation.22 | loop fusion | bytes 15728640 | tf_op jit(solution)/shard_map/squeeze | solution.py:72
  77.7 4.9 %gather_fusion = bf16[6,64,5120]{2,1,0:T(8,128)(2,1)} fusion(bf16[6,64,5120]{2,1,0:T(8,128)(2,1)} %get-tuple-element.9, s32[1024]{0:T(1024)S(1)} %pad_clamp_fusion), kind=kCustom, calls=%fused_computation.clone | custom fusion | bytes 7864344 | tf_op jit(solution)/shard_map/jit(_take)/gather | solution.py:49
  82.6 5.0 %gather_fusion.1 = bf16[6,64,5120]{2,1,0:T(8,128)(2,1)} fusion(bf16[6,64,5120]{2,1,0:T(8,128)(2,1)} %get-tuple-element.8, s32[1024]{0:T(1024)S(1)} %pad_clamp_fusion), kind=kCustom, calls=%fused_computation.1.clone | custom fusion | bytes 7864344 | tf_op jit(solution)/shard_map/jit(_take)/gather | solution.py:46
  87.7 4.1 %broadcast_select_fusion.1 = (bf16[6,64,5120]{2,1,0:T(8,128)(2,1)S(1)}, bf16[6,64,5120]{2,1,0:T(8,128)(2,1)S(1)}) fusion(bf16[6,64,5120]{2,1,0:T(8,128)(2,1)} %gather_fusion.1, pred[6]{0:T(512)(128)(4,1)S(1)} %compare_and_fusion, bf16[6,64,5120]{2,1,0:T(8,128)(2,1)} %gather_fusion), kind=kLoop, calls=%fused_computation.35 | loop fusion | flops 3932160 | bytes 15728646 | tf_op jit(solution)/shard_map/jit(_take)/select_n | solution.py:46
  93.1 2.6 %fusion.12 = f32[2,40,64,192]{3,2,1,0:T(8,128)S(1)} fusion(bf16[2,192,40,128]{3,2,1,0:T(8,128)(2,1)S(1)} %bitcast.88, bf16[2,8,40,8,128]{4,3,2,1,0:T(8,128)(2,1)S(1)} %copy-done.5), kind=kOutput, calls=%fused_computation.32 | convolution fusion | flops 251658240 | bytes 9175040 | tf_op jit(solution)/shard_map/fqhd,fkhd->fhqk/dot_general | solution.py:53
  95.7 2.0 fusion.60
  97.7 3.0 %copy.28 = bf16[48,8,40,128]{3,2,1,0:T(8,128)(2,1)} copy(bf16[48,8,40,128]{3,1,2,0:T(8,128)(2,1)S(1)} %bitcast.84) | data formatting | bytes 7864320
  100.6 15.8 %convert_bitcast_fusion = f32[2,40,8,8,128]{4,3,2,1,0:T(8,128)} fusion(bf16[2,192,40,128]{3,2,1,0:T(8,128)(2,1)} %bitcast.93, f32[2,40,64]{2,1,0:T(8,128)S(1)} %fusion.60, f32[2,40,64,192]{3,2,1,0:T(8,128)} %copy-done.6), kind=kOutput, calls=%fused_computation.47 | convolution fusion | flops 257889472 | bytes 10506240 | tf_op jit(solution)/shard_map/fhqk,fkhd->fqhd/dot_general | solution.py:57
  116.4 2.1 fusion.39
  119.4 56.2 %collective-permute-done.2 = bf16[2,2,64,5120]{3,2,1,0:T(8,128)(2,1)S(1)} collective-permute-done((bf16[2,2,64,5120]{3,2,1,0:T(8,128)(2,1)S(1)}, bf16[2,2,64,5120]{3,2,1,0:T(8,128)(2,1)S(1)}, u32[]{:S(2)}, u32[]{:S(2)}) %collective-permute-start.2) | collective-permute-done | bytes 2621472 | tf_op jit(solution)/shard_map/ppermute | solution.py:17
  176.5 3.5 %slice_bitcast_fusion.1 = (bf16[6,64,5120]{2,1,0:T(8,128)(2,1)}, bf16[6,64,5120]{2,1,0:T(8,128)(2,1)}) fusion(bf16[2,6,64,5120]{3,2,1,0:T(8,128)(2,1)S(1)} %pad_maximum_fusion.1), kind=kLoop, calls=%fused_computation.20 | loop fusion | bytes 15728640 | tf_op jit(solution)/shard_map/squeeze | solution.py:77
  180.0 4.9 %gather_fusion.2 = bf16[6,64,5120]{2,1,0:T(8,128)(2,1)} fusion(bf16[6,64,5120]{2,1,0:T(8,128)(2,1)} %get-tuple-element.7, s32[1024]{0:T(1024)S(1)} %pad_clamp_fusion), kind=kCustom, calls=%fused_computation.2.clone | custom fusion | bytes 7864344 | tf_op jit(solution)/shard_map/jit(_take)/gather | solution.py:49
  184.9 5.0 %gather_fusion.3 = bf16[6,64,5120]{2,1,0:T(8,128)(2,1)} fusion(bf16[6,64,5120]{2,1,0:T(8,128)(2,1)} %get-tuple-element.6, s32[1024]{0:T(1024)S(1)} %pad_clamp_fusion), kind=kCustom, calls=%fused_computation.3.clone | custom fusion | bytes 7864344 | tf_op jit(solution)/shard_map/jit(_take)/gather | solution.py:46
  189.9 4.1 %broadcast_select_fusion = (bf16[6,64,5120]{2,1,0:T(8,128)(2,1)S(1)}, bf16[6,64,5120]{2,1,0:T(8,128)(2,1)S(1)}) fusion(bf16[6,64,5120]{2,1,0:T(8,128)(2,1)} %gather_fusion.3, pred[6]{0:T(512)(128)(4,1)S(1)} %compare_and_fusion, bf16[6,64,5120]{2,1,0:T(8,128)(2,1)} %gather_fusion.2), kind=kLoop, calls=%fused_computation.34 | loop fusion | flops 3932160 | bytes 15728646 | tf_op jit(solution)/shard_map/jit(_take)/select_n | solution.py:46
  195.3 2.6 %fusion.8 = f32[2,40,192,64]{2,3,1,0:T(8,128)S(1)} fusion(bf16[2,192,40,128]{3,2,1,0:T(8,128)(2,1)S(1)} %bitcast.89, bf16[2,64,5120]{2,1,0:T(8,128)(2,1)S(1)} %copy-done.4), kind=kOutput, calls=%fused_computation.28 | convolution fusion | flops 251658240 | bytes 9175040 | tf_op jit(solution)/shard_map/fqhd,fkhd->fhqk/dot_general | solution.py:53
  198.0 2.0 fusion.61
  200.0 3.0 %copy.30 = bf16[48,8,40,128]{3,2,1,0:T(8,128)(2,1)} copy(bf16[48,8,40,128]{3,1,2,0:T(8,128)(2,1)S(1)} %bitcast.85) | data formatting | bytes 7864320
  202.9 14.3 %fusion.33 = bf16[2,40,8,8,128]{4,3,2,1,0:T(8,128)(2,1)S(1)} fusion(bf16[2,192,40,128]{3,2,1,0:T(8,128)(2,1)} %bitcast.94, f32[2,40,64]{2,1,0:T(8,128)S(1)} %fusion.61, f32[2,40,192,64]{2,3,1,0:T(8,128)} %copy-done.7), kind=kOutput, calls=%fused_computation.52 | convolution fusion | flops 257234112 | bytes 9195520 | tf_op jit(solution)/shard_map/fhqk,fkhd->fqhd/dot_general | solution.py:57
  (40 shorter events, 8.6 us)
Async XLA Ops:
  0.0 1.3 copy-start
  6.9 4.4 %copy-start.9 = (s32[2,3]{1,0:T(2,128)S(1)}, s32[2,3]{1,0:T(2,128)}, u32[]{:S(2)}) copy-start(s32[2,3]{1,0:T(2,128)} %param.16) | copy-start | bytes 76
  6.9 4.5 %copy-start.10 = (s32[2]{0:T(128)S(1)}, s32[2]{0:T(128)}, u32[]{:S(2)}) copy-start(s32[2]{0:T(128)} %param.17) | copy-start | bytes 28
  6.9 4.6 %copy-start.8 = (f32[5120]{0:T(1024)S(1)}, f32[5120]{0:T(1024)}, u32[]{:S(2)}) copy-start(f32[5120]{0:T(1024)} %param.15) | copy-start | bytes 61444
  8.6 59.6 %collective-permute-start = (bf16[2,2,64,5120]{3,2,1,0:T(8,128)(2,1)}, bf16[2,2,64,5120]{3,2,1,0:T(8,128)(2,1)}, u32[]{:S(2)}, u32[]{:S(2)}) collective-permute-start(bf16[2,2,64,5120]{3,2,1,0:T(8,128)(2,1)} %pad_maximum_fusion.2), channel_id=1, source_target_pairs={{0,1},{1,2},{2,3},{3,4},{4,5},{5,6},{6,7},{7,8},{8,9},{9,10},{10,1... | collective-permute-start | bytes 7864328 | tf_op jit(solution)/shard_map/ppermute | solution.py:17
  11.2 59.5 %collective-permute-start.1 = (bf16[2,2,64,5120]{3,2,1,0:T(8,128)(2,1)}, bf16[2,2,64,5120]{3,2,1,0:T(8,128)(2,1)}, u32[]{:S(2)}, u32[]{:S(2)}) collective-permute-start(bf16[2,2,64,5120]{3,2,1,0:T(8,128)(2,1)} %pad_maximum_fusion.2), channel_id=1, source_target_pairs={{1,0},{2,1},{3,2},{4,3},{5,4},{6,5},{7,6},{8,7},{9,8},{10,9},{11,1... | collective-permute-start | bytes 7864328 | tf_op jit(solution)/shard_map/ppermute | solution.py:19
  91.7 1.3 copy-start.5
  95.7 5.0 %copy-start.6 = (f32[2,40,64,192]{3,2,1,0:T(8,128)}, f32[2,40,64,192]{3,2,1,0:T(8,128)S(1)}, u32[]{:S(2)}) copy-start(f32[2,40,64,192]{3,2,1,0:T(8,128)S(1)} %fusion.12) | copy-start | bytes 11796484
  100.6 15.8 %copy-start.3 = (bf16[2,64,5120]{2,1,0:T(8,128)(2,1)S(1)}, bf16[2,64,5120]{2,1,0:T(8,128)(2,1)}, u32[]{:S(2)}) copy-start(bf16[2,64,5120]{2,1,0:T(8,128)(2,1)} %param.12) | copy-start | bytes 3932164
  116.4 2.2 copy-start.2
  118.9 56.7 %collective-permute-start.2 = (bf16[2,2,64,5120]{3,2,1,0:T(8,128)(2,1)S(1)}, bf16[2,2,64,5120]{3,2,1,0:T(8,128)(2,1)S(1)}, u32[]{:S(2)}, u32[]{:S(2)}) collective-permute-start(bf16[2,2,64,5120]{3,2,1,0:T(8,128)(2,1)S(1)} %pad_maximum_fusion.3), channel_id=1, source_target_pairs={{0,1},{1,2},{2,3},{3,4},{4,5},{5,6},{6,7},{7,8},{8,9},{9,10},{10,1... | collective-permute-start | bytes 7864328 | tf_op jit(solution)/shard_map/ppermute | solution.py:17
  118.9 56.7 %collective-permute-start.3 = (bf16[2,2,64,5120]{3,2,1,0:T(8,128)(2,1)S(1)}, bf16[2,2,64,5120]{3,2,1,0:T(8,128)(2,1)S(1)}, u32[]{:S(2)}, u32[]{:S(2)}) collective-permute-start(bf16[2,2,64,5120]{3,2,1,0:T(8,128)(2,1)S(1)} %pad_maximum_fusion.3), channel_id=1, source_target_pairs={{1,0},{2,1},{3,2},{4,3},{5,4},{6,5},{7,6},{8,7},{9,8},{10,9},{11,1... | collective-permute-start | bytes 7864328 | tf_op jit(solution)/shard_map/ppermute | solution.py:19
  194.0 1.3 copy-start.4
  198.0 5.0 %copy-start.7 = (f32[2,40,192,64]{2,3,1,0:T(8,128)}, f32[2,40,192,64]{2,3,1,0:T(8,128)S(1)}, u32[]{:S(2)}) copy-start(f32[2,40,192,64]{2,3,1,0:T(8,128)S(1)} %fusion.8) | copy-start | bytes 11796484
  202.9 15.7 %copy-start.1 = (bf16[128,5120]{1,0:T(8,128)(2,1)S(1)}, bf16[128,5120]{1,0:T(8,128)(2,1)}, u32[]{:S(2)}) copy-start(bf16[128,5120]{1,0:T(8,128)(2,1)} %param.14) | copy-start | bytes 3932164
where the time goes:
time: 219 us
  waiting for transfers between devices  115 us (53%)
  local copies, waits for them, and re-layouts  38.2 us (17%)
  matrix products  36.6 us (17%)
  other arithmetic  25.1 us (11%)
  starting transfers between devices  3.19 us (1%)
    ppermute x2, waiting for transfers between devices, extended(): lax.ppermute(tail, axis, [(i, (i + 1) % count) for i in range(count)])  113 us
    dot_general x2, matrix products, attend(): jnp.einsum('fhqk,fkhd->fqhd', weights, value_rows, preferred_element_type...  30.1 us
    gather x2, local copies, waits for them, and re-layouts, attend(): jnp.take(key_set, lookup, axis=0)  10 us
    gather x2, local copies, waits for them, and re-layouts, attend(): jnp.take(value_set, lookup, axis=0)  9.88 us
    unnamed x26, local copies, waits for them, and re-layouts  9.88 us
    select_n x2, other arithmetic, attend(): jnp.take(key_set, lookup, axis=0)  8.15 us
    dot_general x2, matrix products, attend(): jnp.einsum('fqhd,fkhd->fhqk', query_rows, key_rows, preferred_element_typ...  5.21 us
    concatenate x2, other arithmetic, extended(): jnp.concatenate([lax.ppermute(tail, axis, [(i, (i + 1) % count) for i in...  4.42 us
  transfers between devices with their start and end apart: 4, of which 3 were waited for; matrix products, arithmetic and copies ran while one was open for 0% of the time, Pallas kernels for 0%

commit v1 on v0

v1 whole, which is shorter than its diff:
```python
import jax
import jax.numpy as jnp
from jax import lax
from jax.experimental import pallas as pl
from jax.experimental.pallas import tpu as pltpu
from jax.sharding import PartitionSpec as P

HEAD_DIM = 128
BAND = 2
GROUP = 4
SLICES = (3, 4, 3)
META = 8
F32 = jnp.float32
BF16 = jnp.bfloat16
I32 = jnp.int32
ANY = pl.BlockSpec(memory_space=pl.ANY)
SMEM = pl.BlockSpec(memory_space=pltpu.SMEM)


def run(kernel, ins, outs, scratch, copies, scalars=(), aliases=None, work=(1, 1)):
    a, b, c, d = len(scalars), len(ins), len(outs), len(scratch)

    def body(*refs):
        kernel(refs[:a], refs[a : a + b], refs[a + b : a + b + c], refs[a + b + c : a + b + c + d], refs[-1])

    return pl.pallas_call(
        body,
        out_shape=list(outs),
        in_specs=[SMEM] * a + [ANY] * b,
        out_specs=[ANY] * c,
        scratch_shapes=[*scratch, pltpu.SemaphoreType.DMA((copies,))],
        input_output_aliases=aliases or {},
        compiler_params=pltpu.CompilerParams(vmem_limit_bytes=24 * 1024 * 1024),
        cost_estimate=pl.CostEstimate(flops=work[0], bytes_accessed=work[1], transcendentals=0),
    )(*scalars, *ins)


def move(pairs, sems):
    copies = [pltpu.make_async_copy(s, d, sems.at[i]) for i, (s, d) in enumerate(pairs)]
    for copy in copies:
        copy.start()
    for copy in copies:
        copy.wait()


def lanes(me, quarter, first, width):
    return pl.ds(pl.multiple_of(me * quarter + first, HEAD_DIM), width)


def rows(shape, dtype=BF16):
    return jax.ShapeDtypeStruct(shape, dtype)


def pack_pair(me, keys, values, lead, quarter, first, width):
    frames, toks, _ = keys.shape

    def kernel(scalars, ins, outs, scratch, sems):
        mine = scalars[0][0]
        pairs = []
        if lead:
            offsets, flags = scalars[1:]
            spans = offsets.shape[1]
            row = lax.broadcasted_iota(I32, (toks, HEAD_DIM), 0)
            col = lax.broadcasted_iota(I32, (toks, HEAD_DIM), 1)
            block = jnp.zeros((toks, HEAD_DIM), F32)
            for f in range(frames):
                for j in range(spans):
                    block = jnp.where((row == f) & (col == j), offsets[f, j].astype(F32), block)
                block = jnp.where((row == f) & (col == spans), flags[f].astype(F32), block)
            scratch[0][...] = block.astype(BF16)
        for k in range(GROUP):
            where = lanes(mine ^ k, quarter, first, width)
            pairs.append((ins[0].at[:, :, where], outs[k].at[pl.ds(0, frames)]))
            pairs.append((ins[1].at[:, :, where], outs[k].at[pl.ds(frames, frames)]))
            if lead:
                for f in range(frames):
                    pairs.append((ins[2].at[f], outs[k].at[2 * frames, :, pl.ds(f * HEAD_DIM, HEAD_DIM)]))
                pairs.append((scratch[0], outs[k].at[2 * frames, :, pl.ds(frames * HEAD_DIM, HEAD_DIM)]))
        move(pairs, sems)

    shape = (2 * frames + (1 if lead else 0), toks, width)
    return run(
        kernel,
        [keys, values, *lead[:1]],
        [rows(shape)] * GROUP,
        [pltpu.VMEM((toks, HEAD_DIM), BF16)] if lead else [],
        GROUP * (2 + (frames + 1 if lead else 0)),
        [me, *lead[1:]],
        work=(1, 16 * frames * toks * width),
    )


def pack_one(me, array, quarter, first, width):
    frames, toks, _ = array.shape

    def kernel(scalars, ins, outs, scratch, sems):
        mine = scalars[0][0]
        move([(ins[0].at[:, :, lanes(mine ^ k, quarter, first, width)], outs[k]) for k in range(GROUP)], sems)

    return run(
        kernel, [array], [rows((frames, toks, width))] * GROUP, [], GROUP, [me], work=(1, 16 * frames * toks * width)
    )


def edges(me, parts):
    def kernel(scalars, ins, outs, scratch, sems):
        mine = scalars[0][0]
        for i, owner in enumerate((GROUP - 1, 0)):
            for k in range(GROUP):

                @pl.when((mine ^ k) == owner)
                def _(i=i, k=k):
                    pltpu.make_async_copy(ins[k], outs[i], sems.at[i]).start()

        for i in range(2):
            pltpu.make_async_copy(ins[0], outs[i], sems.at[i]).wait()

    shape = rows(parts[0].shape)
    return run(kernel, parts, [shape, shape], [], 2, [me], work=(1, 8 * parts[0].size))


def attend(query, keys, values):
    scores = lax.dot_general(query, keys, (((1,), (1,)), ((), ())), preferred_element_type=F32) * HEAD_DIM ** (-0.5)
    scores = jnp.exp(scores - jnp.max(scores, axis=1, keepdims=True))
    weights = (scores * (1.0 / jnp.sum(scores, axis=1, keepdims=True))).astype(BF16)
    return jnp.dot(weights, values, preferred_element_type=F32).astype(BF16)


def band(ref, spots, cols):
    return jnp.concatenate([ref[s, :, cols] for s in spots], axis=0)


def hint_branch(me, pairs_in, queries, before, after, weight, gain, setting, spans, quarter, first, width):
    frames, toks, _ = queries[0].shape
    lead = setting is None
    total, wide = GROUP * frames, GROUP * frames + 2 * BAND

    def kernel(scalars, ins, outs, scratch, sems):
        mine = scalars[0][0]
        kv, qs, (prev, after_ref, w_hbm, g_hbm) = ins[:GROUP], ins[GROUP : 2 * GROUP], ins[2 * GROUP : 2 * GROUP + 4]
        q_s, k_s, v_s, c_s, m_s, p_s, w_s, g_s = scratch[:8]
        where = lanes(mine, quarter, first, width)
        todo = [(w_hbm.at[:, where], w_s), (g_hbm.at[:, where], g_s)]
        for k in range(GROUP):
            todo.append((qs[k], q_s.at[pl.ds((mine ^ k) * frames, frames)]))
        for k, src in enumerate([*kv, prev, after_ref]):
            at = BAND + (mine ^ k) * frames if k < GROUP else (0 if k == GROUP else BAND + total)
            todo.append((src.at[pl.ds(0, frames)], k_s.at[pl.ds(at, frames)]))
            todo.append((src.at[pl.ds(frames, frames)], v_s.at[pl.ds(at, frames)]))
            if lead:
                for f in range(frames):
                    todo.append((src.at[2 * frames, :, pl.ds(f * HEAD_DIM, HEAD_DIM)], p_s.at[at + f]))
                if k < GROUP:
                    block = src.at[2 * frames, pl.ds(0, 2 * META), pl.ds(frames * HEAD_DIM, HEAD_DIM)]
                    todo.append((block, scratch[8].at[mine ^ k]))
        if not lead:
            todo.append((ins[-1], p_s))
        move(todo, sems)
        if lead:
            meta_bf, meta_v, meta = scratch[8:]
            for s in range(GROUP):
                meta_v[s] = meta_bf[s].astype(F32).astype(I32)[:META]
            move([(meta_v, meta), (meta_v, outs[4]), (p_s, outs[3])], sems)
        else:
            meta = scalars[1]

        def hints(f, _):
            hint = jnp.dot(p_s[f], w_s[...], preferred_element_type=F32).astype(BF16).astype(F32)
            k_s[f] = (k_s[f].astype(F32) + hint).astype(BF16)
            c_s[f] = (v_s[f].astype(F32) + hint).astype(BF16)
            at = f - BAND

            @pl.when((at >= 0) & (at < total))
            def _():
                q_s[at] = (q_s[at].astype(F32) + hint).astype(BF16)

            return 0

        lax.fori_loop(0, wide, hints, 0)

        def frame(f, _):
            s, r = lax.div(f, frames), lax.rem(f, frames)
            spots = [BAND + f + meta[s, r, j] for j in range(spans)]
            flag = meta[s, r, spans].astype(F32)
            for h in range(width // HEAD_DIM):
                cols = slice(h * HEAD_DIM, (h + 1) * HEAD_DIM)
                out = attend(q_s[f, :, cols], band(k_s, spots, cols), band(c_s, spots, cols))
                residual = (flag * g_s[:, cols] * out.astype(F32)).astype(BF16)
                m_s[f, :, cols] = (v_s[BAND + f, :, cols].astype(F32) + residual.astype(F32)).astype(BF16)
            return 0

        lax.fori_loop(0, total, frame, 0)
        move([(m_s, outs[0]), (m_s.at[pl.ds(total - BAND, BAND)], outs[1]), (m_s.at[pl.ds(0, BAND)], outs[2])], sems)

    outs = [rows((total, toks, width)), rows((BAND, toks, width)), rows((BAND, toks, width))]
    scratch = [
        pltpu.VMEM((total, toks, width), BF16),
        pltpu.VMEM((wide, toks, width), BF16),
        pltpu.VMEM((wide, toks, width), BF16),
        pltpu.VMEM((wide, toks, width), BF16),
        pltpu.VMEM((total, toks, width), BF16),
        pltpu.VMEM((wide, toks, HEAD_DIM), BF16),
        pltpu.VMEM((HEAD_DIM, width), BF16),
        pltpu.VMEM((1, width), F32),
    ]
    ins = [*pairs_in, *queries, before, after, weight, gain]
    scalars = [me]
    if lead:
        outs += [rows((wide, toks, HEAD_DIM)), rows((GROUP, META, HEAD_DIM), I32)]
        scratch += [
            pltpu.VMEM((GROUP, 2 * META, HEAD_DIM), BF16),
            pltpu.VMEM((GROUP, META, HEAD_DIM), I32),
            pltpu.SMEM((GROUP, META, HEAD_DIM), I32),
        ]
    else:
        ins.append(setting[0])
        scalars.append(setting[1])
    work = (4 * total * toks * spans * toks * width, 10 * total * toks * width)
    return run(kernel, ins, outs, scratch, 3 + GROUP + (GROUP + 2) * (3 + frames), scalars, work=work)


def base_block(me, pairs_in, queries, before, after, mixed, mixed_before, mixed_after, meta, spans):
    frames, toks, width = queries[0].shape
    total, wide = GROUP * frames, GROUP * frames + 2 * BAND

    def kernel(scalars, ins, outs, scratch, sems):
        mine, meta = scalars[0][0], scalars[1]
        kv, qs, (prev, after_ref) = ins[:GROUP], ins[GROUP : 2 * GROUP], ins[2 * GROUP : 2 * GROUP + 2]
        q_s, k_s, m_s, o_s = scratch
        todo = [
            (ins[-3], m_s.at[pl.ds(BAND, total)]),
            (ins[-2], m_s.at[pl.ds(0, BAND)]),
            (ins[-1], m_s.at[pl.ds(BAND + total, BAND)]),
            (prev.at[pl.ds(0, frames)], k_s.at[pl.ds(0, BAND)]),
            (after_ref.at[pl.ds(0, frames)], k_s.at[pl.ds(BAND + total, BAND)]),
        ]
        for k in range(GROUP):
            at = (mine ^ k) * frames
            todo.append((qs[k], q_s.at[pl.ds(at, frames)]))
            todo.append((kv[k].at[pl.ds(0, frames)], k_s.at[pl.ds(BAND + at, frames)]))
        move(todo, sems)

        def frame(f, _):
            s, r = lax.div(f, frames), lax.rem(f, frames)
            spots = [BAND + f + meta[s, r, j] for j in range(spans)]
            for h in range(width // HEAD_DIM):
                cols = slice(h * HEAD_DIM, (h + 1) * HEAD_DIM)
                o_s[f, :, cols] = attend(q_s[f, :, cols], band(k_s, spots, cols), band(m_s, spots, cols))
            return 0

        lax.fori_loop(0, total, frame, 0)
        move([(o_s.at[pl.ds((mine ^ k) * frames, frames)], outs[k]) for k in range(GROUP)], sems)

    scratch = [
        pltpu.VMEM((total, toks, width), BF16),
        pltpu.VMEM((wide, toks, width), BF16),
        pltpu.VMEM((wide, toks, width), BF16),
        pltpu.VMEM((total, toks, width), BF16),
    ]
    ins = [*pairs_in, *queries, before, after, mixed, mixed_before, mixed_after]
    work = (4 * total * toks * spans * toks * width, 8 * total * toks * width)
    return run(kernel, ins, [rows((frames, toks, width))] * GROUP, scratch, 5 + 2 * GROUP, [me, meta], work=work)


def place(me, parts, into, model_width, quarter, first):
    frames, toks, width = parts[0].shape

    def kernel(scalars, ins, outs, scratch, sems):
        mine = scalars[0][0]
        move([(ins[k], outs[0].at[:, :, lanes(mine ^ k, quarter, first, width)]) for k in range(GROUP)], sems)

    held = [] if into is None else [into]
    return run(
        kernel,
        [*parts, *held],
        [rows((frames, toks, model_width))],
        [],
        GROUP,
        [me],
        {} if into is None else {1 + GROUP: 0},
        (1, 16 * frames * toks * width),
    )[0]


def solution(mesh):
    count = mesh.shape["tm"]
    assert count % GROUP == 0
    across = [[(i, i ^ k) for i in range(count)] for k in range(GROUP)]
    upward = [(i, (i + GROUP) % count) for i in range(count)]
    downward = [(i, (i - GROUP) % count) for i in range(count)]

    def exchange(parts):
        return [parts[0]] + [lax.ppermute(parts[k], "tm", across[k]) for k in range(1, GROUP)]

    def body(queries, key_states, value_states, pose_depth, hint_weight, control_gain, band_offsets, control_flags):
        frames, _, model_width = queries.shape
        spans = band_offsets.shape[1]
        quarter = model_width // GROUP
        assert frames == BAND and sum(SLICES) * HEAD_DIM == quarter
        me = lax.rem(lax.axis_index("tm"), GROUP).astype(I32).reshape(1)
        gain = control_gain.reshape(1, -1)
        cuts = [(sum(SLICES[:c]) * HEAD_DIM, n * HEAD_DIM) for c, n in enumerate(SLICES)]
        state = []
        for c, (first, width) in enumerate(cuts):
            lead = [pose_depth, band_offsets, control_flags] if c == 0 else []
            pair = exchange(pack_pair(me, key_states, value_states, lead, quarter, first, width))
            state.append(pair)
        sides, asked = [], []
        for c, (first, width) in enumerate(cuts):
            last, start = edges(me, state[c])
            sides.append((lax.ppermute(last, "tm", upward), lax.ppermute(start, "tm", downward)))
            asked.append(exchange(pack_one(me, queries, quarter, first, width)))
        setting, mixed = None, []
        for c, (first, width) in enumerate(cuts):
            got = hint_branch(
                me, state[c], asked[c], *sides[c], hint_weight, gain, setting, spans, quarter, first, width
            )
            if setting is None:
                setting = got[3:]
            mixed.append((got[0], lax.ppermute(got[1], "tm", upward), lax.ppermute(got[2], "tm", downward)))
        out = None
        for c, (first, width) in enumerate(cuts):
            parts = base_block(me, state[c], asked[c], *sides[c], *mixed[c], setting[1], spans)
            out = place(me, exchange(parts), out, model_width, quarter, first)
        return out

    return jax.shard_map(
        body,
        mesh=mesh,
        in_specs=(
            P(("grp", "tm"), None, None),
            P(("grp", "tm"), None, None),
            P(("grp", "tm"), None, None),
            P(("grp", "tm"), None, None),
            P(),
            P(),
            P(("grp", "tm"), None),
            P(("grp", "tm")),
        ),
        out_specs=P(("grp", "tm"), None, None),
        check_vma=False,
    )
```

time: 219 us -> 180 us (0.82)
  Pallas kernels: 0 us -> 94.5 us
  waiting for transfers between devices: 115 us -> 36.6 us
  starting transfers between devices: 3.19 us -> 46.5 us
  matrix products: 36.6 us -> 0 us
  local copies, waits for them, and re-layouts: 38.2 us -> 2.1 us
  other arithmetic: 25.1 us -> 0 us
    pallas_call x0 -> x18, Pallas kernels: none -> 94.5 us  [run(): pl.pallas_call(body, out_shape=list(outs), in_specs=[SMEM] * a + [ANY] *...]
    ppermute x4 -> x39, waiting for transfers between devices: 115 us -> 36.6 us  [the longest x27 33.5 us: exchange(): lax.ppermute(parts[k], 'tm', across[k])]
    ppermute x4 -> x39, starting transfers between devices: 3.19 us -> 46.5 us  [the longest x27 27.3 us: exchange(): lax.ppermute(parts[k], 'tm', across[k])]
    dot_general x5 -> x0, matrix products: 36.6 us -> none  [the longest x2 30.1 us: attend(): jnp.einsum('fhqk,fkhd->fqhd', weights, value_rows, preferred_element_type...]
    gather x4 -> x0, local copies, waits for them, and re-layouts: 19.9 us -> none  [the longest x2 10 us: attend(): jnp.take(key_set, lookup, axis=0)]
    select_n x3 -> x0, other arithmetic: 8.15 us -> none  [the longest x2 8.15 us: attend(): jnp.take(key_set, lookup, axis=0)]
    unnamed x26 -> x18, local copies, waits for them, and re-layouts: 9.88 us -> 2.1 us
    squeeze x2 -> x0, local copies, waits for them, and re-layouts: 6.92 us -> none  [the longest x1 3.46 us: body(): control_out = attend(control_queries, control_wide[0], control_wide[1])]
  transfers between devices with their start and end apart: 4 -> 39, of which waited for: 3 -> 10; matrix products, arithmetic and copies ran while one was open for 0% -> 0% of each run, Pallas kernels for 0% -> 52%
where the time goes in v1:
time: 180 us
  Pallas kernels  94.5 us (52%)
  starting transfers between devices  46.5 us (26%)
  waiting for transfers between devices  36.6 us (20%)
  local copies, waits for them, and re-layouts  2.1 us (1%)
    pallas_call x18, Pallas kernels, run(): pl.pallas_call(body, out_shape=list(outs), in_specs=[SMEM] * a + [ANY] *...  94.5 us
    ppermute x27, waiting for transfers between devices, exchange(): lax.ppermute(parts[k], 'tm', across[k])  33.5 us
    ppermute x27, starting transfers between devices, exchange(): lax.ppermute(parts[k], 'tm', across[k])  27.3 us
    ppermute x3, starting transfers between devices, body(): lax.ppermute(got[2], 'tm', downward)  9.75 us
    ppermute x3, starting transfers between devices, body(): lax.ppermute(start, 'tm', downward)  6.75 us
  transfers between devices with their start and end apart: 39, of which 10 were waited for; matrix products, arithmetic and copies ran while one was open for 0% of the time, Pallas kernels for 52%

profile of v1, /device:TPU:1, one launch (start us, length us, event | category | flops | bytes accessed | tf_op | source)
XLA Modules:
  0.0 180.0 jit_solution(6344054439373629179)
XLA Ops:
  2.2 2.3 %collective-permute-start.4 = (bf16[2,64,384]{2,1,0:T(8,128)(2,1)S(1)}, bf16[2,64,384]{2,1,0:T(8,128)(2,1)S(1)}, u32[]{:S(2)}, u32[]{:S(2)}) collective-permute-start(bf16[2,64,384]{2,1,0:T(8,128)(2,1)S(1)} %get-tuple-element.64), channel_id=1, source_target_pairs={{0,2},{1,3},{2,0},{3,1},{4,6},{5,7},{6,4},{7,5},{8,10},{9,11},{10,... | collective-permute-start | bytes 294920 | tf_op jit(solution)/shard_map/ppermute | solution.py:293
  9.9 2.2 %collective-permute-done.5.refs_8_.refs_9_ = bf16[2,64,384]{2,1,0:T(8,128)(2,1)S(1)} collective-permute-done((bf16[2,64,384]{2,1,0:T(8,128)(2,1)S(1)}, bf16[2,64,384]{2,1,0:T(8,128)(2,1)S(1)}, u32[]{:S(2)}, u32[]{:S(2)}) %collective-permute-start.5) | collective-permute-done | bytes 98336 | tf_op jit(solution)/shard_map/ppermute | solution.py:293
  14.4 2.1 %collective-permute-done.1.refs_3_.refs_4_ = bf16[5,64,384]{2,1,0:T(8,128)(2,1)S(1)} collective-permute-done((bf16[5,64,384]{2,1,0:T(8,128)(2,1)S(1)}, bf16[5,64,384]{2,1,0:T(8,128)(2,1)S(1)}, u32[]{:S(2)}, u32[]{:S(2)}) %collective-permute-start.1) | collective-permute-done | bytes 245792 | tf_op jit(solution)/shard_map/ppermute | solution.py:293
  16.5 1.9 %collective-permute-start.10 = (bf16[4,64,384]{2,1,0:T(8,128)(2,1)S(1)}, bf16[4,64,384]{2,1,0:T(8,128)(2,1)S(1)}, u32[]{:S(2)}, u32[]{:S(2)}) collective-permute-start(bf16[4,64,384]{2,1,0:T(8,128)(2,1)S(1)} %get-tuple-element.72), channel_id=1, source_target_pairs={{0,3},{1,2},{2,1},{3,0},{4,7},{5,6},{6,5},{7,4},{8,11},{9,10},{10,... | collective-permute-start | bytes 589832 | tf_op jit(solution)/shard_map/ppermute | solution.py:293
  18.4 4.2 %collective-permute-done.2.refs_4_.refs_5_ = bf16[5,64,384]{2,1,0:T(8,128)(2,1)S(1)} collective-permute-done((bf16[5,64,384]{2,1,0:T(8,128)(2,1)S(1)}, bf16[5,64,384]{2,1,0:T(8,128)(2,1)S(1)}, u32[]{:S(2)}, u32[]{:S(2)}) %collective-permute-start.2) | collective-permute-done | bytes 245792 | tf_op jit(solution)/shard_map/ppermute | solution.py:293
  23.1 4.2 %collective-permute-done.22.refs_3_.refs_4_ = bf16[4,64,512]{2,1,0:T(8,128)(2,1)S(1)} collective-permute-done((bf16[4,64,512]{2,1,0:T(8,128)(2,1)S(1)}, bf16[4,64,512]{2,1,0:T(8,128)(2,1)S(1)}, u32[]{:S(2)}, u32[]{:S(2)}) %collective-permute-start.22) | collective-permute-done | bytes 262176 | tf_op jit(solution)/shard_map/ppermute | solution.py:293
  28.6 5.6 %collective-permute-done.23.refs_4_.refs_5_ = bf16[4,64,512]{2,1,0:T(8,128)(2,1)S(1)} collective-permute-done((bf16[4,64,512]{2,1,0:T(8,128)(2,1)S(1)}, bf16[4,64,512]{2,1,0:T(8,128)(2,1)S(1)}, u32[]{:S(2)}, u32[]{:S(2)}) %collective-permute-start.23) | collective-permute-done | bytes 262176 | tf_op jit(solution)/shard_map/ppermute | solution.py:293
  35.5 8.7 %collective-permute-done.25.refs_8_ = bf16[2,64,512]{2,1,0:T(8,128)(2,1)S(1)} collective-permute-done((bf16[2,64,512]{2,1,0:T(8,128)(2,1)S(1)}, bf16[2,64,512]{2,1,0:T(8,128)(2,1)S(1)}, u32[]{:S(2)}, u32[]{:S(2)}) %collective-permute-start.25) | collective-permute-done | bytes 131104 | tf_op jit(solution)/shard_map/ppermute | solution.py:293
  45.5 2.0 %collective-permute-start.7 = (bf16[5,64,384]{2,1,0:T(8,128)(2,1)S(1)}, bf16[5,64,384]{2,1,0:T(8,128)(2,1)S(1)}, u32[]{:S(2)}, u32[]{:S(2)}) collective-permute-start(bf16[5,64,384]{2,1,0:T(8,128)(2,1)S(1)} %get-tuple-element.67), channel_id=1, source_target_pairs={{0,12},{1,13},{2,14},{3,15},{4,0},{5,1},{6,2},{7,3},{8,4},{9,5},{1... | collective-permute-start | bytes 737288 | tf_op jit(solution)/shard_map/ppermute | solution.py:311
  49.0 2.2 %collective-permute-start.26 = (bf16[2,64,512]{2,1,0:T(8,128)(2,1)S(1)}, bf16[2,64,512]{2,1,0:T(8,128)(2,1)S(1)}, u32[]{:S(2)}, u32[]{:S(2)}) collective-permute-start(bf16[2,64,512]{2,1,0:T(8,128)(2,1)S(1)} %get-tuple-element.94), channel_id=1, source_target_pairs={{0,3},{1,2},{2,1},{3,0},{4,7},{5,6},{6,5},{7,4},{8,11},{9,10},{10,... | collective-permute-start | bytes 393224 | tf_op jit(solution)/shard_map/ppermute | solution.py:293
  51.8 3.2 %collective-permute-done.26.refs_9_ = bf16[2,64,512]{2,1,0:T(8,128)(2,1)S(1)} collective-permute-done((bf16[2,64,512]{2,1,0:T(8,128)(2,1)S(1)}, bf16[2,64,512]{2,1,0:T(8,128)(2,1)S(1)}, u32[]{:S(2)}, u32[]{:S(2)}) %collective-permute-start.26) | collective-permute-done | bytes 131104 | tf_op jit(solution)/shard_map/ppermute | solution.py:293
  55.0 3.3 %collective-permute-start.15 = (bf16[4,64,384]{2,1,0:T(8,128)(2,1)S(1)}, bf16[4,64,384]{2,1,0:T(8,128)(2,1)S(1)}, u32[]{:S(2)}, u32[]{:S(2)}) collective-permute-start(bf16[4,64,384]{2,1,0:T(8,128)(2,1)S(1)} %get-tuple-element.78), channel_id=1, source_target_pairs={{0,12},{1,13},{2,14},{3,15},{4,0},{5,1},{6,2},{7,3},{8,4},{9,5},{1... | collective-permute-start | bytes 589832 | tf_op jit(solution)/shard_map/ppermute | solution.py:311
  61.0 3.1 %collective-permute-done.28.refs_11_ = bf16[4,64,512]{2,1,0:T(8,128)(2,1)S(1)} collective-permute-done((bf16[4,64,512]{2,1,0:T(8,128)(2,1)S(1)}, bf16[4,64,512]{2,1,0:T(8,128)(2,1)S(1)}, u32[]{:S(2)}, u32[]{:S(2)}) %collective-permute-start.28) | collective-permute-done | bytes 262176 | tf_op jit(solution)/shard_map/ppermute | solution.py:311
  64.1 3.9 %collective-permute-start.13 = (bf16[2,64,384]{2,1,0:T(8,128)(2,1)S(1)}, bf16[2,64,384]{2,1,0:T(8,128)(2,1)S(1)}, u32[]{:S(2)}, u32[]{:S(2)}) collective-permute-start(bf16[2,64,384]{2,1,0:T(8,128)(2,1)S(1)} %get-tuple-element.76), channel_id=1, source_target_pairs={{0,3},{1,2},{2,1},{3,0},{4,7},{5,6},{6,5},{7,4},{8,11},{9,10},{10,... | collective-permute-start | bytes 294920 | tf_op jit(solution)/shard_map/ppermute | solution.py:293
  67.9 15.1 %shard_map.85 = (bf16[8,64,384]{2,1,0:T(8,128)(2,1)S(1)}, bf16[2,64,384]{2,1,0:T(8,128)(2,1)S(1)}, bf16[2,64,384]{2,1,0:T(8,128)(2,1)S(1)}, bf16[12,64,128]{2,1,0:T(8,128)(2,1)S(1)}, s32[4,8,128]{2,1,0:T(8,128)S(1)}) custom-call(s32[1]{0:T(128)} %bitcast.refs_0_, bf16[5,64,384]{2,1,0:T(8,128)(2,1)S(1)} %get-tuple-element.58.refs_1_.refs_2_, ...), custom_call_target="tpu_custom_call" | custom-call | flops 150994944 | bytes 1966080 | tf_op jit(solution)/shard_map/pallas_call | solution.py:26
  83.0 18.5 %shard_map.94 = (bf16[8,64,512]{2,1,0:T(8,128)(2,1)S(1)}, bf16[2,64,512]{2,1,0:T(8,128)(2,1)S(1)}, bf16[2,64,512]{2,1,0:T(8,128)(2,1)S(1)}) custom-call(s32[1]{0:T(128)} %bitcast.refs_0_, s32[4,8,128]{2,1,0:T(8,128)S(1)} %get-tuple-element.68.refs_1_, bf16[4,64,512]{2,1,0:T(8,128)(2,1)S(1)} %get-tuple-element.87.refs_1_.refs_2_, ...), custom_call_target="tpu_custom_call" | custom-call | flops 201326592 | bytes 2621440 | tf_op jit(solution)/shard_map/pallas_call | solution.py:26
  101.6 3.2 %collective-permute-start.30 = (bf16[2,64,512]{2,1,0:T(8,128)(2,1)S(1)}, bf16[2,64,512]{2,1,0:T(8,128)(2,1)S(1)}, u32[]{:S(2)}, u32[]{:S(2)}) collective-permute-start(bf16[2,64,512]{2,1,0:T(8,128)(2,1)S(1)} %get-tuple-element.99), channel_id=1, source_target_pairs={{0,12},{1,13},{2,14},{3,15},{4,0},{5,1},{6,2},{7,3},{8,4},{9,5},{1... | collective-permute-start | bytes 393224 | tf_op jit(solution)/shard_map/ppermute | solution.py:320
  104.9 3.3 %collective-permute-start.35 = (bf16[2,64,384]{2,1,0:T(8,128)(2,1)S(1)}, bf16[2,64,384]{2,1,0:T(8,128)(2,1)S(1)}, u32[]{:S(2)}, u32[]{:S(2)}) collective-permute-start(bf16[2,64,384]{2,1,0:T(8,128)(2,1)S(1)} %get-tuple-element.106), channel_id=1, source_target_pairs={{0,12},{1,13},{2,14},{3,15},{4,0},{5,1},{6,2},{7,3},{8,4},{9,5},{1... | collective-permute-start | bytes 294920 | tf_op jit(solution)/shard_map/ppermute | solution.py:320
  108.2 15.1 %shard_map.89 = (bf16[8,64,384]{2,1,0:T(8,128)(2,1)S(1)}, bf16[2,64,384]{2,1,0:T(8,128)(2,1)S(1)}, bf16[2,64,384]{2,1,0:T(8,128)(2,1)S(1)}) custom-call(s32[1]{0:T(128)} %bitcast.refs_0_, s32[4,8,128]{2,1,0:T(8,128)S(1)} %get-tuple-element.68.refs_1_, bf16[4,64,384]{2,1,0:T(8,128)(2,1)S(1)} %get-tuple-element.69.refs_1_.refs_2_, ...), custom_call_target="tpu_custom_call" | custom-call | flops 150994944 | bytes 1966080 | tf_op jit(solution)/shard_map/pallas_call | solution.py:26
  123.4 3.2 %collective-permute-start.17 = (bf16[2,64,384]{2,1,0:T(8,128)(2,1)S(1)}, bf16[2,64,384]{2,1,0:T(8,128)(2,1)S(1)}, u32[]{:S(2)}, u32[]{:S(2)}) collective-permute-start(bf16[2,64,384]{2,1,0:T(8,128)(2,1)S(1)} %get-tuple-element.82), channel_id=1, source_target_pairs={{0,12},{1,13},{2,14},{3,15},{4,0},{5,1},{6,2},{7,3},{8,4},{9,5},{1... | collective-permute-start | bytes 294920 | tf_op jit(solution)/shard_map/ppermute | solution.py:320
  126.6 12.4 %shard_map.96 = (bf16[2,64,384]{2,1,0:T(8,128)(2,1)S(1)}, bf16[2,64,384]{2,1,0:T(8,128)(2,1)S(1)}, bf16[2,64,384]{2,1,0:T(8,128)(2,1)S(1)}, bf16[2,64,384]{2,1,0:T(8,128)(2,1)S(1)}) custom-call(s32[1]{0:T(128)} %bitcast.refs_0_, s32[4,8,128]{2,1,0:T(8,128)S(1)} %get-tuple-element.68.refs_1_, bf16[5,64,384]{2,1,0:T(8,128)(2,1)S(1)} %get-tuple-element.58.refs_1_.refs_2_, ...), custom_call_target="tpu_custom_call" | custom-call | flops 150994944 | bytes 1572864 | tf_op jit(solution)/shard_map/pallas_call | solution.py:26
  140.4 15.6 %shard_map.95 = (bf16[2,64,512]{2,1,0:T(8,128)(2,1)S(1)}, bf16[2,64,512]{2,1,0:T(8,128)(2,1)S(1)}, bf16[2,64,512]{2,1,0:T(8,128)(2,1)S(1)}, bf16[2,64,512]{2,1,0:T(8,128)(2,1)S(1)}) custom-call(s32[1]{0:T(128)} %bitcast.refs_0_, s32[4,8,128]{2,1,0:T(8,128)S(1)} %get-tuple-element.68.refs_1_, bf16[4,64,512]{2,1,0:T(8,128)(2,1)S(1)} %get-tuple-element.87.refs_1_.refs_2_, ...), custom_call_target="tpu_custom_call" | custom-call | flops 201326592 | bytes 2097152 | tf_op jit(solution)/shard_map/pallas_call | solution.py:26
  159.7 12.4 %shard_map.90 = (bf16[2,64,384]{2,1,0:T(8,128)(2,1)S(1)}, bf16[2,64,384]{2,1,0:T(8,128)(2,1)S(1)}, bf16[2,64,384]{2,1,0:T(8,128)(2,1)S(1)}, bf16[2,64,384]{2,1,0:T(8,128)(2,1)S(1)}) custom-call(s32[1]{0:T(128)} %bitcast.refs_0_, s32[4,8,128]{2,1,0:T(8,128)S(1)} %get-tuple-element.68.refs_1_, bf16[4,64,384]{2,1,0:T(8,128)(2,1)S(1)} %get-tuple-element.69.refs_1_.refs_2_, ...), custom_call_target="tpu_custom_call" | custom-call | flops 150994944 | bytes 1572864 | tf_op jit(solution)/shard_map/pallas_call | solution.py:26
  177.0 2.3 %collective-permute-done.20.refs_4_ = bf16[2,64,384]{2,1,0:T(8,128)(2,1)S(1)} collective-permute-done((bf16[2,64,384]{2,1,0:T(8,128)(2,1)S(1)}, bf16[2,64,384]{2,1,0:T(8,128)(2,1)S(1)}, u32[]{:S(2)}, u32[]{:S(2)}) %collective-permute-start.20) | collective-permute-done | bytes 98336 | tf_op jit(solution)/shard_map/ppermute | solution.py:293
  (90 shorter events, 29.7 us)
Async XLA Ops:
  12.6 21.5 %collective-permute-start.23 = (bf16[4,64,512]{2,1,0:T(8,128)(2,1)S(1)}, bf16[4,64,512]{2,1,0:T(8,128)(2,1)S(1)}, u32[]{:S(2)}, u32[]{:S(2)}) collective-permute-start(bf16[4,64,512]{2,1,0:T(8,128)(2,1)S(1)} %get-tuple-element.90), channel_id=1, source_target_pairs={{0,3},{1,2},{2,1},{3,0},{4,7},{5,6},{6,5},{7,4},{8,11},{9,10},{10,... | collective-permute-start | bytes 786440 | tf_op jit(solution)/shard_map/ppermute | solution.py:293
  16.5 29.0 %collective-permute-start.10 = (bf16[4,64,384]{2,1,0:T(8,128)(2,1)S(1)}, bf16[4,64,384]{2,1,0:T(8,128)(2,1)S(1)}, u32[]{:S(2)}, u32[]{:S(2)}) collective-permute-start(bf16[4,64,384]{2,1,0:T(8,128)(2,1)S(1)} %get-tuple-element.72), channel_id=1, source_target_pairs={{0,3},{1,2},{2,1},{3,0},{4,7},{5,6},{6,5},{7,4},{8,11},{9,10},{10,... | collective-permute-start | bytes 589832 | tf_op jit(solution)/shard_map/ppermute | solution.py:293
  22.6 25.0 %collective-permute-start.8 = (bf16[4,64,384]{2,1,0:T(8,128)(2,1)S(1)}, bf16[4,64,384]{2,1,0:T(8,128)(2,1)S(1)}, u32[]{:S(2)}, u32[]{:S(2)}) collective-permute-start(bf16[4,64,384]{2,1,0:T(8,128)(2,1)S(1)} %get-tuple-element.70), channel_id=1, source_target_pairs={{0,1},{1,0},{2,3},{3,2},{4,5},{5,4},{6,7},{7,6},{8,9},{9,8},{10,11... | collective-permute-start | bytes 589832 | tf_op jit(solution)/shard_map/ppermute | solution.py:293
  22.6 26.4 %collective-permute-start.9 = (bf16[4,64,384]{2,1,0:T(8,128)(2,1)S(1)}, bf16[4,64,384]{2,1,0:T(8,128)(2,1)S(1)}, u32[]{:S(2)}, u32[]{:S(2)}) collective-permute-start(bf16[4,64,384]{2,1,0:T(8,128)(2,1)S(1)} %get-tuple-element.71), channel_id=1, source_target_pairs={{0,2},{1,3},{2,0},{3,1},{4,6},{5,7},{6,4},{7,5},{8,10},{9,11},{10,... | collective-permute-start | bytes 589832 | tf_op jit(solution)/shard_map/ppermute | solution.py:293
  27.4 16.9 %collective-permute-start.25 = (bf16[2,64,512]{2,1,0:T(8,128)(2,1)S(1)}, bf16[2,64,512]{2,1,0:T(8,128)(2,1)S(1)}, u32[]{:S(2)}, u32[]{:S(2)}) collective-permute-start(bf16[2,64,512]{2,1,0:T(8,128)(2,1)S(1)} %get-tuple-element.93), channel_id=1, source_target_pairs={{0,2},{1,3},{2,0},{3,1},{4,6},{5,7},{6,4},{7,5},{8,10},{9,11},{10,... | collective-permute-start | bytes 393224 | tf_op jit(solution)/shard_map/ppermute | solution.py:293
  34.1 20.9 %collective-permute-start.6 = (bf16[5,64,384]{2,1,0:T(8,128)(2,1)S(1)}, bf16[5,64,384]{2,1,0:T(8,128)(2,1)S(1)}, u32[]{:S(2)}, u32[]{:S(2)}) collective-permute-start(bf16[5,64,384]{2,1,0:T(8,128)(2,1)S(1)} %get-tuple-element.66), channel_id=1, source_target_pairs={{0,4},{1,5},{2,6},{3,7},{4,8},{5,9},{6,10},{7,11},{8,12},{9,13},{1... | collective-permute-start | bytes 737288 | tf_op jit(solution)/shard_map/ppermute | solution.py:311
  44.2 16.0 %collective-permute-start.27 = (bf16[4,64,512]{2,1,0:T(8,128)(2,1)S(1)}, bf16[4,64,512]{2,1,0:T(8,128)(2,1)S(1)}, u32[]{:S(2)}, u32[]{:S(2)}) collective-permute-start(bf16[4,64,512]{2,1,0:T(8,128)(2,1)S(1)} %get-tuple-element.95), channel_id=1, source_target_pairs={{0,4},{1,5},{2,6},{3,7},{4,8},{5,9},{6,10},{7,11},{8,12},{9,13},{1... | collective-permute-start | bytes 786440 | tf_op jit(solution)/shard_map/ppermute | solution.py:311
  47.6 16.5 %collective-permute-start.28 = (bf16[4,64,512]{2,1,0:T(8,128)(2,1)S(1)}, bf16[4,64,512]{2,1,0:T(8,128)(2,1)S(1)}, u32[]{:S(2)}, u32[]{:S(2)}) collective-permute-start(bf16[4,64,512]{2,1,0:T(8,128)(2,1)S(1)} %get-tuple-element.96), channel_id=1, source_target_pairs={{0,12},{1,13},{2,14},{3,15},{4,0},{5,1},{6,2},{7,3},{8,4},{9,5},{1... | collective-permute-start | bytes 786440 | tf_op jit(solution)/shard_map/ppermute | solution.py:311
  55.0 49.9 %collective-permute-start.14 = (bf16[4,64,384]{2,1,0:T(8,128)(2,1)S(1)}, bf16[4,64,384]{2,1,0:T(8,128)(2,1)S(1)}, u32[]{:S(2)}, u32[]{:S(2)}) collective-permute-start(bf16[4,64,384]{2,1,0:T(8,128)(2,1)S(1)} %get-tuple-element.77), channel_id=1, source_target_pairs={{0,4},{1,5},{2,6},{3,7},{4,8},{5,9},{6,10},{7,11},{8,12},{9,13},{1... | collective-permute-start | bytes 589832 | tf_op jit(solution)/shard_map/ppermute | solution.py:311
  55.0 53.2 %collective-permute-start.15 = (bf16[4,64,384]{2,1,0:T(8,128)(2,1)S(1)}, bf16[4,64,384]{2,1,0:T(8,128)(2,1)S(1)}, u32[]{:S(2)}, u32[]{:S(2)}) collective-permute-start(bf16[4,64,384]{2,1,0:T(8,128)(2,1)S(1)} %get-tuple-element.78), channel_id=1, source_target_pairs={{0,12},{1,13},{2,14},{3,15},{4,0},{5,1},{6,2},{7,3},{8,4},{9,5},{1... | collective-permute-start | bytes 589832 | tf_op jit(solution)/shard_map/ppermute | solution.py:311
  58.4 43.2 %collective-permute-start.11 = (bf16[2,64,384]{2,1,0:T(8,128)(2,1)S(1)}, bf16[2,64,384]{2,1,0:T(8,128)(2,1)S(1)}, u32[]{:S(2)}, u32[]{:S(2)}) collective-permute-start(bf16[2,64,384]{2,1,0:T(8,128)(2,1)S(1)} %get-tuple-element.74), channel_id=1, source_target_pairs={{0,1},{1,0},{2,3},{3,2},{4,5},{5,4},{6,7},{7,6},{8,9},{9,8},{10,11... | collective-permute-start | bytes 294920 | tf_op jit(solution)/shard_map/ppermute | solution.py:293
  60.3 41.4 %collective-permute-start.12 = (bf16[2,64,384]{2,1,0:T(8,128)(2,1)S(1)}, bf16[2,64,384]{2,1,0:T(8,128)(2,1)S(1)}, u32[]{:S(2)}, u32[]{:S(2)}) collective-permute-start(bf16[2,64,384]{2,1,0:T(8,128)(2,1)S(1)} %get-tuple-element.75), channel_id=1, source_target_pairs={{0,2},{1,3},{2,0},{3,1},{4,6},{5,7},{6,4},{7,5},{8,10},{9,11},{10,... | collective-permute-start | bytes 294920 | tf_op jit(solution)/shard_map/ppermute | solution.py:293
  64.1 40.8 %collective-permute-start.13 = (bf16[2,64,384]{2,1,0:T(8,128)(2,1)S(1)}, bf16[2,64,384]{2,1,0:T(8,128)(2,1)S(1)}, u32[]{:S(2)}, u32[]{:S(2)}) collective-permute-start(bf16[2,64,384]{2,1,0:T(8,128)(2,1)S(1)} %get-tuple-element.76), channel_id=1, source_target_pairs={{0,3},{1,2},{2,1},{3,0},{4,7},{5,6},{6,5},{7,4},{8,11},{9,10},{10,... | collective-permute-start | bytes 294920 | tf_op jit(solution)/shard_map/ppermute | solution.py:293
  101.6 38.8 %collective-permute-start.29 = (bf16[2,64,512]{2,1,0:T(8,128)(2,1)S(1)}, bf16[2,64,512]{2,1,0:T(8,128)(2,1)S(1)}, u32[]{:S(2)}, u32[]{:S(2)}) collective-permute-start(bf16[2,64,512]{2,1,0:T(8,128)(2,1)S(1)} %get-tuple-element.98), channel_id=1, source_target_pairs={{0,4},{1,5},{2,6},{3,7},{4,8},{5,9},{6,10},{7,11},{8,12},{9,13},{1... | collective-permute-start | bytes 393224 | tf_op jit(solution)/shard_map/ppermute | solution.py:320
  101.6 38.8 %collective-permute-start.30 = (bf16[2,64,512]{2,1,0:T(8,128)(2,1)S(1)}, bf16[2,64,512]{2,1,0:T(8,128)(2,1)S(1)}, u32[]{:S(2)}, u32[]{:S(2)}) collective-permute-start(bf16[2,64,512]{2,1,0:T(8,128)(2,1)S(1)} %get-tuple-element.99), channel_id=1, source_target_pairs={{0,12},{1,13},{2,14},{3,15},{4,0},{5,1},{6,2},{7,3},{8,4},{9,5},{1... | collective-permute-start | bytes 393224 | tf_op jit(solution)/shard_map/ppermute | solution.py:320
  104.9 18.5 %collective-permute-start.34 = (bf16[2,64,384]{2,1,0:T(8,128)(2,1)S(1)}, bf16[2,64,384]{2,1,0:T(8,128)(2,1)S(1)}, u32[]{:S(2)}, u32[]{:S(2)}) collective-permute-start(bf16[2,64,384]{2,1,0:T(8,128)(2,1)S(1)} %get-tuple-element.105), channel_id=1, source_target_pairs={{0,4},{1,5},{2,6},{3,7},{4,8},{5,9},{6,10},{7,11},{8,12},{9,13},{1... | collective-permute-start | bytes 294920 | tf_op jit(solution)/shard_map/ppermute | solution.py:320
  104.9 21.7 %collective-permute-start.35 = (bf16[2,64,384]{2,1,0:T(8,128)(2,1)S(1)}, bf16[2,64,384]{2,1,0:T(8,128)(2,1)S(1)}, u32[]{:S(2)}, u32[]{:S(2)}) collective-permute-start(bf16[2,64,384]{2,1,0:T(8,128)(2,1)S(1)} %get-tuple-element.106), channel_id=1, source_target_pairs={{0,12},{1,13},{2,14},{3,15},{4,0},{5,1},{6,2},{7,3},{8,4},{9,5},{1... | collective-permute-start | bytes 294920 | tf_op jit(solution)/shard_map/ppermute | solution.py:320
  123.3 33.4 %collective-permute-start.16 = (bf16[2,64,384]{2,1,0:T(8,128)(2,1)S(1)}, bf16[2,64,384]{2,1,0:T(8,128)(2,1)S(1)}, u32[]{:S(2)}, u32[]{:S(2)}) collective-permute-start(bf16[2,64,384]{2,1,0:T(8,128)(2,1)S(1)} %get-tuple-element.81), channel_id=1, source_target_pairs={{0,4},{1,5},{2,6},{3,7},{4,8},{5,9},{6,10},{7,11},{8,12},{9,13},{1... | collective-permute-start | bytes 294920 | tf_op jit(solution)/shard_map/ppermute | solution.py:320
  123.4 34.9 %collective-permute-start.17 = (bf16[2,64,384]{2,1,0:T(8,128)(2,1)S(1)}, bf16[2,64,384]{2,1,0:T(8,128)(2,1)S(1)}, u32[]{:S(2)}, u32[]{:S(2)}) collective-permute-start(bf16[2,64,384]{2,1,0:T(8,128)(2,1)S(1)} %get-tuple-element.82), channel_id=1, source_target_pairs={{0,12},{1,13},{2,14},{3,15},{4,0},{5,1},{6,2},{7,3},{8,4},{9,5},{1... | collective-permute-start | bytes 294920 | tf_op jit(solution)/shard_map/ppermute | solution.py:320
  139.0 19.8 %collective-permute-start.36 = (bf16[2,64,384]{2,1,0:T(8,128)(2,1)S(1)}, bf16[2,64,384]{2,1,0:T(8,128)(2,1)S(1)}, u32[]{:S(2)}, u32[]{:S(2)}) collective-permute-start(bf16[2,64,384]{2,1,0:T(8,128)(2,1)S(1)} %get-tuple-element.108), channel_id=1, source_target_pairs={{0,1},{1,0},{2,3},{3,2},{4,5},{5,4},{6,7},{7,6},{8,9},{9,8},{10,11... | collective-permute-start | bytes 294920 | tf_op jit(solution)/shard_map/ppermute | solution.py:293
  156.0 17.1 %collective-permute-start.31 = (bf16[2,64,512]{2,1,0:T(8,128)(2,1)S(1)}, bf16[2,64,512]{2,1,0:T(8,128)(2,1)S(1)}, u32[]{:S(2)}, u32[]{:S(2)}) collective-permute-start(bf16[2,64,512]{2,1,0:T(8,128)(2,1)S(1)} %get-tuple-element.101), channel_id=1, source_target_pairs={{0,1},{1,0},{2,3},{3,2},{4,5},{5,4},{6,7},{7,6},{8,9},{9,8},{10,11... | collective-permute-start | bytes 393224 | tf_op jit(solution)/shard_map/ppermute | solution.py:293
  156.2 15.9 %collective-permute-start.37 = (bf16[2,64,384]{2,1,0:T(8,128)(2,1)S(1)}, bf16[2,64,384]{2,1,0:T(8,128)(2,1)S(1)}, u32[]{:S(2)}, u32[]{:S(2)}) collective-permute-start(bf16[2,64,384]{2,1,0:T(8,128)(2,1)S(1)} %get-tuple-element.109), channel_id=1, source_target_pairs={{0,2},{1,3},{2,0},{3,1},{4,6},{5,7},{6,4},{7,5},{8,10},{9,11},{10,... | collective-permute-start | bytes 294920 | tf_op jit(solution)/shard_map/ppermute | solution.py:293
  158.3 16.9 %collective-permute-start.32 = (bf16[2,64,512]{2,1,0:T(8,128)(2,1)S(1)}, bf16[2,64,512]{2,1,0:T(8,128)(2,1)S(1)}, u32[]{:S(2)}, u32[]{:S(2)}) collective-permute-start(bf16[2,64,512]{2,1,0:T(8,128)(2,1)S(1)} %get-tuple-element.102), channel_id=1, source_target_pairs={{0,2},{1,3},{2,0},{3,1},{4,6},{5,7},{6,4},{7,5},{8,10},{9,11},{10,... | collective-permute-start | bytes 393224 | tf_op jit(solution)/shard_map/ppermute | solution.py:293
  158.8 16.3 %collective-permute-start.33 = (bf16[2,64,512]{2,1,0:T(8,128)(2,1)S(1)}, bf16[2,64,512]{2,1,0:T(8,128)(2,1)S(1)}, u32[]{:S(2)}, u32[]{:S(2)}) collective-permute-start(bf16[2,64,512]{2,1,0:T(8,128)(2,1)S(1)} %get-tuple-element.103), channel_id=1, source_target_pairs={{0,3},{1,2},{2,1},{3,0},{4,7},{5,6},{6,5},{7,4},{8,11},{9,10},{10,... | collective-permute-start | bytes 393224 | tf_op jit(solution)/shard_map/ppermute | solution.py:293
  (24 other events, 242.3 us)

commit v2 on v1

--- a/solution.py
+++ b/solution.py
@@ -119,11 +119,18 @@
     return run(kernel, parts, [shape, shape], [], 2, [me], work=(1, 8 * parts[0].size))
 
 
-def attend(query, keys, values):
-    scores = lax.dot_general(query, keys, (((1,), (1,)), ((), ())), preferred_element_type=F32) * HEAD_DIM ** (-0.5)
-    scores = jnp.exp(scores - jnp.max(scores, axis=1, keepdims=True))
-    weights = (scores * (1.0 / jnp.sum(scores, axis=1, keepdims=True))).astype(BF16)
-    return jnp.dot(weights, values, preferred_element_type=F32).astype(BF16)
+def attend(jobs):
+    scores = [
+        lax.dot_general(query, keys, (((1,), (1,)), ((), ())), preferred_element_type=F32) * HEAD_DIM ** (-0.5)
+        for query, keys, _ in jobs
+    ]
+    tops = [jnp.max(x, axis=1, keepdims=True) for x in scores]
+    scores = [jnp.exp(x - top) for x, top in zip(scores, tops)]
+    scales = [1.0 / jnp.sum(x, axis=1, keepdims=True) for x in scores]
+    weights = [(x * scale).astype(BF16) for x, scale in zip(scores, scales)]
+    return [
+        jnp.dot(w, values, preferred_element_type=F32).astype(BF16) for w, (_, _, values) in zip(weights, jobs)
+    ]
 
 
 def band(ref, spots, cols):
@@ -178,18 +185,22 @@
 
         lax.fori_loop(0, wide, hints, 0)
 
-        def frame(f, _):
-            s, r = lax.div(f, frames), lax.rem(f, frames)
-            spots = [BAND + f + meta[s, r, j] for j in range(spans)]
-            flag = meta[s, r, spans].astype(F32)
-            for h in range(width // HEAD_DIM):
-                cols = slice(h * HEAD_DIM, (h + 1) * HEAD_DIM)
-                out = attend(q_s[f, :, cols], band(k_s, spots, cols), band(c_s, spots, cols))
+        heads = [slice(h * HEAD_DIM, (h + 1) * HEAD_DIM) for h in range(width // HEAD_DIM)]
+
+        def joint(s, _):
+            at, jobs = [], []
+            for r in range(frames):
+                f = s * frames + r
+                spots = [BAND + f + meta[s, r, j] for j in range(spans)]
+                for cols in heads:
+                    at.append((f, meta[s, r, spans].astype(F32), cols))
+                    jobs.append((q_s[f, :, cols], band(k_s, spots, cols), band(c_s, spots, cols)))
+            for (f, flag, cols), out in zip(at, attend(jobs)):
                 residual = (flag * g_s[:, cols] * out.astype(F32)).astype(BF16)
                 m_s[f, :, cols] = (v_s[BAND + f, :, cols].astype(F32) + residual.astype(F32)).astype(BF16)
             return 0
 
-        lax.fori_loop(0, total, frame, 0)
+        lax.fori_loop(0, GROUP, joint, 0)
         move([(m_s, outs[0]), (m_s.at[pl.ds(total - BAND, BAND)], outs[1]), (m_s.at[pl.ds(0, BAND)], outs[2])], sems)
 
     outs = [rows((total, toks, width)), rows((BAND, toks, width)), rows((BAND, toks, width))]
@@ -240,15 +251,21 @@
             todo.append((kv[k].at[pl.ds(0, frames)], k_s.at[pl.ds(BAND + at, frames)]))
         move(todo, sems)
 
-        def frame(f, _):
-            s, r = lax.div(f, frames), lax.rem(f, frames)
-            spots = [BAND + f + meta[s, r, j] for j in range(spans)]
-            for h in range(width // HEAD_DIM):
-                cols = slice(h * HEAD_DIM, (h + 1) * HEAD_DIM)
-                o_s[f, :, cols] = attend(q_s[f, :, cols], band(k_s, spots, cols), band(m_s, spots, cols))
+        heads = [slice(h * HEAD_DIM, (h + 1) * HEAD_DIM) for h in range(width // HEAD_DIM)]
+
+        def joint(s, _):
+            at, jobs = [], []
+            for r in range(frames):
+                f = s * frames + r
+                spots = [BAND + f + meta[s, r, j] for j in range(spans)]
+                for cols in heads:
+                    at.append((f, cols))
+                    jobs.append((q_s[f, :, cols], band(k_s, spots, cols), band(m_s, spots, cols)))
+            for (f, cols), out in zip(at, attend(jobs)):
+                o_s[f, :, cols] = out
             return 0
 
-        lax.fori_loop(0, total, frame, 0)
+        lax.fori_loop(0, GROUP, joint, 0)
         move([(o_s.at[pl.ds((mine ^ k) * frames, frames)], outs[k]) for k in range(GROUP)], sems)
 
     scratch = [

time: 180 us -> 136 us (0.76)
  Pallas kernels: 94.5 us -> 49.7 us
    pallas_call x18, Pallas kernels: 94.5 us -> 49.7 us  [run(): pl.pallas_call(body, out_shape=list(outs), in_specs=[SMEM] * a + [ANY] *...]
  transfers between devices with their start and end apart: 39 -> 39, of which waited for: 10 -> 10; matrix products, arithmetic and copies ran while one was open for 0% -> 0% of each run, Pallas kernels for 52% -> 36%
where the time goes in v2:
time: 136 us; the launch traced here: 135 us
  Pallas kernels  49.7 us (37%)
  starting transfers between devices  46.6 us (34%)
  waiting for transfers between devices  36.7 us (27%)
  local copies, waits for them, and re-layouts  2.1 us (2%)
    pallas_call x18, Pallas kernels, run(): pl.pallas_call(body, out_shape=list(outs), in_specs=[SMEM] * a + [ANY] *...  49.7 us
    ppermute x27, waiting for transfers between devices, exchange(): lax.ppermute(parts[k], 'tm', across[k])  33.5 us
    ppermute x27, starting transfers between devices, exchange(): lax.ppermute(parts[k], 'tm', across[k])  27.3 us
    ppermute x3, starting transfers between devices, body(): lax.ppermute(got[2], 'tm', downward)  9.75 us
    ppermute x3, starting transfers between devices, body(): lax.ppermute(start, 'tm', downward)  6.75 us
    ppermute x3, waiting for transfers between devices, body(): lax.ppermute(start, 'tm', downward)  3.12 us
  transfers between devices with their start and end apart: 39, of which 10 were waited for; matrix products, arithmetic and copies ran while one was open for 0% of the time, Pallas kernels for 36%

profile of v2, /device:TPU:1, one launch (start us, length us, event | category | flops | bytes accessed | tf_op | source)
XLA Modules:
  0.0 135.3 jit_solution(16099869727711653407)
XLA Ops:
  2.2 2.3 %collective-permute-start.4 = (bf16[2,64,384]{2,1,0:T(8,128)(2,1)S(1)}, bf16[2,64,384]{2,1,0:T(8,128)(2,1)S(1)}, u32[]{:S(2)}, u32[]{:S(2)}) collective-permute-start(bf16[2,64,384]{2,1,0:T(8,128)(2,1)S(1)} %get-tuple-element.64), channel_id=1, source_target_pairs={{0,2},{1,3},{2,0},{3,1},{4,6},{5,7},{6,4},{7,5},{8,10},{9,11},{10,... | collective-permute-start | bytes 294920 | tf_op jit(solution)/shard_map/ppermute | solution.py:310
  9.9 2.2 %collective-permute-done.5.refs_8_.refs_9_ = bf16[2,64,384]{2,1,0:T(8,128)(2,1)S(1)} collective-permute-done((bf16[2,64,384]{2,1,0:T(8,128)(2,1)S(1)}, bf16[2,64,384]{2,1,0:T(8,128)(2,1)S(1)}, u32[]{:S(2)}, u32[]{:S(2)}) %collective-permute-start.5) | collective-permute-done | bytes 98336 | tf_op jit(solution)/shard_map/ppermute | solution.py:310
  14.4 2.1 %collective-permute-done.1.refs_3_.refs_4_ = bf16[5,64,384]{2,1,0:T(8,128)(2,1)S(1)} collective-permute-done((bf16[5,64,384]{2,1,0:T(8,128)(2,1)S(1)}, bf16[5,64,384]{2,1,0:T(8,128)(2,1)S(1)}, u32[]{:S(2)}, u32[]{:S(2)}) %collective-permute-start.1) | collective-permute-done | bytes 245792 | tf_op jit(solution)/shard_map/ppermute | solution.py:310
  16.5 1.9 %collective-permute-start.10 = (bf16[4,64,384]{2,1,0:T(8,128)(2,1)S(1)}, bf16[4,64,384]{2,1,0:T(8,128)(2,1)S(1)}, u32[]{:S(2)}, u32[]{:S(2)}) collective-permute-start(bf16[4,64,384]{2,1,0:T(8,128)(2,1)S(1)} %get-tuple-element.72), channel_id=1, source_target_pairs={{0,3},{1,2},{2,1},{3,0},{4,7},{5,6},{6,5},{7,4},{8,11},{9,10},{10,... | collective-permute-start | bytes 589832 | tf_op jit(solution)/shard_map/ppermute | solution.py:310
  18.4 4.2 %collective-permute-done.2.refs_4_.refs_5_ = bf16[5,64,384]{2,1,0:T(8,128)(2,1)S(1)} collective-permute-done((bf16[5,64,384]{2,1,0:T(8,128)(2,1)S(1)}, bf16[5,64,384]{2,1,0:T(8,128)(2,1)S(1)}, u32[]{:S(2)}, u32[]{:S(2)}) %collective-permute-start.2) | collective-permute-done | bytes 245792 | tf_op jit(solution)/shard_map/ppermute | solution.py:310
  23.1 4.2 %collective-permute-done.22.refs_3_.refs_4_ = bf16[4,64,512]{2,1,0:T(8,128)(2,1)S(1)} collective-permute-done((bf16[4,64,512]{2,1,0:T(8,128)(2,1)S(1)}, bf16[4,64,512]{2,1,0:T(8,128)(2,1)S(1)}, u32[]{:S(2)}, u32[]{:S(2)}) %collective-permute-start.22) | collective-permute-done | bytes 262176 | tf_op jit(solution)/shard_map/ppermute | solution.py:310
  28.6 5.6 %collective-permute-done.23.refs_4_.refs_5_ = bf16[4,64,512]{2,1,0:T(8,128)(2,1)S(1)} collective-permute-done((bf16[4,64,512]{2,1,0:T(8,128)(2,1)S(1)}, bf16[4,64,512]{2,1,0:T(8,128)(2,1)S(1)}, u32[]{:S(2)}, u32[]{:S(2)}) %collective-permute-start.23) | collective-permute-done | bytes 262176 | tf_op jit(solution)/shard_map/ppermute | solution.py:310
  35.5 8.7 %collective-permute-done.25.refs_8_ = bf16[2,64,512]{2,1,0:T(8,128)(2,1)S(1)} collective-permute-done((bf16[2,64,512]{2,1,0:T(8,128)(2,1)S(1)}, bf16[2,64,512]{2,1,0:T(8,128)(2,1)S(1)}, u32[]{:S(2)}, u32[]{:S(2)}) %collective-permute-start.25) | collective-permute-done | bytes 131104 | tf_op jit(solution)/shard_map/ppermute | solution.py:310
  45.5 2.0 %collective-permute-start.7 = (bf16[5,64,384]{2,1,0:T(8,128)(2,1)S(1)}, bf16[5,64,384]{2,1,0:T(8,128)(2,1)S(1)}, u32[]{:S(2)}, u32[]{:S(2)}) collective-permute-start(bf16[5,64,384]{2,1,0:T(8,128)(2,1)S(1)} %get-tuple-element.67), channel_id=1, source_target_pairs={{0,12},{1,13},{2,14},{3,15},{4,0},{5,1},{6,2},{7,3},{8,4},{9,5},{1... | collective-permute-start | bytes 737288 | tf_op jit(solution)/shard_map/ppermute | solution.py:328
  49.0 2.2 %collective-permute-start.26 = (bf16[2,64,512]{2,1,0:T(8,128)(2,1)S(1)}, bf16[2,64,512]{2,1,0:T(8,128)(2,1)S(1)}, u32[]{:S(2)}, u32[]{:S(2)}) collective-permute-start(bf16[2,64,512]{2,1,0:T(8,128)(2,1)S(1)} %get-tuple-element.94), channel_id=1, source_target_pairs={{0,3},{1,2},{2,1},{3,0},{4,7},{5,6},{6,5},{7,4},{8,11},{9,10},{10,... | collective-permute-start | bytes 393224 | tf_op jit(solution)/shard_map/ppermute | solution.py:310
  51.8 3.2 %collective-permute-done.26.refs_9_ = bf16[2,64,512]{2,1,0:T(8,128)(2,1)S(1)} collective-permute-done((bf16[2,64,512]{2,1,0:T(8,128)(2,1)S(1)}, bf16[2,64,512]{2,1,0:T(8,128)(2,1)S(1)}, u32[]{:S(2)}, u32[]{:S(2)}) %collective-permute-start.26) | collective-permute-done | bytes 131104 | tf_op jit(solution)/shard_map/ppermute | solution.py:310
  55.0 3.3 %collective-permute-start.15 = (bf16[4,64,384]{2,1,0:T(8,128)(2,1)S(1)}, bf16[4,64,384]{2,1,0:T(8,128)(2,1)S(1)}, u32[]{:S(2)}, u32[]{:S(2)}) collective-permute-start(bf16[4,64,384]{2,1,0:T(8,128)(2,1)S(1)} %get-tuple-element.78), channel_id=1, source_target_pairs={{0,12},{1,13},{2,14},{3,15},{4,0},{5,1},{6,2},{7,3},{8,4},{9,5},{1... | collective-permute-start | bytes 589832 | tf_op jit(solution)/shard_map/ppermute | solution.py:328
  61.0 3.1 %collective-permute-done.28.refs_11_ = bf16[4,64,512]{2,1,0:T(8,128)(2,1)S(1)} collective-permute-done((bf16[4,64,512]{2,1,0:T(8,128)(2,1)S(1)}, bf16[4,64,512]{2,1,0:T(8,128)(2,1)S(1)}, u32[]{:S(2)}, u32[]{:S(2)}) %collective-permute-start.28) | collective-permute-done | bytes 262176 | tf_op jit(solution)/shard_map/ppermute | solution.py:328
  64.1 3.9 %collective-permute-start.13 = (bf16[2,64,384]{2,1,0:T(8,128)(2,1)S(1)}, bf16[2,64,384]{2,1,0:T(8,128)(2,1)S(1)}, u32[]{:S(2)}, u32[]{:S(2)}) collective-permute-start(bf16[2,64,384]{2,1,0:T(8,128)(2,1)S(1)} %get-tuple-element.76), channel_id=1, source_target_pairs={{0,3},{1,2},{2,1},{3,0},{4,7},{5,6},{6,5},{7,4},{8,11},{9,10},{10,... | collective-permute-start | bytes 294920 | tf_op jit(solution)/shard_map/ppermute | solution.py:310
  67.9 8.4 %shard_map.85 = (bf16[8,64,384]{2,1,0:T(8,128)(2,1)S(1)}, bf16[2,64,384]{2,1,0:T(8,128)(2,1)S(1)}, bf16[2,64,384]{2,1,0:T(8,128)(2,1)S(1)}, bf16[12,64,128]{2,1,0:T(8,128)(2,1)S(1)}, s32[4,8,128]{2,1,0:T(8,128)S(1)}) custom-call(s32[1]{0:T(128)} %bitcast.refs_0_, bf16[5,64,384]{2,1,0:T(8,128)(2,1)S(1)} %get-tuple-element.58.refs_1_.refs_2_, ...), custom_call_target="tpu_custom_call" | custom-call | flops 150994944 | bytes 1966080 | tf_op jit(solution)/shard_map/pallas_call | solution.py:26
  76.4 9.4 %shard_map.94 = (bf16[8,64,512]{2,1,0:T(8,128)(2,1)S(1)}, bf16[2,64,512]{2,1,0:T(8,128)(2,1)S(1)}, bf16[2,64,512]{2,1,0:T(8,128)(2,1)S(1)}) custom-call(s32[1]{0:T(128)} %bitcast.refs_0_, s32[4,8,128]{2,1,0:T(8,128)S(1)} %get-tuple-element.68.refs_1_, bf16[4,64,512]{2,1,0:T(8,128)(2,1)S(1)} %get-tuple-element.87.refs_1_.refs_2_, ...), custom_call_target="tpu_custom_call" | custom-call | flops 201326592 | bytes 2621440 | tf_op jit(solution)/shard_map/pallas_call | solution.py:26
  85.9 3.2 %collective-permute-start.30 = (bf16[2,64,512]{2,1,0:T(8,128)(2,1)S(1)}, bf16[2,64,512]{2,1,0:T(8,128)(2,1)S(1)}, u32[]{:S(2)}, u32[]{:S(2)}) collective-permute-start(bf16[2,64,512]{2,1,0:T(8,128)(2,1)S(1)} %get-tuple-element.99), channel_id=1, source_target_pairs={{0,12},{1,13},{2,14},{3,15},{4,0},{5,1},{6,2},{7,3},{8,4},{9,5},{1... | collective-permute-start | bytes 393224 | tf_op jit(solution)/shard_map/ppermute | solution.py:337
  89.2 3.3 %collective-permute-start.35 = (bf16[2,64,384]{2,1,0:T(8,128)(2,1)S(1)}, bf16[2,64,384]{2,1,0:T(8,128)(2,1)S(1)}, u32[]{:S(2)}, u32[]{:S(2)}) collective-permute-start(bf16[2,64,384]{2,1,0:T(8,128)(2,1)S(1)} %get-tuple-element.106), channel_id=1, source_target_pairs={{0,12},{1,13},{2,14},{3,15},{4,0},{5,1},{6,2},{7,3},{8,4},{9,5},{1... | collective-permute-start | bytes 294920 | tf_op jit(solution)/shard_map/ppermute | solution.py:337
  92.4 8.5 %shard_map.89 = (bf16[8,64,384]{2,1,0:T(8,128)(2,1)S(1)}, bf16[2,64,384]{2,1,0:T(8,128)(2,1)S(1)}, bf16[2,64,384]{2,1,0:T(8,128)(2,1)S(1)}) custom-call(s32[1]{0:T(128)} %bitcast.refs_0_, s32[4,8,128]{2,1,0:T(8,128)S(1)} %get-tuple-element.68.refs_1_, bf16[4,64,384]{2,1,0:T(8,128)(2,1)S(1)} %get-tuple-element.69.refs_1_.refs_2_, ...), custom_call_target="tpu_custom_call" | custom-call | flops 150994944 | bytes 1966080 | tf_op jit(solution)/shard_map/pallas_call | solution.py:26
  101.0 3.2 %collective-permute-start.17 = (bf16[2,64,384]{2,1,0:T(8,128)(2,1)S(1)}, bf16[2,64,384]{2,1,0:T(8,128)(2,1)S(1)}, u32[]{:S(2)}, u32[]{:S(2)}) collective-permute-start(bf16[2,64,384]{2,1,0:T(8,128)(2,1)S(1)} %get-tuple-element.82), channel_id=1, source_target_pairs={{0,12},{1,13},{2,14},{3,15},{4,0},{5,1},{6,2},{7,3},{8,4},{9,5},{1... | collective-permute-start | bytes 294920 | tf_op jit(solution)/shard_map/ppermute | solution.py:337
  104.2 5.7 %shard_map.96 = (bf16[2,64,384]{2,1,0:T(8,128)(2,1)S(1)}, bf16[2,64,384]{2,1,0:T(8,128)(2,1)S(1)}, bf16[2,64,384]{2,1,0:T(8,128)(2,1)S(1)}, bf16[2,64,384]{2,1,0:T(8,128)(2,1)S(1)}) custom-call(s32[1]{0:T(128)} %bitcast.refs_0_, s32[4,8,128]{2,1,0:T(8,128)S(1)} %get-tuple-element.68.refs_1_, bf16[5,64,384]{2,1,0:T(8,128)(2,1)S(1)} %get-tuple-element.58.refs_1_.refs_2_, ...), custom_call_target="tpu_custom_call" | custom-call | flops 150994944 | bytes 1572864 | tf_op jit(solution)/shard_map/pallas_call | solution.py:26
  111.3 6.6 %shard_map.95 = (bf16[2,64,512]{2,1,0:T(8,128)(2,1)S(1)}, bf16[2,64,512]{2,1,0:T(8,128)(2,1)S(1)}, bf16[2,64,512]{2,1,0:T(8,128)(2,1)S(1)}, bf16[2,64,512]{2,1,0:T(8,128)(2,1)S(1)}) custom-call(s32[1]{0:T(128)} %bitcast.refs_0_, s32[4,8,128]{2,1,0:T(8,128)S(1)} %get-tuple-element.68.refs_1_, bf16[4,64,512]{2,1,0:T(8,128)(2,1)S(1)} %get-tuple-element.87.refs_1_.refs_2_, ...), custom_call_target="tpu_custom_call" | custom-call | flops 201326592 | bytes 2097152 | tf_op jit(solution)/shard_map/pallas_call | solution.py:26
  121.6 5.7 %shard_map.90 = (bf16[2,64,384]{2,1,0:T(8,128)(2,1)S(1)}, bf16[2,64,384]{2,1,0:T(8,128)(2,1)S(1)}, bf16[2,64,384]{2,1,0:T(8,128)(2,1)S(1)}, bf16[2,64,384]{2,1,0:T(8,128)(2,1)S(1)}) custom-call(s32[1]{0:T(128)} %bitcast.refs_0_, s32[4,8,128]{2,1,0:T(8,128)S(1)} %get-tuple-element.68.refs_1_, bf16[4,64,384]{2,1,0:T(8,128)(2,1)S(1)} %get-tuple-element.69.refs_1_.refs_2_, ...), custom_call_target="tpu_custom_call" | custom-call | flops 150994944 | bytes 1572864 | tf_op jit(solution)/shard_map/pallas_call | solution.py:26
  132.3 2.2 %collective-permute-done.20.refs_4_ = bf16[2,64,384]{2,1,0:T(8,128)(2,1)S(1)} collective-permute-done((bf16[2,64,384]{2,1,0:T(8,128)(2,1)S(1)}, bf16[2,64,384]{2,1,0:T(8,128)(2,1)S(1)}, u32[]{:S(2)}, u32[]{:S(2)}) %collective-permute-start.20) | collective-permute-done | bytes 98336 | tf_op jit(solution)/shard_map/ppermute | solution.py:310
  (90 shorter events, 29.7 us)
Async XLA Ops:
  8.5 14.1 %collective-permute-start.2 = (bf16[5,64,384]{2,1,0:T(8,128)(2,1)S(1)}, bf16[5,64,384]{2,1,0:T(8,128)(2,1)S(1)}, u32[]{:S(2)}, u32[]{:S(2)}) collective-permute-start(bf16[5,64,384]{2,1,0:T(8,128)(2,1)S(1)} %get-tuple-element.61), channel_id=1, source_target_pairs={{0,3},{1,2},{2,1},{3,0},{4,7},{5,6},{6,5},{7,4},{8,11},{9,10},{10,... | collective-permute-start | bytes 737288 | tf_op jit(solution)/shard_map/ppermute | solution.py:310
  12.1 10.5 %collective-permute-start.21 = (bf16[4,64,512]{2,1,0:T(8,128)(2,1)S(1)}, bf16[4,64,512]{2,1,0:T(8,128)(2,1)S(1)}, u32[]{:S(2)}, u32[]{:S(2)}) collective-permute-start(bf16[4,64,512]{2,1,0:T(8,128)(2,1)S(1)} %get-tuple-element.88), channel_id=1, source_target_pairs={{0,1},{1,0},{2,3},{3,2},{4,5},{5,4},{6,7},{7,6},{8,9},{9,8},{10,11... | collective-permute-start | bytes 786440 | tf_op jit(solution)/shard_map/ppermute | solution.py:310
  12.1 15.3 %collective-permute-start.22 = (bf16[4,64,512]{2,1,0:T(8,128)(2,1)S(1)}, bf16[4,64,512]{2,1,0:T(8,128)(2,1)S(1)}, u32[]{:S(2)}, u32[]{:S(2)}) collective-permute-start(bf16[4,64,512]{2,1,0:T(8,128)(2,1)S(1)} %get-tuple-element.89), channel_id=1, source_target_pairs={{0,2},{1,3},{2,0},{3,1},{4,6},{5,7},{6,4},{7,5},{8,10},{9,11},{10,... | collective-permute-start | bytes 786440 | tf_op jit(solution)/shard_map/ppermute | solution.py:310
  12.6 21.5 %collective-permute-start.23 = (bf16[4,64,512]{2,1,0:T(8,128)(2,1)S(1)}, bf16[4,64,512]{2,1,0:T(8,128)(2,1)S(1)}, u32[]{:S(2)}, u32[]{:S(2)}) collective-permute-start(bf16[4,64,512]{2,1,0:T(8,128)(2,1)S(1)} %get-tuple-element.90), channel_id=1, source_target_pairs={{0,3},{1,2},{2,1},{3,0},{4,7},{5,6},{6,5},{7,4},{8,11},{9,10},{10,... | collective-permute-start | bytes 786440 | tf_op jit(solution)/shard_map/ppermute | solution.py:310
  16.5 29.0 %collective-permute-start.10 = (bf16[4,64,384]{2,1,0:T(8,128)(2,1)S(1)}, bf16[4,64,384]{2,1,0:T(8,128)(2,1)S(1)}, u32[]{:S(2)}, u32[]{:S(2)}) collective-permute-start(bf16[4,64,384]{2,1,0:T(8,128)(2,1)S(1)} %get-tuple-element.72), channel_id=1, source_target_pairs={{0,3},{1,2},{2,1},{3,0},{4,7},{5,6},{6,5},{7,4},{8,11},{9,10},{10,... | collective-permute-start | bytes 589832 | tf_op jit(solution)/shard_map/ppermute | solution.py:310
  22.6 25.0 %collective-permute-start.8 = (bf16[4,64,384]{2,1,0:T(8,128)(2,1)S(1)}, bf16[4,64,384]{2,1,0:T(8,128)(2,1)S(1)}, u32[]{:S(2)}, u32[]{:S(2)}) collective-permute-start(bf16[4,64,384]{2,1,0:T(8,128)(2,1)S(1)} %get-tuple-element.70), channel_id=1, source_target_pairs={{0,1},{1,0},{2,3},{3,2},{4,5},{5,4},{6,7},{7,6},{8,9},{9,8},{10,11... | collective-permute-start | bytes 589832 | tf_op jit(solution)/shard_map/ppermute | solution.py:310
  22.6 26.4 %collective-permute-start.9 = (bf16[4,64,384]{2,1,0:T(8,128)(2,1)S(1)}, bf16[4,64,384]{2,1,0:T(8,128)(2,1)S(1)}, u32[]{:S(2)}, u32[]{:S(2)}) collective-permute-start(bf16[4,64,384]{2,1,0:T(8,128)(2,1)S(1)} %get-tuple-element.71), channel_id=1, source_target_pairs={{0,2},{1,3},{2,0},{3,1},{4,6},{5,7},{6,4},{7,5},{8,10},{9,11},{10,... | collective-permute-start | bytes 589832 | tf_op jit(solution)/shard_map/ppermute | solution.py:310
  27.4 16.9 %collective-permute-start.25 = (bf16[2,64,512]{2,1,0:T(8,128)(2,1)S(1)}, bf16[2,64,512]{2,1,0:T(8,128)(2,1)S(1)}, u32[]{:S(2)}, u32[]{:S(2)}) collective-permute-start(bf16[2,64,512]{2,1,0:T(8,128)(2,1)S(1)} %get-tuple-element.93), channel_id=1, source_target_pairs={{0,2},{1,3},{2,0},{3,1},{4,6},{5,7},{6,4},{7,5},{8,10},{9,11},{10,... | collective-permute-start | bytes 393224 | tf_op jit(solution)/shard_map/ppermute | solution.py:310
  34.1 20.9 %collective-permute-start.6 = (bf16[5,64,384]{2,1,0:T(8,128)(2,1)S(1)}, bf16[5,64,384]{2,1,0:T(8,128)(2,1)S(1)}, u32[]{:S(2)}, u32[]{:S(2)}) collective-permute-start(bf16[5,64,384]{2,1,0:T(8,128)(2,1)S(1)} %get-tuple-element.66), channel_id=1, source_target_pairs={{0,4},{1,5},{2,6},{3,7},{4,8},{5,9},{6,10},{7,11},{8,12},{9,13},{1... | collective-permute-start | bytes 737288 | tf_op jit(solution)/shard_map/ppermute | solution.py:328
  44.2 16.0 %collective-permute-start.27 = (bf16[4,64,512]{2,1,0:T(8,128)(2,1)S(1)}, bf16[4,64,512]{2,1,0:T(8,128)(2,1)S(1)}, u32[]{:S(2)}, u32[]{:S(2)}) collective-permute-start(bf16[4,64,512]{2,1,0:T(8,128)(2,1)S(1)} %get-tuple-element.95), channel_id=1, source_target_pairs={{0,4},{1,5},{2,6},{3,7},{4,8},{5,9},{6,10},{7,11},{8,12},{9,13},{1... | collective-permute-start | bytes 786440 | tf_op jit(solution)/shard_map/ppermute | solution.py:328
  45.5 12.9 %collective-permute-start.7 = (bf16[5,64,384]{2,1,0:T(8,128)(2,1)S(1)}, bf16[5,64,384]{2,1,0:T(8,128)(2,1)S(1)}, u32[]{:S(2)}, u32[]{:S(2)}) collective-permute-start(bf16[5,64,384]{2,1,0:T(8,128)(2,1)S(1)} %get-tuple-element.67), channel_id=1, source_target_pairs={{0,12},{1,13},{2,14},{3,15},{4,0},{5,1},{6,2},{7,3},{8,4},{9,5},{1... | collective-permute-start | bytes 737288 | tf_op jit(solution)/shard_map/ppermute | solution.py:328
  47.6 16.5 %collective-permute-start.28 = (bf16[4,64,512]{2,1,0:T(8,128)(2,1)S(1)}, bf16[4,64,512]{2,1,0:T(8,128)(2,1)S(1)}, u32[]{:S(2)}, u32[]{:S(2)}) collective-permute-start(bf16[4,64,512]{2,1,0:T(8,128)(2,1)S(1)} %get-tuple-element.96), channel_id=1, source_target_pairs={{0,12},{1,13},{2,14},{3,15},{4,0},{5,1},{6,2},{7,3},{8,4},{9,5},{1... | collective-permute-start | bytes 786440 | tf_op jit(solution)/shard_map/ppermute | solution.py:328
  55.0 34.2 %collective-permute-start.14 = (bf16[4,64,384]{2,1,0:T(8,128)(2,1)S(1)}, bf16[4,64,384]{2,1,0:T(8,128)(2,1)S(1)}, u32[]{:S(2)}, u32[]{:S(2)}) collective-permute-start(bf16[4,64,384]{2,1,0:T(8,128)(2,1)S(1)} %get-tuple-element.77), channel_id=1, source_target_pairs={{0,4},{1,5},{2,6},{3,7},{4,8},{5,9},{6,10},{7,11},{8,12},{9,13},{1... | collective-permute-start | bytes 589832 | tf_op jit(solution)/shard_map/ppermute | solution.py:328
  55.0 37.4 %collective-permute-start.15 = (bf16[4,64,384]{2,1,0:T(8,128)(2,1)S(1)}, bf16[4,64,384]{2,1,0:T(8,128)(2,1)S(1)}, u32[]{:S(2)}, u32[]{:S(2)}) collective-permute-start(bf16[4,64,384]{2,1,0:T(8,128)(2,1)S(1)} %get-tuple-element.78), channel_id=1, source_target_pairs={{0,12},{1,13},{2,14},{3,15},{4,0},{5,1},{6,2},{7,3},{8,4},{9,5},{1... | collective-permute-start | bytes 589832 | tf_op jit(solution)/shard_map/ppermute | solution.py:328
  58.4 27.4 %collective-permute-start.11 = (bf16[2,64,384]{2,1,0:T(8,128)(2,1)S(1)}, bf16[2,64,384]{2,1,0:T(8,128)(2,1)S(1)}, u32[]{:S(2)}, u32[]{:S(2)}) collective-permute-start(bf16[2,64,384]{2,1,0:T(8,128)(2,1)S(1)} %get-tuple-element.74), channel_id=1, source_target_pairs={{0,1},{1,0},{2,3},{3,2},{4,5},{5,4},{6,7},{7,6},{8,9},{9,8},{10,11... | collective-permute-start | bytes 294920 | tf_op jit(solution)/shard_map/ppermute | solution.py:310
  60.3 25.6 %collective-permute-start.12 = (bf16[2,64,384]{2,1,0:T(8,128)(2,1)S(1)}, bf16[2,64,384]{2,1,0:T(8,128)(2,1)S(1)}, u32[]{:S(2)}, u32[]{:S(2)}) collective-permute-start(bf16[2,64,384]{2,1,0:T(8,128)(2,1)S(1)} %get-tuple-element.75), channel_id=1, source_target_pairs={{0,2},{1,3},{2,0},{3,1},{4,6},{5,7},{6,4},{7,5},{8,10},{9,11},{10,... | collective-permute-start | bytes 294920 | tf_op jit(solution)/shard_map/ppermute | solution.py:310
  64.1 25.1 %collective-permute-start.13 = (bf16[2,64,384]{2,1,0:T(8,128)(2,1)S(1)}, bf16[2,64,384]{2,1,0:T(8,128)(2,1)S(1)}, u32[]{:S(2)}, u32[]{:S(2)}) collective-permute-start(bf16[2,64,384]{2,1,0:T(8,128)(2,1)S(1)} %get-tuple-element.76), channel_id=1, source_target_pairs={{0,3},{1,2},{2,1},{3,0},{4,7},{5,6},{6,5},{7,4},{8,11},{9,10},{10,... | collective-permute-start | bytes 294920 | tf_op jit(solution)/shard_map/ppermute | solution.py:310
  85.8 25.5 %collective-permute-start.29 = (bf16[2,64,512]{2,1,0:T(8,128)(2,1)S(1)}, bf16[2,64,512]{2,1,0:T(8,128)(2,1)S(1)}, u32[]{:S(2)}, u32[]{:S(2)}) collective-permute-start(bf16[2,64,512]{2,1,0:T(8,128)(2,1)S(1)} %get-tuple-element.98), channel_id=1, source_target_pairs={{0,4},{1,5},{2,6},{3,7},{4,8},{5,9},{6,10},{7,11},{8,12},{9,13},{1... | collective-permute-start | bytes 393224 | tf_op jit(solution)/shard_map/ppermute | solution.py:337
  85.9 25.4 %collective-permute-start.30 = (bf16[2,64,512]{2,1,0:T(8,128)(2,1)S(1)}, bf16[2,64,512]{2,1,0:T(8,128)(2,1)S(1)}, u32[]{:S(2)}, u32[]{:S(2)}) collective-permute-start(bf16[2,64,512]{2,1,0:T(8,128)(2,1)S(1)} %get-tuple-element.99), channel_id=1, source_target_pairs={{0,12},{1,13},{2,14},{3,15},{4,0},{5,1},{6,2},{7,3},{8,4},{9,5},{1... | collective-permute-start | bytes 393224 | tf_op jit(solution)/shard_map/ppermute | solution.py:337
  89.2 11.8 %collective-permute-start.34 = (bf16[2,64,384]{2,1,0:T(8,128)(2,1)S(1)}, bf16[2,64,384]{2,1,0:T(8,128)(2,1)S(1)}, u32[]{:S(2)}, u32[]{:S(2)}) collective-permute-start(bf16[2,64,384]{2,1,0:T(8,128)(2,1)S(1)} %get-tuple-element.105), channel_id=1, source_target_pairs={{0,4},{1,5},{2,6},{3,7},{4,8},{5,9},{6,10},{7,11},{8,12},{9,13},{1... | collective-permute-start | bytes 294920 | tf_op jit(solution)/shard_map/ppermute | solution.py:337
  89.2 15.1 %collective-permute-start.35 = (bf16[2,64,384]{2,1,0:T(8,128)(2,1)S(1)}, bf16[2,64,384]{2,1,0:T(8,128)(2,1)S(1)}, u32[]{:S(2)}, u32[]{:S(2)}) collective-permute-start(bf16[2,64,384]{2,1,0:T(8,128)(2,1)S(1)} %get-tuple-element.106), channel_id=1, source_target_pairs={{0,12},{1,13},{2,14},{3,15},{4,0},{5,1},{6,2},{7,3},{8,4},{9,5},{1... | collective-permute-start | bytes 294920 | tf_op jit(solution)/shard_map/ppermute | solution.py:337
  100.9 17.7 %collective-permute-start.16 = (bf16[2,64,384]{2,1,0:T(8,128)(2,1)S(1)}, bf16[2,64,384]{2,1,0:T(8,128)(2,1)S(1)}, u32[]{:S(2)}, u32[]{:S(2)}) collective-permute-start(bf16[2,64,384]{2,1,0:T(8,128)(2,1)S(1)} %get-tuple-element.81), channel_id=1, source_target_pairs={{0,4},{1,5},{2,6},{3,7},{4,8},{5,9},{6,10},{7,11},{8,12},{9,13},{1... | collective-permute-start | bytes 294920 | tf_op jit(solution)/shard_map/ppermute | solution.py:337
  101.0 19.2 %collective-permute-start.17 = (bf16[2,64,384]{2,1,0:T(8,128)(2,1)S(1)}, bf16[2,64,384]{2,1,0:T(8,128)(2,1)S(1)}, u32[]{:S(2)}, u32[]{:S(2)}) collective-permute-start(bf16[2,64,384]{2,1,0:T(8,128)(2,1)S(1)} %get-tuple-element.82), channel_id=1, source_target_pairs={{0,12},{1,13},{2,14},{3,15},{4,0},{5,1},{6,2},{7,3},{8,4},{9,5},{1... | collective-permute-start | bytes 294920 | tf_op jit(solution)/shard_map/ppermute | solution.py:337
  110.0 10.7 %collective-permute-start.36 = (bf16[2,64,384]{2,1,0:T(8,128)(2,1)S(1)}, bf16[2,64,384]{2,1,0:T(8,128)(2,1)S(1)}, u32[]{:S(2)}, u32[]{:S(2)}) collective-permute-start(bf16[2,64,384]{2,1,0:T(8,128)(2,1)S(1)} %get-tuple-element.108), channel_id=1, source_target_pairs={{0,1},{1,0},{2,3},{3,2},{4,5},{5,4},{6,7},{7,6},{8,9},{9,8},{10,11... | collective-permute-start | bytes 294920 | tf_op jit(solution)/shard_map/ppermute | solution.py:310
  (24 other events, 222.5 us)

commit v3 on v2

v3 whole, which is shorter than its diff:
```python
import jax
import jax.numpy as jnp
from jax import lax
from jax.experimental import pallas as pl
from jax.experimental.pallas import tpu as pltpu
from jax.sharding import PartitionSpec as P

HEAD_DIM = 128
BAND = 2
GROUP = 4
SLICES = (5, 5)
META = 8
ORDER = [("KV", 0), ("KV", 1), ("Q", 0), ("Z", 0), ("Q", 1), ("Z", 1), ("H", 0), ("H", 1), ("B", 0), ("B", 1), ("P", 0), ("P", 1)]
DEPTH_Y, DEPTH_Z = 2, 2
F32 = jnp.float32
BF16 = jnp.bfloat16
I32 = jnp.int32
VMEM = pl.BlockSpec(memory_space=pltpu.VMEM)
SMEM = pl.BlockSpec(memory_space=pltpu.SMEM)
HBM = pl.BlockSpec(memory_space=pltpu.HBM)


def run(kernel, name, ins, outs, scratch, copies, scalars=(), where=VMEM, to=VMEM, aliases=None, us=1.0):
    a, b, c, d = len(scalars), len(ins), len(outs), len(scratch)

    def body(*refs):
        kernel(refs[:a], refs[a : a + b], refs[a + b : a + b + c], refs[a + b + c : a + b + c + d], refs[-1])

    return pl.pallas_call(
        body,
        out_shape=list(outs),
        in_specs=[SMEM] * a + (where if isinstance(where, list) else [where] * b),
        out_specs=[to] * c,
        scratch_shapes=[*scratch, pltpu.SemaphoreType.DMA((max(copies, 1),))],
        input_output_aliases=aliases or {},
        compiler_params=pltpu.CompilerParams(vmem_limit_bytes=16 * 1024 * 1024),
        cost_estimate=pl.CostEstimate(flops=1, bytes_accessed=int(us * 3.4e6), transcendentals=0),
        name=name,
    )(*scalars, *ins)


def move(pairs, sems):
    copies = [pltpu.make_async_copy(s, d, sems.at[i]) for i, (s, d) in enumerate(pairs)]
    for copy in copies:
        copy.start()
    for copy in copies:
        copy.wait()


def lanes(me, quarter, first, width):
    return pl.ds(pl.multiple_of(me * quarter + first, HEAD_DIM), width)


def rows(shape, dtype=BF16):
    return jax.ShapeDtypeStruct(shape, dtype)


def pack_pair(me, keys, values, lead, quarter, first, width):
    frames, toks, _ = keys.shape

    def kernel(scalars, ins, outs, scratch, sems):
        mine = scalars[0][0]
        pairs = []
        for k in (1, 2, 3, 0):
            where = lanes(mine ^ k, quarter, first, width)
            pairs.append((ins[0].at[:, :, where], outs[k].at[pl.ds(0, frames)]))
            pairs.append((ins[1].at[:, :, where], outs[k].at[pl.ds(frames, frames)]))
            if lead:
                for f in range(frames):
                    pairs.append((ins[2].at[f], outs[k].at[2 * frames, :, pl.ds(f * HEAD_DIM, HEAD_DIM)]))
        if lead:
            offsets, flags = scalars[1:]
            spans = offsets.shape[1]
            row = lax.broadcasted_iota(I32, (toks, HEAD_DIM), 0)
            col = lax.broadcasted_iota(I32, (toks, HEAD_DIM), 1)
            block = jnp.zeros((toks, HEAD_DIM), F32)
            for f in range(frames):
                for j in range(spans):
                    block = jnp.where((row == f) & (col == j), offsets[f, j].astype(F32), block)
                block = jnp.where((row == f) & (col == spans), flags[f].astype(F32), block)
            scratch[0][...] = block.astype(BF16)
            for k in range(GROUP):
                pairs.append((scratch[0], outs[k].at[2 * frames, :, pl.ds(frames * HEAD_DIM, HEAD_DIM)]))
        move(pairs, sems)

    shape = (2 * frames + (1 if lead else 0), toks, width)
    return run(
        kernel,
        "pack_pair",
        [keys, values, *lead[:1]],
        [rows(shape)] * GROUP,
        [pltpu.VMEM((toks, HEAD_DIM), BF16)] if lead else [],
        GROUP * (2 + (frames + 1 if lead else 0)),
        [me, *lead[1:]],
        where=HBM,
    )


def pack_one(me, array, weight, gain, quarter, first, width):
    frames, toks, _ = array.shape

    def kernel(scalars, ins, outs, scratch, sems):
        mine = scalars[0][0]
        pairs = [(ins[0].at[:, :, lanes(mine ^ k, quarter, first, width)], outs[k]) for k in (1, 2, 3, 0)]
        for i in (1, 2):
            pairs.append((ins[i].at[:, lanes(mine, quarter, first, width)], outs[GROUP - 1 + i]))
        move(pairs, sems)

    outs = [rows((frames, toks, width))] * GROUP + [rows((weight.shape[0], width)), rows((1, width), F32)]
    return run(kernel, "pack_one", [array, weight, gain], outs, [], GROUP + 2, [me], where=HBM)


def edges(me, parts):
    def kernel(scalars, ins, outs, scratch, sems):
        mine = scalars[0][0]
        for out, owner in zip(outs, (GROUP - 1, 0)):
            for k in range(GROUP):

                @pl.when((mine ^ k) == owner)
                def _(out=out, k=k):
                    out[...] = ins[k][...]

    shape = rows(parts[0].shape)
    return run(kernel, "edges", parts, [shape, shape], [], 0, [me], us=0.2)


def attend(jobs):
    scores = [
        lax.dot_general(query, keys, (((1,), (1,)), ((), ())), preferred_element_type=F32) * HEAD_DIM ** (-0.5)
        for query, keys, _ in jobs
    ]
    tops = [jnp.max(x, axis=1, keepdims=True) for x in scores]
    scores = [jnp.exp(x - top) for x, top in zip(scores, tops)]
    scales = [1.0 / jnp.sum(x, axis=1, keepdims=True) for x in scores]
    weights = [(x * scale).astype(BF16) for x, scale in zip(scores, scales)]
    return [
        jnp.dot(w, values, preferred_element_type=F32).astype(BF16) for w, (_, _, values) in zip(weights, jobs)
    ]


def band(ref, spots, cols):
    return jnp.concatenate([ref[s, :, cols] for s in spots], axis=0)


def hint_branch(me, pairs_in, queries, before, after, weight, gain, setting, spans):
    frames, toks, width = queries[0].shape
    lead = setting is None
    total, wide = GROUP * frames, GROUP * frames + 2 * BAND
    heads = [slice(h * HEAD_DIM, (h + 1) * HEAD_DIM) for h in range(width // HEAD_DIM)]

    def kernel(scalars, ins, outs, scratch, sems):
        mine = scalars[0][0]
        kv, qs, (prev, following, w_ref, g_ref) = ins[:GROUP], ins[GROUP : 2 * GROUP], ins[2 * GROUP : 2 * GROUP + 4]
        mixed, up, down, keys_out = outs[:4]
        q_s, k_s, c_s = scratch[:3]
        if lead:
            pose_out, meta_out = outs[4:]
            meta = scratch[3]
            for k in range(GROUP):
                block = kv[k][2 * frames, : 2 * META, frames * HEAD_DIM : (frames + 1) * HEAD_DIM]
                meta_out[mine ^ k] = block.astype(F32).astype(I32)[:META]
            known = pltpu.make_async_copy(meta_out, meta, sems.at[0])
            known.start()
        else:
            meta = scalars[1]
        for k, src in enumerate([*kv, prev, following]):
            at = BAND + (mine ^ k) * frames if k < GROUP else (0 if k == GROUP else BAND + total)
            if lead:
                patches = [src[2 * frames, :, f * HEAD_DIM : (f + 1) * HEAD_DIM] for f in range(frames)]
                for f in range(frames):
                    pose_out[at + f] = patches[f]
            else:
                patches = [ins[-1][at + f] for f in range(frames)]
            hint = jnp.dot(jnp.concatenate(patches, axis=0), w_ref[...], preferred_element_type=F32)
            hint = hint.astype(BF16).astype(F32)
            for f in range(frames):
                own = hint[f * toks : (f + 1) * toks]
                keys_out[at + f] = src[f]
                k_s[at + f] = (src[f].astype(F32) + own).astype(BF16)
                c_s[at + f] = (src[frames + f].astype(F32) + own).astype(BF16)
                if k < GROUP:
                    q_s[k * frames + f] = (qs[k][f].astype(F32) + own).astype(BF16)
        if lead:
            known.wait()
        for k in range(GROUP):
            s = mine ^ k
            at, jobs = [], []
            for r in range(frames):
                f = s * frames + r
                spots = [BAND + f + meta[s, r, j] for j in range(spans)]
                for cols in heads:
                    at.append((r, meta[s, r, spans].astype(F32), cols))
                    jobs.append((q_s[k * frames + r, :, cols], band(k_s, spots, cols), band(c_s, spots, cols)))
            for (r, flag, cols), out in zip(at, attend(jobs)):
                residual = (flag * g_ref[:, cols] * out.astype(F32)).astype(BF16)
                plain = kv[k][frames + r, :, cols].astype(F32)
                mixed[s * frames + r, :, cols] = (plain + residual.astype(F32)).astype(BF16)
        up[...] = mixed[total - BAND :]
        down[...] = mixed[:BAND]

    outs = [rows((total, toks, width)), rows((BAND, toks, width)), rows((BAND, toks, width)), rows((wide, toks, width))]
    scratch = [
        pltpu.VMEM((total, toks, width), BF16),
        pltpu.VMEM((wide, toks, width), BF16),
        pltpu.VMEM((wide, toks, width), BF16),
    ]
    ins = [*pairs_in, *queries, before, after, weight, gain]
    scalars = [me]
    if lead:
        outs += [rows((wide, toks, HEAD_DIM)), rows((GROUP, META, HEAD_DIM), I32)]
        scratch.append(pltpu.SMEM((GROUP, META, HEAD_DIM), I32))
    else:
        ins.append(setting[0])
        scalars.append(setting[1])
    return run(kernel, "hint_branch", ins, outs, scratch, 1, scalars, us=1.2 * len(heads))


def base_block(me, queries, keys, mixed, mixed_before, mixed_after, meta, spans):
    frames, toks, width = queries[0].shape
    total, wide = GROUP * frames, GROUP * frames + 2 * BAND
    heads = [slice(h * HEAD_DIM, (h + 1) * HEAD_DIM) for h in range(width // HEAD_DIM)]

    def kernel(scalars, ins, outs, scratch, sems):
        mine, meta = scalars[0][0], scalars[1]
        qs, k_ref, m_s = ins[:GROUP], ins[GROUP], scratch[0]
        m_s[BAND : BAND + total] = ins[GROUP + 1][...]
        m_s[:BAND] = ins[GROUP + 2][...]
        m_s[BAND + total :] = ins[GROUP + 3][...]
        for k in range(GROUP):
            s = mine ^ k
            at, jobs = [], []
            for r in range(frames):
                spots = [BAND + s * frames + r + meta[s, r, j] for j in range(spans)]
                for cols in heads:
                    at.append((r, cols))
                    jobs.append((qs[k][r, :, cols], band(k_ref, spots, cols), band(m_s, spots, cols)))
            for (r, cols), out in zip(at, attend(jobs)):
                outs[k][r, :, cols] = out

    ins = [*queries, keys, mixed, mixed_before, mixed_after]
    scratch = [pltpu.VMEM((wide, toks, width), BF16)]
    outs = [rows((frames, toks, width))] * GROUP
    return run(kernel, "base_block", ins, outs, scratch, 0, [me, meta], us=0.8 * len(heads))


def place(me, parts, into, model_width, quarter, first):
    frames, toks, width = parts[0].shape

    def kernel(scalars, ins, outs, scratch, sems):
        mine = scalars[0][0]
        move([(ins[k], outs[0].at[:, :, lanes(mine ^ k, quarter, first, width)]) for k in range(GROUP)], sems)

    held = [] if into is None else [into]
    return run(
        kernel,
        "place",
        [*parts, *held],
        [rows((frames, toks, model_width))],
        [],
        GROUP,
        [me],
        where=[VMEM] * GROUP + [HBM] * len(held),
        to=HBM,
        aliases={} if into is None else {1 + GROUP: 0},
        us=0.8,
    )[0]


def solution(mesh):
    count = mesh.shape["tm"]
    assert count % GROUP == 0
    across = [[(i, i ^ k) for i in range(count)] for k in range(GROUP)]
    upward = [(i, (i + GROUP) % count) for i in range(count)]
    downward = [(i, (i - GROUP) % count) for i in range(count)]

    def exchange(parts):
        return [parts[0]] + [lax.ppermute(parts[k], "tm", across[k]) for k in range(1, GROUP)]

    def body(queries, key_states, value_states, pose_depth, hint_weight, control_gain, band_offsets, control_flags):
        frames, _, model_width = queries.shape
        spans = band_offsets.shape[1]
        quarter = model_width // GROUP
        assert frames == BAND and sum(SLICES) * HEAD_DIM == quarter
        me = lax.rem(lax.axis_index("tm"), GROUP).astype(I32).reshape(1)
        gain = control_gain.reshape(1, -1)
        cuts = [(sum(SLICES[:c]) * HEAD_DIM, n * HEAD_DIM) for c, n in enumerate(SLICES)]
        wires = {"y": [], "z": []}

        def after(values, *deps):
            deps = [d for d in deps if d is not None]
            if not deps:
                return values
            return lax.optimization_barrier((values, deps))[0]

        def held(wire, depth):
            return wires[wire][-depth] if len(wires[wire]) >= depth else None

        def across_group(parts):
            sent = after(parts[1:], held("y", DEPTH_Y))
            got = [lax.ppermute(p, "tm", across[k + 1]) for k, p in enumerate(sent)]
            wires["y"].append(got[-1])
            return [parts[0], *got]

        def along(last, start):
            last, start = after([last, start], held("z", DEPTH_Z))
            got = (lax.ppermute(last, "tm", upward), lax.ppermute(start, "tm", downward))
            wires["z"].append(got[-1])
            return got

        n = len(cuts)
        pairs, asked, shares, sides, mixed, parts = {}, {}, {}, {}, {}, {}
        state = {"setting": None, "out": None}

        def step(name, c):
            first, width = cuts[c]
            if name == "KV":
                lead = [pose_depth, band_offsets, control_flags] if c == 0 else []
                pairs[c] = across_group(pack_pair(me, key_states, value_states, lead, quarter, first, width))
            elif name == "Q":
                *sent, weight, share = pack_one(me, queries, hint_weight, gain, quarter, first, width)
                asked[c] = across_group(sent)
                shares[c] = (weight, share)
            elif name == "Z":
                sides[c] = along(*edges(me, pairs[c]))
            elif name == "H":
                got = hint_branch(me, pairs[c], asked[c], *sides[c], *shares[c], state["setting"], spans)
                if state["setting"] is None:
                    state["setting"] = got[4:]
                mixed[c] = (got[3], got[0], *along(got[1], got[2]))
            elif name == "B":
                parts[c] = across_group(base_block(me, asked[c], *mixed[c], state["setting"][1], spans))
            else:
                state["out"] = place(me, parts[c], state["out"], model_width, quarter, first)

        for name, c in ORDER:
            step(name, c)
        return state["out"]

    return jax.shard_map(
        body,
        mesh=mesh,
        in_specs=(
            P(("grp", "tm"), None, None),
            P(("grp", "tm"), None, None),
            P(("grp", "tm"), None, None),
            P(("grp", "tm"), None, None),
            P(),
            P(),
            P(("grp", "tm"), None),
            P(("grp", "tm")),
        ),
        out_specs=P(("grp", "tm"), None, None),
        check_vma=False,
    )
```

time: 136 us -> 94.6 us (0.70)
  Pallas kernels: 49.7 us -> 19.4 us
  starting transfers between devices: 46.6 us -> 35.1 us
  local copies, waits for them, and re-layouts: 2.1 us -> 4.75 us
  waiting for transfers between devices: 36.7 us -> 34.5 us
    pallas_call x18 -> x12, Pallas kernels: 49.7 us -> 19.4 us  [run(): pl.pallas_call(body, out_shape=list(outs), in_specs=[SMEM] * a + (where i...]
    ppermute x39 -> x26, starting transfers between devices: 46.6 us -> 35.1 us  [the longest x18 19.4 us: across_group(): got = [lax.ppermute(p, 'tm', across[k + 1]) for k, p in enumerate(sent)]]
    unnamed x18 -> x20, local copies, waits for them, and re-layouts: 2.1 us -> 4.75 us
    ppermute x39 -> x26, waiting for transfers between devices: 36.7 us -> 34.5 us  [the longest x18 33.8 us: across_group(): got = [lax.ppermute(p, 'tm', across[k + 1]) for k, p in enumerate(sent)]]
  transfers between devices with their start and end apart: 39 -> 26, of which waited for: 10 -> 10; matrix products, arithmetic and copies ran while one was open for 0% -> 0% of each run, Pallas kernels for 36% -> 19%
where the time goes in v3:
time: 94.6 us; the launch traced here: 94 us
  starting transfers between devices  35.1 us (37%)
  waiting for transfers between devices  34.5 us (36%)
  Pallas kernels  19.4 us (21%)
  local copies, waits for them, and re-layouts  4.75 us (5%)
    ppermute x18, waiting for transfers between devices, across_group(): got = [lax.ppermute(p, 'tm', across[k + 1]) for k, p in enumerate(sent)]  33.8 us
    ppermute x18, starting transfers between devices, across_group(): got = [lax.ppermute(p, 'tm', across[k + 1]) for k, p in enumerate(sent)]  19.4 us
    pallas_call x12, Pallas kernels, run(): pl.pallas_call(body, out_shape=list(outs), in_specs=[SMEM] * a + (where i...  19.4 us
    ppermute x4, starting transfers between devices, along(): lax.ppermute(start, 'tm', downward)  8.92 us
    ppermute x4, starting transfers between devices, along(): lax.ppermute(last, 'tm', upward)  6.77 us
    unnamed x20, local copies, waits for them, and re-layouts  4.75 us
  transfers between devices with their start and end apart: 26, of which 10 were waited for; matrix products, arithmetic and copies ran while one was open for 0% of the time, Pallas kernels for 19%

profile of v3, /device:TPU:1, one launch (start us, length us, event | category | flops | bytes accessed | tf_op | source)
XLA Modules:
  0.0 94.0 jit_solution(17118254583529657454)
XLA Ops:
  5.7 2.7 %collective-permute-start.2 = (bf16[5,64,640]{2,1,0:T(8,128)(2,1)S(1)}, bf16[5,64,640]{2,1,0:T(8,128)(2,1)S(1)}, u32[]{:S(2)}, u32[]{:S(2)}) collective-permute-start(bf16[5,64,640]{2,1,0:T(8,128)(2,1)S(1)} %get-tuple-element.66), channel_id=1, source_target_pairs={{0,3},{1,2},{2,1},{3,0},{4,7},{5,6},{6,5},{7,4},{8,11},{9,10},{10,... | collective-permute-start | bytes 1228808 | tf_op jit(solution)/shard_map/ppermute | solution.py:300
  9.0 2.0 %collective-permute-start.8 = (bf16[4,64,640]{2,1,0:T(8,128)(2,1)S(1)}, bf16[4,64,640]{2,1,0:T(8,128)(2,1)S(1)}, u32[]{:S(2)}, u32[]{:S(2)}) collective-permute-start(bf16[4,64,640]{2,1,0:T(8,128)(2,1)S(1)} %get-tuple-element.83), channel_id=1, source_target_pairs={{0,3},{1,2},{2,1},{3,0},{4,7},{5,6},{6,5},{7,4},{8,11},{9,10},{10,... | collective-permute-start | bytes 983048 | tf_op jit(solution)/shard_map/ppermute | solution.py:300
  11.0 7.5 %collective-permute-done.2.refs_4_ = bf16[5,64,640]{2,1,0:T(8,128)(2,1)S(1)} collective-permute-done((bf16[5,64,640]{2,1,0:T(8,128)(2,1)S(1)}, bf16[5,64,640]{2,1,0:T(8,128)(2,1)S(1)}, u32[]{:S(2)}, u32[]{:S(2)}) %collective-permute-start.2) | collective-permute-done | bytes 409632 | tf_op jit(solution)/shard_map/ppermute | solution.py:300
  19.9 6.6 %collective-permute-done.1.refs_3_ = bf16[5,64,640]{2,1,0:T(8,128)(2,1)S(1)} collective-permute-done((bf16[5,64,640]{2,1,0:T(8,128)(2,1)S(1)}, bf16[5,64,640]{2,1,0:T(8,128)(2,1)S(1)}, u32[]{:S(2)}, u32[]{:S(2)}) %collective-permute-start.1) | collective-permute-done | bytes 409632 | tf_op jit(solution)/shard_map/ppermute | solution.py:300
  26.6 2.2 %collective-permute-start.6 = (bf16[5,64,640]{2,1,0:T(8,128)(2,1)S(1)}, bf16[5,64,640]{2,1,0:T(8,128)(2,1)S(1)}, u32[]{:S(2)}, u32[]{:S(2)}) collective-permute-start(bf16[5,64,640]{2,1,0:T(8,128)(2,1)S(1)} %get-tuple-element.74), channel_id=1, source_target_pairs={{0,4},{1,5},{2,6},{3,7},{4,8},{5,9},{6,10},{7,11},{8,12},{9,13},{1... | collective-permute-start | bytes 1228808 | tf_op jit(solution)/shard_map/ppermute | solution.py:306
  28.8 2.1 %collective-permute-start.7 = (bf16[5,64,640]{2,1,0:T(8,128)(2,1)S(1)}, bf16[5,64,640]{2,1,0:T(8,128)(2,1)S(1)}, u32[]{:S(2)}, u32[]{:S(2)}) collective-permute-start(bf16[5,64,640]{2,1,0:T(8,128)(2,1)S(1)} %get-tuple-element.75), channel_id=1, source_target_pairs={{0,12},{1,13},{2,14},{3,15},{4,0},{5,1},{6,2},{7,3},{8,4},{9,5},{1... | collective-permute-start | bytes 1228808 | tf_op jit(solution)/shard_map/ppermute | solution.py:306
  31.1 3.4 %collective-permute-done.8.refs_4_.refs_5_ = bf16[4,64,640]{2,1,0:T(8,128)(2,1)S(1)} collective-permute-done((bf16[4,64,640]{2,1,0:T(8,128)(2,1)S(1)}, bf16[4,64,640]{2,1,0:T(8,128)(2,1)S(1)}, u32[]{:S(2)}, u32[]{:S(2)}) %collective-permute-start.8) | collective-permute-done | bytes 327712 | tf_op jit(solution)/shard_map/ppermute | solution.py:300
  36.1 4.4 %collective-permute-done.13.refs_3_.refs_4_ = bf16[4,64,640]{2,1,0:T(8,128)(2,1)S(1)} collective-permute-done((bf16[4,64,640]{2,1,0:T(8,128)(2,1)S(1)}, bf16[4,64,640]{2,1,0:T(8,128)(2,1)S(1)}, u32[]{:S(2)}, u32[]{:S(2)}) %collective-permute-start.13) | collective-permute-done | bytes 327712 | tf_op jit(solution)/shard_map/ppermute | solution.py:300
  40.5 2.2 %collective-permute-start.4 = (bf16[2,64,640]{2,1,0:T(8,128)(2,1)S(1)}, bf16[2,64,640]{2,1,0:T(8,128)(2,1)S(1)}, u32[]{:S(2)}, u32[]{:S(2)}) collective-permute-start(bf16[2,64,640]{2,1,0:T(8,128)(2,1)S(1)} %get-tuple-element.72), channel_id=1, source_target_pairs={{0,2},{1,3},{2,0},{3,1},{4,6},{5,7},{6,4},{7,5},{8,10},{9,11},{10,... | collective-permute-start | bytes 491528 | tf_op jit(solution)/shard_map/ppermute | solution.py:300
  42.8 1.6 %collective-permute-done.5.refs_8_.refs_5_ = bf16[2,64,640]{2,1,0:T(8,128)(2,1)S(1)} collective-permute-done((bf16[2,64,640]{2,1,0:T(8,128)(2,1)S(1)}, bf16[2,64,640]{2,1,0:T(8,128)(2,1)S(1)}, u32[]{:S(2)}, u32[]{:S(2)}) %collective-permute-start.5) | collective-permute-done | bytes 163872 | tf_op jit(solution)/shard_map/ppermute | solution.py:300
  44.4 2.0 %collective-permute-start.14 = (bf16[4,64,640]{2,1,0:T(8,128)(2,1)S(1)}, bf16[4,64,640]{2,1,0:T(8,128)(2,1)S(1)}, u32[]{:S(2)}, u32[]{:S(2)}) collective-permute-start(bf16[4,64,640]{2,1,0:T(8,128)(2,1)S(1)} %get-tuple-element.90), channel_id=1, source_target_pairs={{0,4},{1,5},{2,6},{3,7},{4,8},{5,9},{6,10},{7,11},{8,12},{9,13},{1... | collective-permute-start | bytes 983048 | tf_op jit(solution)/shard_map/ppermute | solution.py:306
  46.4 2.0 %collective-permute-start.15 = (bf16[4,64,640]{2,1,0:T(8,128)(2,1)S(1)}, bf16[4,64,640]{2,1,0:T(8,128)(2,1)S(1)}, u32[]{:S(2)}, u32[]{:S(2)}) collective-permute-start(bf16[4,64,640]{2,1,0:T(8,128)(2,1)S(1)} %get-tuple-element.91), channel_id=1, source_target_pairs={{0,12},{1,13},{2,14},{3,15},{4,0},{5,1},{6,2},{7,3},{8,4},{9,5},{1... | collective-permute-start | bytes 983048 | tf_op jit(solution)/shard_map/ppermute | solution.py:306
  48.6 2.0 %collective-permute-start.11 = (bf16[2,64,640]{2,1,0:T(8,128)(2,1)S(1)}, bf16[2,64,640]{2,1,0:T(8,128)(2,1)S(1)}, u32[]{:S(2)}, u32[]{:S(2)}) collective-permute-start(bf16[2,64,640]{2,1,0:T(8,128)(2,1)S(1)} %get-tuple-element.86), channel_id=1, source_target_pairs={{0,3},{1,2},{2,1},{3,0},{4,7},{5,6},{6,5},{7,4},{8,11},{9,10},{10,... | collective-permute-start | bytes 491528 | tf_op jit(solution)/shard_map/ppermute | solution.py:300
  51.1 4.4 %hint_branch.2 = (bf16[8,64,640]{2,1,0:T(8,128)(2,1)S(1)}, bf16[2,64,640]{2,1,0:T(8,128)(2,1)S(1)}, bf16[2,64,640]{2,1,0:T(8,128)(2,1)S(1)}, bf16[12,64,640]{2,1...) custom-call(s32[1]{0:T(128)} %bitcast.refs_0_, ...), custom_call_target="tpu_custom_call" | custom-call | flops 1 | bytes 20400000 | tf_op jit(solution)/shard_map/hint_branch/pallas_call | solution.py:29
  56.4 2.1 %collective-permute-done.10.refs_8_.refs_4_ = bf16[2,64,640]{2,1,0:T(8,128)(2,1)S(1)} collective-permute-done((bf16[2,64,640]{2,1,0:T(8,128)(2,1)S(1)}, bf16[2,64,640]{2,1,0:T(8,128)(2,1)S(1)}, u32[]{:S(2)}, u32[]{:S(2)}) %collective-permute-start.10) | collective-permute-done | bytes 163872 | tf_op jit(solution)/shard_map/ppermute | solution.py:300
  58.6 3.2 %collective-permute-start.22 = (bf16[2,64,640]{2,1,0:T(8,128)(2,1)S(1)}, bf16[2,64,640]{2,1,0:T(8,128)(2,1)S(1)}, u32[]{:S(2)}, u32[]{:S(2)}) collective-permute-start(bf16[2,64,640]{2,1,0:T(8,128)(2,1)S(1)} %get-tuple-element.113), channel_id=1, source_target_pairs={{0,12},{1,13},{2,14},{3,15},{4,0},{5,1},{6,2},{7,3},{8,4},{9,5},{1... | collective-permute-start | bytes 491528 | tf_op jit(solution)/shard_map/ppermute | solution.py:306
  62.4 4.4 %hint_branch.3 = (bf16[8,64,640]{2,1,0:T(8,128)(2,1)S(1)}, bf16[2,64,640]{2,1,0:T(8,128)(2,1)S(1)}, bf16[2,64,640]{2,1,0:T(8,128)(2,1)S(1)}, bf16[12,64,640]{2,1,0:T(8,128)(2,1)S(1)}) custom-call(s32[1]{0:T(128)} %bitcast.refs_0_, s32[4,8,128]{2,1,0:T(8,128)S(1)} %get-tuple-element.78.refs_1_, bf16[4,64,640]{2,1,0:T(8,128)(2,1)S(1)} %get-tuple-element.87.refs_1_.refs_2_, ...), custom_call_target="tpu_custom_call" | custom-call | flops 1 | bytes 20400000 | tf_op jit(solution)/shard_map/hint_branch/pallas_call | solution.py:29
  66.8 1.7 %collective-permute-start.16 = (bf16[2,64,640]{2,1,0:T(8,128)(2,1)S(1)}, bf16[2,64,640]{2,1,0:T(8,128)(2,1)S(1)}, u32[]{:S(2)}, u32[]{:S(2)}) collective-permute-start(bf16[2,64,640]{2,1,0:T(8,128)(2,1)S(1)} %get-tuple-element.99), channel_id=1, source_target_pairs={{0,4},{1,5},{2,6},{3,7},{4,8},{5,9},{6,10},{7,11},{8,12},{9,13},{1... | collective-permute-start | bytes 491528 | tf_op jit(solution)/shard_map/ppermute | solution.py:306
  70.2 3.5 %base_block.3 = (bf16[2,64,640]{2,1,0:T(8,128)(2,1)S(1)}, bf16[2,64,640]{2,1,0:T(8,128)(2,1)S(1)}, bf16[2,64,640]{2,1,0:T(8,128)(2,1)S(1)}, bf16[2,64,640]{2,1,0:T(8,128)(2,1)S(1)}) custom-call(s32[1]{0:T(128)} %bitcast.refs_0_, s32[4,8,128]{2,1,0:T(8,128)S(1)} %get-tuple-element.78.refs_1_, bf16[2,64,640]{2,1,0:T(8,128)(2,1)S(1)} %get-tuple-element.67.refs_5_.refs_2_, ...), custom_call_target="tpu_custom_call" | custom-call | flops 1 | bytes 13600000 | tf_op jit(solution)/shard_map/base_block/pallas_call | solution.py:29
  73.7 2.7 %collective-permute-start.23 = (bf16[2,64,640]{2,1,0:T(8,128)(2,1)S(1)}, bf16[2,64,640]{2,1,0:T(8,128)(2,1)S(1)}, u32[]{:S(2)}, u32[]{:S(2)}) collective-permute-start(bf16[2,64,640]{2,1,0:T(8,128)(2,1)S(1)} %get-tuple-element.118), channel_id=1, source_target_pairs={{0,1},{1,0},{2,3},{3,2},{4,5},{5,4},{6,7},{7,6},{8,9},{9,8},{10,11... | collective-permute-start | bytes 491528 | tf_op jit(solution)/shard_map/ppermute | solution.py:300
  78.1 3.5 %base_block.2 = (bf16[2,64,640]{2,1,0:T(8,128)(2,1)S(1)}, bf16[2,64,640]{2,1,0:T(8,128)(2,1)S(1)}, bf16[2,64,640]{2,1,0:T(8,128)(2,1)S(1)}, bf16[2,64,640]{2,1,0:T(8,128)(2,1)S(1)}) custom-call(s32[1]{0:T(128)} %bitcast.refs_0_, s32[4,8,128]{2,1,0:T(8,128)S(1)} %get-tuple-element.78.refs_1_, bf16[2,64,640]{2,1,0:T(8,128)(2,1)S(1)} %get-tuple-element.79.refs_6_.refs_2_, ...), custom_call_target="tpu_custom_call" | custom-call | flops 1 | bytes 13600000 | tf_op jit(solution)/shard_map/base_block/pallas_call | solution.py:29
  84.0 2.3 %collective-permute-done.25.refs_4_ = bf16[2,64,640]{2,1,0:T(8,128)(2,1)S(1)} collective-permute-done((bf16[2,64,640]{2,1,0:T(8,128)(2,1)S(1)}, bf16[2,64,640]{2,1,0:T(8,128)(2,1)S(1)}, u32[]{:S(2)}, u32[]{:S(2)}) %collective-permute-start.25) | collective-permute-done | bytes 163872 | tf_op jit(solution)/shard_map/ppermute | solution.py:300
  87.2 2.3 %collective-permute-done.19.refs_3_ = bf16[2,64,640]{2,1,0:T(8,128)(2,1)S(1)} collective-permute-done((bf16[2,64,640]{2,1,0:T(8,128)(2,1)S(1)}, bf16[2,64,640]{2,1,0:T(8,128)(2,1)S(1)}, u32[]{:S(2)}, u32[]{:S(2)}) %collective-permute-start.19) | collective-permute-done | bytes 163872 | tf_op jit(solution)/shard_map/ppermute | solution.py:300
  89.4 3.6 %collective-permute-done.20.refs_4_ = bf16[2,64,640]{2,1,0:T(8,128)(2,1)S(1)} collective-permute-done((bf16[2,64,640]{2,1,0:T(8,128)(2,1)S(1)}, bf16[2,64,640]{2,1,0:T(8,128)(2,1)S(1)}, u32[]{:S(2)}, u32[]{:S(2)}) %collective-permute-start.20) | collective-permute-done | bytes 163872 | tf_op jit(solution)/shard_map/ppermute | solution.py:300
  (60 shorter events, 19.3 us)
Async XLA Ops:
  5.7 12.7 %collective-permute-start.2 = (bf16[5,64,640]{2,1,0:T(8,128)(2,1)S(1)}, bf16[5,64,640]{2,1,0:T(8,128)(2,1)S(1)}, u32[]{:S(2)}, u32[]{:S(2)}) collective-permute-start(bf16[5,64,640]{2,1,0:T(8,128)(2,1)S(1)} %get-tuple-element.66), channel_id=1, source_target_pairs={{0,3},{1,2},{2,1},{3,0},{4,7},{5,6},{6,5},{7,4},{8,11},{9,10},{10,... | collective-permute-start | bytes 1228808 | tf_op jit(solution)/shard_map/ppermute | solution.py:300
  8.4 11.5 %collective-permute-start = (bf16[5,64,640]{2,1,0:T(8,128)(2,1)S(1)}, bf16[5,64,640]{2,1,0:T(8,128)(2,1)S(1)}, u32[]{:S(2)}, u32[]{:S(2)}) collective-permute-start(bf16[5,64,640]{2,1,0:T(8,128)(2,1)S(1)} %get-tuple-element.64), channel_id=1, source_target_pairs={{0,1},{1,0},{2,3},{3,2},{4,5},{5,4},{6,7},{7,6},{8,9},{9,8},{10,11... | collective-permute-start | bytes 1228808 | tf_op jit(solution)/shard_map/ppermute | solution.py:300
  8.4 18.0 %collective-permute-start.1 = (bf16[5,64,640]{2,1,0:T(8,128)(2,1)S(1)}, bf16[5,64,640]{2,1,0:T(8,128)(2,1)S(1)}, u32[]{:S(2)}, u32[]{:S(2)}) collective-permute-start(bf16[5,64,640]{2,1,0:T(8,128)(2,1)S(1)} %get-tuple-element.65), channel_id=1, source_target_pairs={{0,2},{1,3},{2,0},{3,1},{4,6},{5,7},{6,4},{7,5},{8,10},{9,11},{10,... | collective-permute-start | bytes 1228808 | tf_op jit(solution)/shard_map/ppermute | solution.py:300
  9.0 25.6 %collective-permute-start.8 = (bf16[4,64,640]{2,1,0:T(8,128)(2,1)S(1)}, bf16[4,64,640]{2,1,0:T(8,128)(2,1)S(1)}, u32[]{:S(2)}, u32[]{:S(2)}) collective-permute-start(bf16[4,64,640]{2,1,0:T(8,128)(2,1)S(1)} %get-tuple-element.83), channel_id=1, source_target_pairs={{0,3},{1,2},{2,1},{3,0},{4,7},{5,6},{6,5},{7,4},{8,11},{9,10},{10,... | collective-permute-start | bytes 983048 | tf_op jit(solution)/shard_map/ppermute | solution.py:300
  11.0 25.0 %collective-permute-start.12 = (bf16[4,64,640]{2,1,0:T(8,128)(2,1)S(1)}, bf16[4,64,640]{2,1,0:T(8,128)(2,1)S(1)}, u32[]{:S(2)}, u32[]{:S(2)}) collective-permute-start(bf16[4,64,640]{2,1,0:T(8,128)(2,1)S(1)} %get-tuple-element.88), channel_id=1, source_target_pairs={{0,1},{1,0},{2,3},{3,2},{4,5},{5,4},{6,7},{7,6},{8,9},{9,8},{10,11... | collective-permute-start | bytes 983048 | tf_op jit(solution)/shard_map/ppermute | solution.py:300
  18.4 22.1 %collective-permute-start.13 = (bf16[4,64,640]{2,1,0:T(8,128)(2,1)S(1)}, bf16[4,64,640]{2,1,0:T(8,128)(2,1)S(1)}, u32[]{:S(2)}, u32[]{:S(2)}) collective-permute-start(bf16[4,64,640]{2,1,0:T(8,128)(2,1)S(1)} %get-tuple-element.89), channel_id=1, source_target_pairs={{0,2},{1,3},{2,0},{3,1},{4,6},{5,7},{6,4},{7,5},{8,10},{9,11},{10,... | collective-permute-start | bytes 983048 | tf_op jit(solution)/shard_map/ppermute | solution.py:300
  26.6 24.0 %collective-permute-start.6 = (bf16[5,64,640]{2,1,0:T(8,128)(2,1)S(1)}, bf16[5,64,640]{2,1,0:T(8,128)(2,1)S(1)}, u32[]{:S(2)}, u32[]{:S(2)}) collective-permute-start(bf16[5,64,640]{2,1,0:T(8,128)(2,1)S(1)} %get-tuple-element.74), channel_id=1, source_target_pairs={{0,4},{1,5},{2,6},{3,7},{4,8},{5,9},{6,10},{7,11},{8,12},{9,13},{1... | collective-permute-start | bytes 1228808 | tf_op jit(solution)/shard_map/ppermute | solution.py:306
  28.8 21.8 %collective-permute-start.7 = (bf16[5,64,640]{2,1,0:T(8,128)(2,1)S(1)}, bf16[5,64,640]{2,1,0:T(8,128)(2,1)S(1)}, u32[]{:S(2)}, u32[]{:S(2)}) collective-permute-start(bf16[5,64,640]{2,1,0:T(8,128)(2,1)S(1)} %get-tuple-element.75), channel_id=1, source_target_pairs={{0,12},{1,13},{2,14},{3,15},{4,0},{5,1},{6,2},{7,3},{8,4},{9,5},{1... | collective-permute-start | bytes 1228808 | tf_op jit(solution)/shard_map/ppermute | solution.py:306
  34.5 9.9 %collective-permute-start.5 = (bf16[2,64,640]{2,1,0:T(8,128)(2,1)S(1)}, bf16[2,64,640]{2,1,0:T(8,128)(2,1)S(1)}, u32[]{:S(2)}, u32[]{:S(2)}) collective-permute-start(bf16[2,64,640]{2,1,0:T(8,128)(2,1)S(1)} %get-tuple-element.73), channel_id=1, source_target_pairs={{0,3},{1,2},{2,1},{3,0},{4,7},{5,6},{6,5},{7,4},{8,11},{9,10},{10,... | collective-permute-start | bytes 491528 | tf_op jit(solution)/shard_map/ppermute | solution.py:300
  36.0 10.4 %collective-permute-start.3 = (bf16[2,64,640]{2,1,0:T(8,128)(2,1)S(1)}, bf16[2,64,640]{2,1,0:T(8,128)(2,1)S(1)}, u32[]{:S(2)}, u32[]{:S(2)}) collective-permute-start(bf16[2,64,640]{2,1,0:T(8,128)(2,1)S(1)} %get-tuple-element.71), channel_id=1, source_target_pairs={{0,1},{1,0},{2,3},{3,2},{4,5},{5,4},{6,7},{7,6},{8,9},{9,8},{10,11... | collective-permute-start | bytes 491528 | tf_op jit(solution)/shard_map/ppermute | solution.py:300
  40.5 8.1 %collective-permute-start.4 = (bf16[2,64,640]{2,1,0:T(8,128)(2,1)S(1)}, bf16[2,64,640]{2,1,0:T(8,128)(2,1)S(1)}, u32[]{:S(2)}, u32[]{:S(2)}) collective-permute-start(bf16[2,64,640]{2,1,0:T(8,128)(2,1)S(1)} %get-tuple-element.72), channel_id=1, source_target_pairs={{0,2},{1,3},{2,0},{3,1},{4,6},{5,7},{6,4},{7,5},{8,10},{9,11},{10,... | collective-permute-start | bytes 491528 | tf_op jit(solution)/shard_map/ppermute | solution.py:300
  44.4 17.3 %collective-permute-start.14 = (bf16[4,64,640]{2,1,0:T(8,128)(2,1)S(1)}, bf16[4,64,640]{2,1,0:T(8,128)(2,1)S(1)}, u32[]{:S(2)}, u32[]{:S(2)}) collective-permute-start(bf16[4,64,640]{2,1,0:T(8,128)(2,1)S(1)} %get-tuple-element.90), channel_id=1, source_target_pairs={{0,4},{1,5},{2,6},{3,7},{4,8},{5,9},{6,10},{7,11},{8,12},{9,13},{1... | collective-permute-start | bytes 983048 | tf_op jit(solution)/shard_map/ppermute | solution.py:306
  46.4 16.1 %collective-permute-start.15 = (bf16[4,64,640]{2,1,0:T(8,128)(2,1)S(1)}, bf16[4,64,640]{2,1,0:T(8,128)(2,1)S(1)}, u32[]{:S(2)}, u32[]{:S(2)}) collective-permute-start(bf16[4,64,640]{2,1,0:T(8,128)(2,1)S(1)} %get-tuple-element.91), channel_id=1, source_target_pairs={{0,12},{1,13},{2,14},{3,15},{4,0},{5,1},{6,2},{7,3},{8,4},{9,5},{1... | collective-permute-start | bytes 983048 | tf_op jit(solution)/shard_map/ppermute | solution.py:306
  50.6 7.9 %collective-permute-start.10 = (bf16[2,64,640]{2,1,0:T(8,128)(2,1)S(1)}, bf16[2,64,640]{2,1,0:T(8,128)(2,1)S(1)}, u32[]{:S(2)}, u32[]{:S(2)}) collective-permute-start(bf16[2,64,640]{2,1,0:T(8,128)(2,1)S(1)} %get-tuple-element.85), channel_id=1, source_target_pairs={{0,2},{1,3},{2,0},{3,1},{4,6},{5,7},{6,4},{7,5},{8,10},{9,11},{10,... | collective-permute-start | bytes 491528 | tf_op jit(solution)/shard_map/ppermute | solution.py:300
  50.6 11.1 %collective-permute-start.9 = (bf16[2,64,640]{2,1,0:T(8,128)(2,1)S(1)}, bf16[2,64,640]{2,1,0:T(8,128)(2,1)S(1)}, u32[]{:S(2)}, u32[]{:S(2)}) collective-permute-start(bf16[2,64,640]{2,1,0:T(8,128)(2,1)S(1)} %get-tuple-element.84), channel_id=1, source_target_pairs={{0,1},{1,0},{2,3},{3,2},{4,5},{5,4},{6,7},{7,6},{8,9},{9,8},{10,11... | collective-permute-start | bytes 491528 | tf_op jit(solution)/shard_map/ppermute | solution.py:300
  55.6 14.6 %collective-permute-start.21 = (bf16[2,64,640]{2,1,0:T(8,128)(2,1)S(1)}, bf16[2,64,640]{2,1,0:T(8,128)(2,1)S(1)}, u32[]{:S(2)}, u32[]{:S(2)}) collective-permute-start(bf16[2,64,640]{2,1,0:T(8,128)(2,1)S(1)} %get-tuple-element.112), channel_id=1, source_target_pairs={{0,4},{1,5},{2,6},{3,7},{4,8},{5,9},{6,10},{7,11},{8,12},{9,13},{1... | collective-permute-start | bytes 491528 | tf_op jit(solution)/shard_map/ppermute | solution.py:306
  58.6 11.6 %collective-permute-start.22 = (bf16[2,64,640]{2,1,0:T(8,128)(2,1)S(1)}, bf16[2,64,640]{2,1,0:T(8,128)(2,1)S(1)}, u32[]{:S(2)}, u32[]{:S(2)}) collective-permute-start(bf16[2,64,640]{2,1,0:T(8,128)(2,1)S(1)} %get-tuple-element.113), channel_id=1, source_target_pairs={{0,12},{1,13},{2,14},{3,15},{4,0},{5,1},{6,2},{7,3},{8,4},{9,5},{1... | collective-permute-start | bytes 491528 | tf_op jit(solution)/shard_map/ppermute | solution.py:306
  66.8 11.3 %collective-permute-start.16 = (bf16[2,64,640]{2,1,0:T(8,128)(2,1)S(1)}, bf16[2,64,640]{2,1,0:T(8,128)(2,1)S(1)}, u32[]{:S(2)}, u32[]{:S(2)}) collective-permute-start(bf16[2,64,640]{2,1,0:T(8,128)(2,1)S(1)} %get-tuple-element.99), channel_id=1, source_target_pairs={{0,4},{1,5},{2,6},{3,7},{4,8},{5,9},{6,10},{7,11},{8,12},{9,13},{1... | collective-permute-start | bytes 491528 | tf_op jit(solution)/shard_map/ppermute | solution.py:306
  68.6 9.6 %collective-permute-start.17 = (bf16[2,64,640]{2,1,0:T(8,128)(2,1)S(1)}, bf16[2,64,640]{2,1,0:T(8,128)(2,1)S(1)}, u32[]{:S(2)}, u32[]{:S(2)}) collective-permute-start(bf16[2,64,640]{2,1,0:T(8,128)(2,1)S(1)} %get-tuple-element.100), channel_id=1, source_target_pairs={{0,12},{1,13},{2,14},{3,15},{4,0},{5,1},{6,2},{7,3},{8,4},{9,5},{1... | collective-permute-start | bytes 491528 | tf_op jit(solution)/shard_map/ppermute | solution.py:306
  73.7 10.0 %collective-permute-start.23 = (bf16[2,64,640]{2,1,0:T(8,128)(2,1)S(1)}, bf16[2,64,640]{2,1,0:T(8,128)(2,1)S(1)}, u32[]{:S(2)}, u32[]{:S(2)}) collective-permute-start(bf16[2,64,640]{2,1,0:T(8,128)(2,1)S(1)} %get-tuple-element.118), channel_id=1, source_target_pairs={{0,1},{1,0},{2,3},{3,2},{4,5},{5,4},{6,7},{7,6},{8,9},{9,8},{10,11... | collective-permute-start | bytes 491528 | tf_op jit(solution)/shard_map/ppermute | solution.py:300
  76.4 7.6 %collective-permute-start.24 = (bf16[2,64,640]{2,1,0:T(8,128)(2,1)S(1)}, bf16[2,64,640]{2,1,0:T(8,128)(2,1)S(1)}, u32[]{:S(2)}, u32[]{:S(2)}) collective-permute-start(bf16[2,64,640]{2,1,0:T(8,128)(2,1)S(1)} %get-tuple-element.119), channel_id=1, source_target_pairs={{0,2},{1,3},{2,0},{3,1},{4,6},{5,7},{6,4},{7,5},{8,10},{9,11},{10,... | collective-permute-start | bytes 491528 | tf_op jit(solution)/shard_map/ppermute | solution.py:300
  78.0 8.3 %collective-permute-start.25 = (bf16[2,64,640]{2,1,0:T(8,128)(2,1)S(1)}, bf16[2,64,640]{2,1,0:T(8,128)(2,1)S(1)}, u32[]{:S(2)}, u32[]{:S(2)}) collective-permute-start(bf16[2,64,640]{2,1,0:T(8,128)(2,1)S(1)} %get-tuple-element.120), channel_id=1, source_target_pairs={{0,3},{1,2},{2,1},{3,0},{4,7},{5,6},{6,5},{7,4},{8,11},{9,10},{10,... | collective-permute-start | bytes 491528 | tf_op jit(solution)/shard_map/ppermute | solution.py:300
  82.3 7.2 %collective-permute-start.19 = (bf16[2,64,640]{2,1,0:T(8,128)(2,1)S(1)}, bf16[2,64,640]{2,1,0:T(8,128)(2,1)S(1)}, u32[]{:S(2)}, u32[]{:S(2)}) collective-permute-start(bf16[2,64,640]{2,1,0:T(8,128)(2,1)S(1)} %get-tuple-element.106), channel_id=1, source_target_pairs={{0,2},{1,3},{2,0},{3,1},{4,6},{5,7},{6,4},{7,5},{8,10},{9,11},{10,... | collective-permute-start | bytes 491528 | tf_op jit(solution)/shard_map/ppermute | solution.py:300
  83.7 9.3 %collective-permute-start.20 = (bf16[2,64,640]{2,1,0:T(8,128)(2,1)S(1)}, bf16[2,64,640]{2,1,0:T(8,128)(2,1)S(1)}, u32[]{:S(2)}, u32[]{:S(2)}) collective-permute-start(bf16[2,64,640]{2,1,0:T(8,128)(2,1)S(1)} %get-tuple-element.107), channel_id=1, source_target_pairs={{0,3},{1,2},{2,1},{3,0},{4,7},{5,6},{6,5},{7,4},{8,11},{9,10},{10,... | collective-permute-start | bytes 491528 | tf_op jit(solution)/shard_map/ppermute | solution.py:300
  (12 other events, 91.3 us)

commit v4 on v3

v4 whole, which is shorter than its diff:
```python
import jax
import jax.numpy as jnp
from jax import lax
from jax.experimental import pallas as pl
from jax.experimental.pallas import tpu as pltpu
from jax.sharding import PartitionSpec as P

HEAD_DIM = 128
BAND = 2
GROUP = 4
SLICES = (5, 5)
META = 8
PIECE = 16
ORDER = [("KV", 0), ("C", 0), ("KV", 1), ("Z", 0), ("Q", 0), ("Z", 1), ("Q", 1), ("H", 0), ("H", 1), ("B", 0), ("B", 1), ("P", 0), ("P", 1)]
DEPTH_Y, DEPTH_Z = 3, 2
F32 = jnp.float32
BF16 = jnp.bfloat16
I32 = jnp.int32
VMEM = pl.BlockSpec(memory_space=pltpu.VMEM)
SMEM = pl.BlockSpec(memory_space=pltpu.SMEM)
HBM = pl.BlockSpec(memory_space=pltpu.HBM)


def run(kernel, name, ins, outs, scratch, copies, scalars=(), where=VMEM, to=VMEM, aliases=None, us=1.0):
    a, b, c, d = len(scalars), len(ins), len(outs), len(scratch)

    def body(*refs):
        kernel(refs[:a], refs[a : a + b], refs[a + b : a + b + c], refs[a + b + c : a + b + c + d], refs[-1])

    return pl.pallas_call(
        body,
        out_shape=list(outs),
        in_specs=[SMEM] * a + (where if isinstance(where, list) else [where] * b),
        out_specs=[to] * c,
        scratch_shapes=[*scratch, pltpu.SemaphoreType.DMA((max(copies, 1),))],
        input_output_aliases=aliases or {},
        compiler_params=pltpu.CompilerParams(vmem_limit_bytes=16 * 1024 * 1024),
        cost_estimate=pl.CostEstimate(flops=1, bytes_accessed=int(us * 3.4e6), transcendentals=0),
        name=name,
    )(*scalars, *ins)


def move(pairs, sems):
    copies = [pltpu.make_async_copy(s, d, sems.at[i]) for i, (s, d) in enumerate(pairs)]
    for copy in copies:
        copy.start()
    for copy in copies:
        copy.wait()


def lanes(me, quarter, first, width):
    return pl.ds(pl.multiple_of(me * quarter + first, HEAD_DIM), width)


def rows(shape, dtype=BF16):
    return jax.ShapeDtypeStruct(shape, dtype)


def notes_at(i, width):
    blocks = width // HEAD_DIM
    return PIECE * (i // blocks), HEAD_DIM * (i % blocks)


def note_rows(pieces, width):
    return PIECE * -(-pieces * HEAD_DIM // width)


def read_note(ref, top, left, width, i):
    down, right = notes_at(i, width)
    return ref[top + down : top + down + PIECE, left + right : left + right + HEAD_DIM]


def pack(me, ks, arrays, notes, quarter, first, width):
    frames, toks, _ = arrays[0].shape
    size = frames * toks
    pieces = size // PIECE + 1 if notes else 0
    base = len(arrays) * size

    def kernel(scalars, ins, outs, scratch, sems):
        mine = scalars[0][0]
        pairs = list(zip(ins[len(arrays) :], scratch))
        for i, k in enumerate(ks):
            where = lanes(mine ^ k, quarter, first, width)
            for j in range(len(arrays)):
                for f in range(frames):
                    pairs.append((ins[j].at[f, :, where], outs[i].at[pl.ds(j * size + f * toks, toks)]))
        copies = [pltpu.make_async_copy(s, d, sems.at[i]) for i, (s, d) in enumerate(pairs)]
        for copy in copies:
            copy.start()
        if notes:
            for copy in copies[: len(notes)]:
                copy.wait()
            patches, offsets, flags = scratch
            spans = offsets.shape[1]
            row = lax.broadcasted_iota(I32, (PIECE, HEAD_DIM), 0)
            col = lax.broadcasted_iota(I32, (PIECE, HEAD_DIM), 1)
            block = jnp.zeros((PIECE, HEAD_DIM), F32)
            for f in range(frames):
                for j in range(spans):
                    block = jnp.where((row == f) & (col == j), offsets[f, j].astype(F32), block)
                block = jnp.where((row == f) & (col == spans), flags[f].astype(F32), block)
            per = toks // PIECE
            for i in range(pieces):
                top, left = notes_at(i, width)
                if i == pieces - 1:
                    piece = block.astype(BF16)
                else:
                    piece = patches[i // per, PIECE * (i % per) : PIECE * (i % per + 1)]
                for out in outs:
                    out[base + top : base + top + PIECE, left : left + HEAD_DIM] = piece
        for copy in copies[len(notes) :]:
            copy.wait()

    scratch = []
    if notes:
        pose, offsets, flags = notes
        scratch = [pltpu.VMEM(pose.shape, BF16), pltpu.SMEM(offsets.shape, I32), pltpu.SMEM(flags.shape, I32)]
    outs = [rows((base + note_rows(pieces, width), width))] * len(ks)
    copies = frames * len(arrays) * len(ks) + len(notes)
    return run(kernel, "pack", [*arrays, *notes], outs, scratch, copies, [me], where=HBM)


def share_of(me, weight, gain, quarter):
    def kernel(scalars, ins, outs, scratch, sems):
        mine = scalars[0][0]
        move([(i.at[:, lanes(mine, quarter, 0, quarter)], o) for i, o in zip(ins, outs)], sems)

    outs = [rows((weight.shape[0], quarter)), rows((1, quarter), F32)]
    return run(kernel, "share", [weight, gain], outs, [], 2, [me], where=HBM)


def edges(me, near, far, size, first, width, lead):
    pieces = size // PIECE + 1 if lead else 0

    def kernel(scalars, ins, outs, scratch, sems):
        mine = scalars[0][0]
        for out, owner in zip(outs, (GROUP - 1, 0)):
            for k in range(GROUP):

                @pl.when((mine ^ k) == owner)
                def _(out=out, k=k):
                    if k >= 2:
                        out[...] = ins[k][...]
                    else:
                        out[: 2 * size] = ins[k][: 2 * size, first : first + width]
                        for i in range(pieces - 1):
                            top, left = notes_at(i, width)
                            top += 2 * size
                            piece = read_note(ins[k], 3 * size, 0, ins[k].shape[1], i)
                            out[top : top + PIECE, left : left + HEAD_DIM] = piece

    shape = rows(far[0].shape)
    return run(kernel, "edges", [*near, *far], [shape, shape], [], 0, [me], us=0.2)


def attend(jobs):
    scores = [
        lax.dot_general(query, keys, (((1,), (1,)), ((), ())), preferred_element_type=F32) * HEAD_DIM ** (-0.5)
        for query, keys, _ in jobs
    ]
    tops = [jnp.max(x, axis=1, keepdims=True) for x in scores]
    scores = [jnp.exp(x - top) for x, top in zip(scores, tops)]
    scales = [1.0 / jnp.sum(x, axis=1, keepdims=True) for x in scores]
    weights = [(x * scale).astype(BF16) for x, scale in zip(scores, scales)]
    return [
        jnp.dot(w, values, preferred_element_type=F32).astype(BF16) for w, (_, _, values) in zip(weights, jobs)
    ]


def band(ref, spots, cols):
    return jnp.concatenate([ref[s, :, cols] for s in spots], axis=0)


def hint_branch(me, near, pairs, queries, before, after, weight, gain, setting, spans, frames, first):
    size, width = queries[0].shape
    toks = size // frames
    lead = setting is None
    total, wide = GROUP * frames, GROUP * frames + 2 * BAND
    heads = [slice(h * HEAD_DIM, (h + 1) * HEAD_DIM) for h in range(width // HEAD_DIM)]
    own_lanes = slice(first, first + width)

    def kernel(scalars, ins, outs, scratch, sems):
        mine = scalars[0][0]
        kv, qs = ins[:GROUP], ins[GROUP : GROUP + 2]
        prev, following, w_ref, g_ref = ins[GROUP + 2 : GROUP + 6]
        mixed, up, down, keys_out = outs[:4]
        q_s, k_s, c_s = scratch[:3]
        pieces, per = size // PIECE, toks // PIECE

        def taken(k, j, f):
            if k < 2:
                top = j * size + f * toks
                return ins[k][top : top + toks, own_lanes]
            if j == 2:
                return qs[k - 2][f * toks : (f + 1) * toks]
            src = kv[k] if k < GROUP else (prev, following)[k - GROUP]
            return src[j * size + f * toks : j * size + (f + 1) * toks]

        def note(k, i):
            if k < 2:
                return read_note(ins[k], 3 * size, 0, ins[k].shape[1], i)
            src = kv[k] if k < GROUP else (prev, following)[k - GROUP]
            return read_note(src, 2 * size, 0, width, i)

        if lead:
            pose_out, meta_out = outs[4:]
            meta = scratch[3]
            for k in range(GROUP):
                meta_out[mine ^ k] = note(k, pieces).astype(F32).astype(I32)[:META]
            known = pltpu.make_async_copy(meta_out, meta, sems.at[0])
            known.start()
        else:
            meta = scalars[1]
        for k in range(GROUP + 2):
            at = BAND + (mine ^ k) * frames if k < GROUP else (0 if k == GROUP else BAND + total)
            if lead:
                patches = [jnp.concatenate([note(k, f * per + i) for i in range(per)], axis=0) for f in range(frames)]
                for f in range(frames):
                    pose_out[at + f] = patches[f]
            else:
                patches = [ins[-1][at + f] for f in range(frames)]
            hint = jnp.dot(jnp.concatenate(patches, axis=0), w_ref[:, own_lanes], preferred_element_type=F32)
            hint = hint.astype(BF16).astype(F32)
            for f in range(frames):
                own = hint[f * toks : (f + 1) * toks]
                key = taken(k, 0, f)
                keys_out[at + f] = key
                k_s[at + f] = (key.astype(F32) + own).astype(BF16)
                c_s[at + f] = (taken(k, 1, f).astype(F32) + own).astype(BF16)
                if k < GROUP:
                    q_s[k * frames + f] = (taken(k, 2, f).astype(F32) + own).astype(BF16)
        if lead:
            known.wait()
        for k in range(GROUP):
            s = mine ^ k
            at, jobs = [], []
            for r in range(frames):
                f = s * frames + r
                spots = [BAND + f + meta[s, r, j] for j in range(spans)]
                for cols in heads:
                    at.append((r, meta[s, r, spans].astype(F32), cols))
                    jobs.append((q_s[k * frames + r, :, cols], band(k_s, spots, cols), band(c_s, spots, cols)))
            for (r, flag, cols), out in zip(at, attend(jobs)):
                scale = g_ref[:, first + cols.start : first + cols.stop]
                residual = (flag * scale * out.astype(F32)).astype(BF16)
                plain = taken(k, 1, r)[:, cols].astype(F32)
                mixed[s * frames + r, :, cols] = (plain + residual.astype(F32)).astype(BF16)
        up[...] = mixed[total - BAND :]
        down[...] = mixed[:BAND]

    outs = [rows((total, toks, width)), rows((BAND, toks, width)), rows((BAND, toks, width)), rows((wide, toks, width))]
    scratch = [
        pltpu.VMEM((total, toks, width), BF16),
        pltpu.VMEM((wide, toks, width), BF16),
        pltpu.VMEM((wide, toks, width), BF16),
    ]
    ins = [*near, *pairs, *queries, before, after, weight, gain]
    scalars = [me]
    if lead:
        outs += [rows((wide, toks, HEAD_DIM)), rows((GROUP, META, HEAD_DIM), I32)]
        scratch.append(pltpu.SMEM((GROUP, META, HEAD_DIM), I32))
    else:
        ins.append(setting[0])
        scalars.append(setting[1])
    return run(kernel, "hint_branch", ins, outs, scratch, 1, scalars, us=0.5 + 0.8 * len(heads))


def base_block(me, near, queries, keys, mixed, mixed_before, mixed_after, meta, spans, first):
    total, toks, width = mixed.shape
    frames, wide = total // GROUP, total + 2 * BAND
    size = frames * toks
    heads = [slice(h * HEAD_DIM, (h + 1) * HEAD_DIM) for h in range(width // HEAD_DIM)]

    def kernel(scalars, ins, outs, scratch, sems):
        mine, meta = scalars[0][0], scalars[1]
        k_ref, m_s = ins[GROUP], scratch[0]
        m_s[BAND : BAND + total] = ins[GROUP + 1][...]
        m_s[:BAND] = ins[GROUP + 2][...]
        m_s[BAND + total :] = ins[GROUP + 3][...]
        for k in range(GROUP):
            s = mine ^ k
            at, jobs = [], []
            for r in range(frames):
                spots = [BAND + s * frames + r + meta[s, r, j] for j in range(spans)]
                for cols in heads:
                    at.append((r, cols))
                    if k < 2:
                        top = 2 * size + r * toks
                        query = ins[k][top : top + toks, first + cols.start : first + cols.stop]
                    else:
                        query = ins[k][r * toks : (r + 1) * toks, cols]
                    jobs.append((query, band(k_ref, spots, cols), band(m_s, spots, cols)))
            for (r, cols), out in zip(at, attend(jobs)):
                outs[k][r, :, cols] = out

    ins = [*near, *queries, keys, mixed, mixed_before, mixed_after]
    scratch = [pltpu.VMEM((wide, toks, width), BF16)]
    outs = [rows((frames, toks, width))] * GROUP
    return run(kernel, "base_block", ins, outs, scratch, 0, [me, meta], us=0.7 * len(heads))


def place(me, parts, into, model_width, quarter, first):
    frames, toks, width = parts[0].shape

    def kernel(scalars, ins, outs, scratch, sems):
        mine = scalars[0][0]
        move([(ins[k], outs[0].at[:, :, lanes(mine ^ k, quarter, first, width)]) for k in range(GROUP)], sems)

    held = [] if into is None else [into]
    return run(
        kernel,
        "place",
        [*parts, *held],
        [rows((frames, toks, model_width))],
        [],
        GROUP,
        [me],
        where=[VMEM] * GROUP + [HBM] * len(held),
        to=HBM,
        aliases={} if into is None else {1 + GROUP: 0},
        us=0.8,
    )[0]


def solution(mesh):
    count = mesh.shape["tm"]
    assert count % GROUP == 0
    across = [[(i, i ^ k) for i in range(count)] for k in range(GROUP)]
    upward = [(i, (i + GROUP) % count) for i in range(count)]
    downward = [(i, (i - GROUP) % count) for i in range(count)]

    def exchange(parts):
        return [parts[0]] + [lax.ppermute(parts[k], "tm", across[k]) for k in range(1, GROUP)]

    def body(queries, key_states, value_states, pose_depth, hint_weight, control_gain, band_offsets, control_flags):
        frames, _, model_width = queries.shape
        spans = band_offsets.shape[1]
        quarter = model_width // GROUP
        assert frames == BAND and sum(SLICES) * HEAD_DIM == quarter
        me = lax.rem(lax.axis_index("tm"), GROUP).astype(I32).reshape(1)
        gain = control_gain.reshape(1, -1)
        queries, key_states, value_states, pose_depth, hint_weight, gain, band_offsets, control_flags = [
            pltpu.with_memory_space_constraint(a, pltpu.HBM)
            for a in (
                queries, key_states, value_states, pose_depth, hint_weight, gain, band_offsets, control_flags
            )
        ]
        cuts = [(sum(SLICES[:c]) * HEAD_DIM, n * HEAD_DIM) for c, n in enumerate(SLICES)]
        wires = {"y": [], "z": []}

        def after(values, wire, depth):
            if len(wires[wire]) < depth:
                return values
            return lax.optimization_barrier((values, wires[wire][-depth]))[0]

        def far_group(parts):
            got = []
            for part, k in zip(parts, (3, 2)):
                part = after(part, "y", DEPTH_Y)
                got.append(lax.ppermute(part, "tm", across[k]))
                wires["y"].append(got[-1])
            return [got[1], got[0]]

        def along(last, start):
            last, start = after([last, start], "z", DEPTH_Z)
            got = (lax.ppermute(last, "tm", upward), lax.ppermute(start, "tm", downward))
            wires["z"].append(got)
            return got

        size = frames * queries.shape[1]
        notes = [pose_depth, band_offsets, control_flags]
        pairs, asked, sides, mixed, parts = {}, {}, {}, {}, {}
        state = {"setting": None, "out": None}

        def step(name, c):
            first, width = cuts[c]
            if name == "KV":
                sent = pack(me, (3, 2), [key_states, value_states], notes if c == 0 else [], quarter, first, width)
                pairs[c] = far_group(sent)
            elif name == "C":
                mine, other = pack(me, (0, 1), [key_states, value_states, queries], notes, quarter, 0, quarter)
                state["near"] = [mine, lax.ppermute(other, "tm", across[1])]
                state["shares"] = share_of(me, hint_weight, gain, quarter)
            elif name == "Q":
                asked[c] = far_group(pack(me, (3, 2), [queries], [], quarter, first, width))
            elif name == "Z":
                sides[c] = along(*edges(me, state["near"], pairs[c], size, first, width, c == 0))
            elif name == "H":
                got = hint_branch(
                    me, state["near"], pairs[c], asked[c], *sides[c], *state["shares"], state["setting"], spans, frames, first
                )
                if state["setting"] is None:
                    state["setting"] = got[4:]
                mixed[c] = (got[3], got[0], *along(got[1], got[2]))
            elif name == "B":
                mine, other, *far = base_block(
                    me, state["near"], asked[c], *mixed[c], state["setting"][1], spans, first
                )
                far = far_group(far[::-1])
                parts[c] = [mine, lax.ppermute(other, "tm", across[1]), *far]
            else:
                state["out"] = place(me, parts[c], state["out"], model_width, quarter, first)

        for name, c in ORDER:
            step(name, c)
        return state["out"]

    return jax.shard_map(
        body,
        mesh=mesh,
        in_specs=(
            P(("grp", "tm"), None, None),
            P(("grp", "tm"), None, None),
            P(("grp", "tm"), None, None),
            P(("grp", "tm"), None, None),
            P(),
            P(),
            P(("grp", "tm"), None),
            P(("grp", "tm")),
        ),
        out_specs=P(("grp", "tm"), None, None),
        check_vma=False,
    )
```

time: 94.6 us -> 87.1 us (0.921)
  waiting for transfers between devices: 34.5 us -> 27.6 us
  Pallas kernels: 19.4 us -> 24.9 us
  local copies, waits for them, and re-layouts: 4.75 us -> 0 us
  starting transfers between devices: 35.1 us -> 33.3 us
    ppermute x18 -> x15, waiting for transfers between devices: 33.8 us -> 26 us  [the longest x12 26 us: far_group(): got.append(lax.ppermute(part, 'tm', across[k]))]
    pallas_call x12 -> x14, Pallas kernels: 19.4 us -> 24.9 us  [run(): pl.pallas_call(body, out_shape=list(outs), in_specs=[SMEM] * a + (where i...]
    unnamed x20 -> x0, local copies, waits for them, and re-layouts: 4.75 us -> none
    ppermute x4, starting transfers between devices: 6.77 us -> 3.73 us  [along(): lax.ppermute(last, 'tm', upward)]
    ppermute x4, starting transfers between devices: 8.92 us -> 11.2 us  [along(): lax.ppermute(start, 'tm', downward)]
    ppermute x4, waiting for transfers between devices: 0.68 us -> 1.65 us  [along(): lax.ppermute(start, 'tm', downward)]
    ppermute x18 -> x15, starting transfers between devices: 19.4 us -> 18.5 us  [the longest x12 17.9 us: far_group(): got.append(lax.ppermute(part, 'tm', across[k]))]
  transfers between devices with their start and end apart: 26 -> 23, of which waited for: 10 -> 9; matrix products, arithmetic and copies ran while one was open for 0% -> 0% of each run, Pallas kernels for 19% -> 26%
where the time goes in v4:
time: 87.1 us; the launch traced here: 86.2 us
  starting transfers between devices  33.3 us (38%)
  waiting for transfers between devices  27.6 us (32%)
  Pallas kernels  24.9 us (29%)
    ppermute x12, waiting for transfers between devices, far_group(): got.append(lax.ppermute(part, 'tm', across[k]))  26 us
    pallas_call x14, Pallas kernels, run(): pl.pallas_call(body, out_shape=list(outs), in_specs=[SMEM] * a + (where i...  24.9 us
    ppermute x12, starting transfers between devices, far_group(): got.append(lax.ppermute(part, 'tm', across[k]))  17.9 us
    ppermute x4, starting transfers between devices, along(): lax.ppermute(start, 'tm', downward)  11.2 us
    ppermute x4, starting transfers between devices, along(): lax.ppermute(last, 'tm', upward)  3.73 us
  transfers between devices with their start and end apart: 23, of which 9 were waited for; matrix products, arithmetic and copies ran while one was open for 0% of the time, Pallas kernels for 26%

profile of v4, /device:TPU:1, one launch (start us, length us, event | category | flops | bytes accessed | tf_op | source)
XLA Modules:
  0.0 86.2 jit_solution(5552274012481648397)
XLA Ops:
  0.0 1.7 %pack.5 = (bf16[400,1280]{1,0:T(8,128)(2,1)S(1)}, bf16[400,1280]{1,0:T(8,128)(2,1)S(1)}) custom-call(s32[1]{0:T(128)} %bitcast.refs_0_, bf16[2,64,5120]{2,1,0:T(8,128)(2,1)} %refs_1_.9, bf16[2,64,5120]{2,1,0:T(8,128)(2,1)} %refs_2_.5, bf16[2,64,5120]{2,1,0:T(8,128)(2,1)} %refs_1_.11, bf16[2,64,128]{2,1,0:T(8,128)(2,1)} %refs_3_.3, s32[2,3]{1,0:T(2,128)} %refs_4_.3, ...), custom_call_target="tpu_custom_call" | custom-call | flops 1 | bytes 3400000 | tf_op jit(solution)/shard_map/pack/pallas_call | solution.py:30
  1.8 1.3 %pack.6 = (bf16[288,640]{1,0:T(8,128)(2,1)S(1)}, bf16[288,640]{1,0:T(8,128)(2,1)S(1)}) custom-call(s32[1]{0:T(128)} %bitcast.refs_0_, bf16[2,64,5120]{2,1,0:T(8,128)(2,1)} %refs_1_.9, bf16[2,64,5120]{2,1,0:T(8,128)(2,1)} %refs_2_.5, bf16[2,64,128]{2,1,0:T(8,128)(2,1)} %refs_3_.3, s32[2,3]{1,0:T(2,128)} %refs_4_.3, s32[2]{0:T(128)} %refs_5_.3), custom_call_target="tpu_custom_call" | custom-call | flops 1 | bytes 3400000 | tf_op jit(solution)/shard_map/pack/pallas_call | solution.py:30
  3.1 2.7 %collective-permute-start.2 = (bf16[288,640]{1,0:T(8,128)(2,1)S(1)}, bf16[288,640]{1,0:T(8,128)(2,1)S(1)}, u32[]{:S(2)}, u32[]{:S(2)}) collective-permute-start(bf16[288,640]{1,0:T(8,128)(2,1)S(1)} %get-tuple-element.55), channel_id=1, source_target_pairs={{0,3},{1,2},{2,1},{3,0},{4,7},{5,6},{6,5},{7,4},{8,11},{9,10},{10,... | collective-permute-start | bytes 1105928 | tf_op jit(solution)/shard_map/ppermute | solution.py:360
  7.2 2.0 %collective-permute-start.3 = (bf16[256,640]{1,0:T(8,128)(2,1)S(1)}, bf16[256,640]{1,0:T(8,128)(2,1)S(1)}, u32[]{:S(2)}, u32[]{:S(2)}) collective-permute-start(bf16[256,640]{1,0:T(8,128)(2,1)S(1)} %get-tuple-element.57), channel_id=1, source_target_pairs={{0,3},{1,2},{2,1},{3,0},{4,7},{5,6},{6,5},{7,4},{8,11},{9,10},{10,... | collective-permute-start | bytes 983048 | tf_op jit(solution)/shard_map/ppermute | solution.py:360
  9.2 5.7 %collective-permute-done.2.refs_4_ = bf16[288,640]{1,0:T(8,128)(2,1)S(1)} collective-permute-done((bf16[288,640]{1,0:T(8,128)(2,1)S(1)}, bf16[288,640]{1,0:T(8,128)(2,1)S(1)}, u32[]{:S(2)}, u32[]{:S(2)}) %collective-permute-start.2) | collective-permute-done | bytes 368672 | tf_op jit(solution)/shard_map/ppermute | solution.py:360
  14.9 1.8 %collective-permute-start.9 = (bf16[256,640]{1,0:T(8,128)(2,1)S(1)}, bf16[256,640]{1,0:T(8,128)(2,1)S(1)}, u32[]{:S(2)}, u32[]{:S(2)}) collective-permute-start(bf16[256,640]{1,0:T(8,128)(2,1)S(1)} %get-tuple-element.70), channel_id=1, source_target_pairs={{0,2},{1,3},{2,0},{3,1},{4,6},{5,7},{6,4},{7,5},{8,10},{9,11},{10,... | collective-permute-start | bytes 983048 | tf_op jit(solution)/shard_map/ppermute | solution.py:360
  16.7 6.0 %collective-permute-done.1.refs_3_ = bf16[288,640]{1,0:T(8,128)(2,1)S(1)} collective-permute-done((bf16[288,640]{1,0:T(8,128)(2,1)S(1)}, bf16[288,640]{1,0:T(8,128)(2,1)S(1)}, u32[]{:S(2)}, u32[]{:S(2)}) %collective-permute-start.1) | collective-permute-done | bytes 368672 | tf_op jit(solution)/shard_map/ppermute | solution.py:360
  23.9 2.3 %collective-permute-start.7 = (bf16[288,640]{1,0:T(8,128)(2,1)S(1)}, bf16[288,640]{1,0:T(8,128)(2,1)S(1)}, u32[]{:S(2)}, u32[]{:S(2)}) collective-permute-start(bf16[288,640]{1,0:T(8,128)(2,1)S(1)} %get-tuple-element.62), channel_id=1, source_target_pairs={{0,12},{1,13},{2,14},{3,15},{4,0},{5,1},{6,2},{7,3},{8,4},{9,5},{1... | collective-permute-start | bytes 1105928 | tf_op jit(solution)/shard_map/ppermute | solution.py:366
  27.2 3.1 %collective-permute-start.5 = (bf16[128,640]{1,0:T(8,128)(2,1)S(1)}, bf16[128,640]{1,0:T(8,128)(2,1)S(1)}, u32[]{:S(2)}, u32[]{:S(2)}) collective-permute-start(bf16[128,640]{1,0:T(8,128)(2,1)S(1)} %get-tuple-element.60), channel_id=1, source_target_pairs={{0,3},{1,2},{2,1},{3,0},{4,7},{5,6},{6,5},{7,4},{8,11},{9,10},{10,... | collective-permute-start | bytes 491528 | tf_op jit(solution)/shard_map/ppermute | solution.py:360
  30.3 1.6 %collective-permute-start.4 = (bf16[128,640]{1,0:T(8,128)(2,1)S(1)}, bf16[128,640]{1,0:T(8,128)(2,1)S(1)}, u32[]{:S(2)}, u32[]{:S(2)}) collective-permute-start(bf16[128,640]{1,0:T(8,128)(2,1)S(1)} %get-tuple-element.58), channel_id=1, source_target_pairs={{0,2},{1,3},{2,0},{3,1},{4,6},{5,7},{6,4},{7,5},{8,10},{9,11},{10,... | collective-permute-start | bytes 491528 | tf_op jit(solution)/shard_map/ppermute | solution.py:360
  31.9 4.8 %collective-permute-done.9.refs_3_.refs_4_ = bf16[256,640]{1,0:T(8,128)(2,1)S(1)} collective-permute-done((bf16[256,640]{1,0:T(8,128)(2,1)S(1)}, bf16[256,640]{1,0:T(8,128)(2,1)S(1)}, u32[]{:S(2)}, u32[]{:S(2)}) %collective-permute-start.9) | collective-permute-done | bytes 327712 | tf_op jit(solution)/shard_map/ppermute | solution.py:360
  37.9 2.8 %collective-permute-done.5.refs_6_.refs_5_ = bf16[128,640]{1,0:T(8,128)(2,1)S(1)} collective-permute-done((bf16[128,640]{1,0:T(8,128)(2,1)S(1)}, bf16[128,640]{1,0:T(8,128)(2,1)S(1)}, u32[]{:S(2)}, u32[]{:S(2)}) %collective-permute-start.5) | collective-permute-done | bytes 163872 | tf_op jit(solution)/shard_map/ppermute | solution.py:360
  40.7 3.9 %collective-permute-start.12 = (bf16[256,640]{1,0:T(8,128)(2,1)S(1)}, bf16[256,640]{1,0:T(8,128)(2,1)S(1)}, u32[]{:S(2)}, u32[]{:S(2)}) collective-permute-start(bf16[256,640]{1,0:T(8,128)(2,1)S(1)} %get-tuple-element.73), channel_id=1, source_target_pairs={{0,12},{1,13},{2,14},{3,15},{4,0},{5,1},{6,2},{7,3},{8,4},{9,5},{1... | collective-permute-start | bytes 983048 | tf_op jit(solution)/shard_map/ppermute | solution.py:366
  45.6 1.3 %collective-permute-start.8 = (bf16[128,640]{1,0:T(8,128)(2,1)S(1)}, bf16[128,640]{1,0:T(8,128)(2,1)S(1)}, u32[]{:S(2)}, u32[]{:S(2)}) collective-permute-start(bf16[128,640]{1,0:T(8,128)(2,1)S(1)} %get-tuple-element.67), channel_id=1, source_target_pairs={{0,2},{1,3},{2,0},{3,1},{4,6},{5,7},{6,4},{7,5},{8,10},{9,11},{10,... | collective-permute-start | bytes 491528 | tf_op jit(solution)/shard_map/ppermute | solution.py:360
  48.0 4.4 %hint_branch.2 = (bf16[8,64,640]{2,1,0:T(8,128)(2,1)S(1)}, bf16[2,64,640]{2,1,0:T(8,128)(2,1)S(1)}, bf16[2,64,640]{2,1,0:T(8,128)(2,1)S(1)}, bf16[12,64,640]{2,1...) custom-call(s32[1]{0:T(128)} %bitcast.refs_0_, ...), custom_call_target="tpu_custom_call" | custom-call | flops 1 | bytes 15300000 | tf_op jit(solution)/shard_map/hint_branch/pallas_call | solution.py:30
  52.9 2.8 %collective-permute-start.17 = (bf16[2,64,640]{2,1,0:T(8,128)(2,1)S(1)}, bf16[2,64,640]{2,1,0:T(8,128)(2,1)S(1)}, u32[]{:S(2)}, u32[]{:S(2)}) collective-permute-start(bf16[2,64,640]{2,1,0:T(8,128)(2,1)S(1)} %get-tuple-element.89), channel_id=1, source_target_pairs={{0,12},{1,13},{2,14},{3,15},{4,0},{5,1},{6,2},{7,3},{8,4},{9,5},{1... | collective-permute-start | bytes 491528 | tf_op jit(solution)/shard_map/ppermute | solution.py:366
  56.7 4.3 %hint_branch.3 = (bf16[8,64,640]{2,1,0:T(8,128)(2,1)S(1)}, bf16[2,64,640]{2,1,0:T(8,128)(2,1)S(1)}, bf16[2,64,640]{2,1,0:T(8,128)(2,1)S(1)}, bf16[12,64,640]{2,1,0:T(8,128)(2,1)S(1)}) custom-call(s32[1]{0:T(128)} %bitcast.refs_0_, s32[4,8,128]{2,1,0:T(8,128)S(1)} %get-tuple-element.65.refs_1_, bf16[400,1280]{1,0:T(8,128)(2,1)S(1)} %get-tuple-element.52.refs_1_.refs_2_, ...), custom_call_target="tpu_custom_call" | custom-call | flops 1 | bytes 15300000 | tf_op jit(solution)/shard_map/hint_branch/pallas_call | solution.py:30
  62.1 2.2 %collective-permute-start.14 = (bf16[2,64,640]{2,1,0:T(8,128)(2,1)S(1)}, bf16[2,64,640]{2,1,0:T(8,128)(2,1)S(1)}, u32[]{:S(2)}, u32[]{:S(2)}) collective-permute-start(bf16[2,64,640]{2,1,0:T(8,128)(2,1)S(1)} %get-tuple-element.80), channel_id=1, source_target_pairs={{0,12},{1,13},{2,14},{3,15},{4,0},{5,1},{6,2},{7,3},{8,4},{9,5},{1... | collective-permute-start | bytes 491528 | tf_op jit(solution)/shard_map/ppermute | solution.py:366
  64.3 3.5 %base_block.3 = (bf16[2,64,640]{2,1,0:T(8,128)(2,1)S(1)}, bf16[2,64,640]{2,1,0:T(8,128)(2,1)S(1)}, bf16[2,64,640]{2,1,0:T(8,128)(2,1)S(1)}, bf16[2,64,640]{2,1,0:T(8,128)(2,1)S(1)}) custom-call(s32[1]{0:T(128)} %bitcast.refs_0_, s32[4,8,128]{2,1,0:T(8,128)S(1)} %get-tuple-element.65.refs_1_, bf16[400,1280]{1,0:T(8,128)(2,1)S(1)} %get-tuple-element.52.refs_1_.refs_2_, ...), custom_call_target="tpu_custom_call" | custom-call | flops 1 | bytes 11900000 | tf_op jit(solution)/shard_map/base_block/pallas_call | solution.py:30
  67.8 1.9 %collective-permute-start.18 = (bf16[2,64,640]{2,1,0:T(8,128)(2,1)S(1)}, bf16[2,64,640]{2,1,0:T(8,128)(2,1)S(1)}, u32[]{:S(2)}, u32[]{:S(2)}) collective-permute-start(bf16[2,64,640]{2,1,0:T(8,128)(2,1)S(1)} %get-tuple-element.91), channel_id=1, source_target_pairs={{0,3},{1,2},{2,1},{3,0},{4,7},{5,6},{6,5},{7,4},{8,11},{9,10},{10,... | collective-permute-start | bytes 491528 | tf_op jit(solution)/shard_map/ppermute | solution.py:360
  71.0 3.5 %base_block.2 = (bf16[2,64,640]{2,1,0:T(8,128)(2,1)S(1)}, bf16[2,64,640]{2,1,0:T(8,128)(2,1)S(1)}, bf16[2,64,640]{2,1,0:T(8,128)(2,1)S(1)}, bf16[2,64,640]{2,1,0:T(8,128)(2,1)S(1)}) custom-call(s32[1]{0:T(128)} %bitcast.refs_0_, s32[4,8,128]{2,1,0:T(8,128)S(1)} %get-tuple-element.65.refs_1_, bf16[400,1280]{1,0:T(8,128)(2,1)S(1)} %get-tuple-element.52.refs_1_.refs_2_, ...), custom_call_target="tpu_custom_call" | custom-call | flops 1 | bytes 11900000 | tf_op jit(solution)/shard_map/base_block/pallas_call | solution.py:30
  74.5 2.6 %collective-permute-start.20 = (bf16[2,64,640]{2,1,0:T(8,128)(2,1)S(1)}, bf16[2,64,640]{2,1,0:T(8,128)(2,1)S(1)}, u32[]{:S(2)}, u32[]{:S(2)}) collective-permute-start(bf16[2,64,640]{2,1,0:T(8,128)(2,1)S(1)} %get-tuple-element.94), channel_id=1, source_target_pairs={{0,3},{1,2},{2,1},{3,0},{4,7},{5,6},{6,5},{7,4},{8,11},{9,10},{10,... | collective-permute-start | bytes 491528 | tf_op jit(solution)/shard_map/ppermute | solution.py:360
  79.0 2.9 %collective-permute-done.20.refs_4_ = bf16[2,64,640]{2,1,0:T(8,128)(2,1)S(1)} collective-permute-done((bf16[2,64,640]{2,1,0:T(8,128)(2,1)S(1)}, bf16[2,64,640]{2,1,0:T(8,128)(2,1)S(1)}, u32[]{:S(2)}, u32[]{:S(2)}) %collective-permute-start.20) | collective-permute-done | bytes 163872 | tf_op jit(solution)/shard_map/ppermute | solution.py:360
  81.9 3.3 %collective-permute-done.19.refs_3_ = bf16[2,64,640]{2,1,0:T(8,128)(2,1)S(1)} collective-permute-done((bf16[2,64,640]{2,1,0:T(8,128)(2,1)S(1)}, bf16[2,64,640]{2,1,0:T(8,128)(2,1)S(1)}, u32[]{:S(2)}, u32[]{:S(2)}) %collective-permute-start.19) | collective-permute-done | bytes 163872 | tf_op jit(solution)/shard_map/ppermute | solution.py:360
  (36 shorter events, 13.5 us)
Async XLA Ops:
  1.7 21.0 %collective-permute-start = (bf16[400,1280]{1,0:T(8,128)(2,1)S(1)}, bf16[400,1280]{1,0:T(8,128)(2,1)S(1)}, u32[]{:S(2)}, u32[]{:S(2)}) collective-permute-start(bf16[400,1280]{1,0:T(8,128)(2,1)S(1)} %get-tuple-element.53), channel_id=1, source_target_pairs={{0,1},{1,0},{2,3},{3,2},{4,5},{5,4},{6,7},{7,6},{8,9},{9,8},{10,11... | collective-permute-start | bytes 3072008 | tf_op jit(solution)/shard_map/ppermute | solution.py:382
  3.1 11.8 %collective-permute-start.2 = (bf16[288,640]{1,0:T(8,128)(2,1)S(1)}, bf16[288,640]{1,0:T(8,128)(2,1)S(1)}, u32[]{:S(2)}, u32[]{:S(2)}) collective-permute-start(bf16[288,640]{1,0:T(8,128)(2,1)S(1)} %get-tuple-element.55), channel_id=1, source_target_pairs={{0,3},{1,2},{2,1},{3,0},{4,7},{5,6},{6,5},{7,4},{8,11},{9,10},{10,... | collective-permute-start | bytes 1105928 | tf_op jit(solution)/shard_map/ppermute | solution.py:360
  5.8 16.9 %collective-permute-start.1 = (bf16[288,640]{1,0:T(8,128)(2,1)S(1)}, bf16[288,640]{1,0:T(8,128)(2,1)S(1)}, u32[]{:S(2)}, u32[]{:S(2)}) collective-permute-start(bf16[288,640]{1,0:T(8,128)(2,1)S(1)} %get-tuple-element.54), channel_id=1, source_target_pairs={{0,2},{1,3},{2,0},{3,1},{4,6},{5,7},{6,4},{7,5},{8,10},{9,11},{10,... | collective-permute-start | bytes 1105928 | tf_op jit(solution)/shard_map/ppermute | solution.py:360
  7.2 23.1 %collective-permute-start.3 = (bf16[256,640]{1,0:T(8,128)(2,1)S(1)}, bf16[256,640]{1,0:T(8,128)(2,1)S(1)}, u32[]{:S(2)}, u32[]{:S(2)}) collective-permute-start(bf16[256,640]{1,0:T(8,128)(2,1)S(1)} %get-tuple-element.57), channel_id=1, source_target_pairs={{0,3},{1,2},{2,1},{3,0},{4,7},{5,6},{6,5},{7,4},{8,11},{9,10},{10,... | collective-permute-start | bytes 983048 | tf_op jit(solution)/shard_map/ppermute | solution.py:360
  14.9 21.8 %collective-permute-start.9 = (bf16[256,640]{1,0:T(8,128)(2,1)S(1)}, bf16[256,640]{1,0:T(8,128)(2,1)S(1)}, u32[]{:S(2)}, u32[]{:S(2)}) collective-permute-start(bf16[256,640]{1,0:T(8,128)(2,1)S(1)} %get-tuple-element.70), channel_id=1, source_target_pairs={{0,2},{1,3},{2,0},{3,1},{4,6},{5,7},{6,4},{7,5},{8,10},{9,11},{10,... | collective-permute-start | bytes 983048 | tf_op jit(solution)/shard_map/ppermute | solution.py:360
  22.8 24.1 %collective-permute-start.6 = (bf16[288,640]{1,0:T(8,128)(2,1)S(1)}, bf16[288,640]{1,0:T(8,128)(2,1)S(1)}, u32[]{:S(2)}, u32[]{:S(2)}) collective-permute-start(bf16[288,640]{1,0:T(8,128)(2,1)S(1)} %get-tuple-element.61), channel_id=1, source_target_pairs={{0,4},{1,5},{2,6},{3,7},{4,8},{5,9},{6,10},{7,11},{8,12},{9,13},{1... | collective-permute-start | bytes 1105928 | tf_op jit(solution)/shard_map/ppermute | solution.py:366
  23.9 24.1 %collective-permute-start.7 = (bf16[288,640]{1,0:T(8,128)(2,1)S(1)}, bf16[288,640]{1,0:T(8,128)(2,1)S(1)}, u32[]{:S(2)}, u32[]{:S(2)}) collective-permute-start(bf16[288,640]{1,0:T(8,128)(2,1)S(1)} %get-tuple-element.62), channel_id=1, source_target_pairs={{0,12},{1,13},{2,14},{3,15},{4,0},{5,1},{6,2},{7,3},{8,4},{9,5},{1... | collective-permute-start | bytes 1105928 | tf_op jit(solution)/shard_map/ppermute | solution.py:366
  27.2 13.5 %collective-permute-start.5 = (bf16[128,640]{1,0:T(8,128)(2,1)S(1)}, bf16[128,640]{1,0:T(8,128)(2,1)S(1)}, u32[]{:S(2)}, u32[]{:S(2)}) collective-permute-start(bf16[128,640]{1,0:T(8,128)(2,1)S(1)} %get-tuple-element.60), channel_id=1, source_target_pairs={{0,3},{1,2},{2,1},{3,0},{4,7},{5,6},{6,5},{7,4},{8,11},{9,10},{10,... | collective-permute-start | bytes 491528 | tf_op jit(solution)/shard_map/ppermute | solution.py:360
  30.3 15.3 %collective-permute-start.4 = (bf16[128,640]{1,0:T(8,128)(2,1)S(1)}, bf16[128,640]{1,0:T(8,128)(2,1)S(1)}, u32[]{:S(2)}, u32[]{:S(2)}) collective-permute-start(bf16[128,640]{1,0:T(8,128)(2,1)S(1)} %get-tuple-element.58), channel_id=1, source_target_pairs={{0,2},{1,3},{2,0},{3,1},{4,6},{5,7},{6,4},{7,5},{8,10},{9,11},{10,... | collective-permute-start | bytes 491528 | tf_op jit(solution)/shard_map/ppermute | solution.py:360
  36.8 18.9 %collective-permute-start.11 = (bf16[256,640]{1,0:T(8,128)(2,1)S(1)}, bf16[256,640]{1,0:T(8,128)(2,1)S(1)}, u32[]{:S(2)}, u32[]{:S(2)}) collective-permute-start(bf16[256,640]{1,0:T(8,128)(2,1)S(1)} %get-tuple-element.72), channel_id=1, source_target_pairs={{0,4},{1,5},{2,6},{3,7},{4,8},{5,9},{6,10},{7,11},{8,12},{9,13},{1... | collective-permute-start | bytes 983048 | tf_op jit(solution)/shard_map/ppermute | solution.py:366
  40.7 16.0 %collective-permute-start.12 = (bf16[256,640]{1,0:T(8,128)(2,1)S(1)}, bf16[256,640]{1,0:T(8,128)(2,1)S(1)}, u32[]{:S(2)}, u32[]{:S(2)}) collective-permute-start(bf16[256,640]{1,0:T(8,128)(2,1)S(1)} %get-tuple-element.73), channel_id=1, source_target_pairs={{0,12},{1,13},{2,14},{3,15},{4,0},{5,1},{6,2},{7,3},{8,4},{9,5},{1... | collective-permute-start | bytes 983048 | tf_op jit(solution)/shard_map/ppermute | solution.py:366
  45.6 7.3 %collective-permute-start.8 = (bf16[128,640]{1,0:T(8,128)(2,1)S(1)}, bf16[128,640]{1,0:T(8,128)(2,1)S(1)}, u32[]{:S(2)}, u32[]{:S(2)}) collective-permute-start(bf16[128,640]{1,0:T(8,128)(2,1)S(1)} %get-tuple-element.67), channel_id=1, source_target_pairs={{0,2},{1,3},{2,0},{3,1},{4,6},{5,7},{6,4},{7,5},{8,10},{9,11},{10,... | collective-permute-start | bytes 491528 | tf_op jit(solution)/shard_map/ppermute | solution.py:360
  46.9 8.8 %collective-permute-start.10 = (bf16[128,640]{1,0:T(8,128)(2,1)S(1)}, bf16[128,640]{1,0:T(8,128)(2,1)S(1)}, u32[]{:S(2)}, u32[]{:S(2)}) collective-permute-start(bf16[128,640]{1,0:T(8,128)(2,1)S(1)} %get-tuple-element.71), channel_id=1, source_target_pairs={{0,3},{1,2},{2,1},{3,0},{4,7},{5,6},{6,5},{7,4},{8,11},{9,10},{10,... | collective-permute-start | bytes 491528 | tf_op jit(solution)/shard_map/ppermute | solution.py:360
  52.4 11.9 %collective-permute-start.16 = (bf16[2,64,640]{2,1,0:T(8,128)(2,1)S(1)}, bf16[2,64,640]{2,1,0:T(8,128)(2,1)S(1)}, u32[]{:S(2)}, u32[]{:S(2)}) collective-permute-start(bf16[2,64,640]{2,1,0:T(8,128)(2,1)S(1)} %get-tuple-element.88), channel_id=1, source_target_pairs={{0,4},{1,5},{2,6},{3,7},{4,8},{5,9},{6,10},{7,11},{8,12},{9,13},{1... | collective-permute-start | bytes 491528 | tf_op jit(solution)/shard_map/ppermute | solution.py:366
  52.9 11.4 %collective-permute-start.17 = (bf16[2,64,640]{2,1,0:T(8,128)(2,1)S(1)}, bf16[2,64,640]{2,1,0:T(8,128)(2,1)S(1)}, u32[]{:S(2)}, u32[]{:S(2)}) collective-permute-start(bf16[2,64,640]{2,1,0:T(8,128)(2,1)S(1)} %get-tuple-element.89), channel_id=1, source_target_pairs={{0,12},{1,13},{2,14},{3,15},{4,0},{5,1},{6,2},{7,3},{8,4},{9,5},{1... | collective-permute-start | bytes 491528 | tf_op jit(solution)/shard_map/ppermute | solution.py:366
  61.0 9.3 %collective-permute-start.13 = (bf16[2,64,640]{2,1,0:T(8,128)(2,1)S(1)}, bf16[2,64,640]{2,1,0:T(8,128)(2,1)S(1)}, u32[]{:S(2)}, u32[]{:S(2)}) collective-permute-start(bf16[2,64,640]{2,1,0:T(8,128)(2,1)S(1)} %get-tuple-element.79), channel_id=1, source_target_pairs={{0,4},{1,5},{2,6},{3,7},{4,8},{5,9},{6,10},{7,11},{8,12},{9,13},{1... | collective-permute-start | bytes 491528 | tf_op jit(solution)/shard_map/ppermute | solution.py:366
  62.1 8.9 %collective-permute-start.14 = (bf16[2,64,640]{2,1,0:T(8,128)(2,1)S(1)}, bf16[2,64,640]{2,1,0:T(8,128)(2,1)S(1)}, u32[]{:S(2)}, u32[]{:S(2)}) collective-permute-start(bf16[2,64,640]{2,1,0:T(8,128)(2,1)S(1)} %get-tuple-element.80), channel_id=1, source_target_pairs={{0,12},{1,13},{2,14},{3,15},{4,0},{5,1},{6,2},{7,3},{8,4},{9,5},{1... | collective-permute-start | bytes 491528 | tf_op jit(solution)/shard_map/ppermute | solution.py:366
  67.8 9.7 %collective-permute-start.18 = (bf16[2,64,640]{2,1,0:T(8,128)(2,1)S(1)}, bf16[2,64,640]{2,1,0:T(8,128)(2,1)S(1)}, u32[]{:S(2)}, u32[]{:S(2)}) collective-permute-start(bf16[2,64,640]{2,1,0:T(8,128)(2,1)S(1)} %get-tuple-element.91), channel_id=1, source_target_pairs={{0,3},{1,2},{2,1},{3,0},{4,7},{5,6},{6,5},{7,4},{8,11},{9,10},{10,... | collective-permute-start | bytes 491528 | tf_op jit(solution)/shard_map/ppermute | solution.py:360
  69.7 8.4 %collective-permute-start.22 = (bf16[2,64,640]{2,1,0:T(8,128)(2,1)S(1)}, bf16[2,64,640]{2,1,0:T(8,128)(2,1)S(1)}, u32[]{:S(2)}, u32[]{:S(2)}) collective-permute-start(bf16[2,64,640]{2,1,0:T(8,128)(2,1)S(1)} %get-tuple-element.98), channel_id=1, source_target_pairs={{0,2},{1,3},{2,0},{3,1},{4,6},{5,7},{6,4},{7,5},{8,10},{9,11},{10,... | collective-permute-start | bytes 491528 | tf_op jit(solution)/shard_map/ppermute | solution.py:360
  70.3 7.8 %collective-permute-start.21 = (bf16[2,64,640]{2,1,0:T(8,128)(2,1)S(1)}, bf16[2,64,640]{2,1,0:T(8,128)(2,1)S(1)}, u32[]{:S(2)}, u32[]{:S(2)}) collective-permute-start(bf16[2,64,640]{2,1,0:T(8,128)(2,1)S(1)} %get-tuple-element.96), channel_id=1, source_target_pairs={{0,1},{1,0},{2,3},{3,2},{4,5},{5,4},{6,7},{7,6},{8,9},{9,8},{10,11... | collective-permute-start | bytes 491528 | tf_op jit(solution)/shard_map/ppermute | solution.py:400
  74.5 7.4 %collective-permute-start.20 = (bf16[2,64,640]{2,1,0:T(8,128)(2,1)S(1)}, bf16[2,64,640]{2,1,0:T(8,128)(2,1)S(1)}, u32[]{:S(2)}, u32[]{:S(2)}) collective-permute-start(bf16[2,64,640]{2,1,0:T(8,128)(2,1)S(1)} %get-tuple-element.94), channel_id=1, source_target_pairs={{0,3},{1,2},{2,1},{3,0},{4,7},{5,6},{6,5},{7,4},{8,11},{9,10},{10,... | collective-permute-start | bytes 491528 | tf_op jit(solution)/shard_map/ppermute | solution.py:360
  77.1 4.8 %collective-permute-start.15 = (bf16[2,64,640]{2,1,0:T(8,128)(2,1)S(1)}, bf16[2,64,640]{2,1,0:T(8,128)(2,1)S(1)}, u32[]{:S(2)}, u32[]{:S(2)}) collective-permute-start(bf16[2,64,640]{2,1,0:T(8,128)(2,1)S(1)} %get-tuple-element.82), channel_id=1, source_target_pairs={{0,1},{1,0},{2,3},{3,2},{4,5},{5,4},{6,7},{7,6},{8,9},{9,8},{10,11... | collective-permute-start | bytes 491528 | tf_op jit(solution)/shard_map/ppermute | solution.py:400
  77.6 7.6 %collective-permute-start.19 = (bf16[2,64,640]{2,1,0:T(8,128)(2,1)S(1)}, bf16[2,64,640]{2,1,0:T(8,128)(2,1)S(1)}, u32[]{:S(2)}, u32[]{:S(2)}) collective-permute-start(bf16[2,64,640]{2,1,0:T(8,128)(2,1)S(1)} %get-tuple-element.92), channel_id=1, source_target_pairs={{0,2},{1,3},{2,0},{3,1},{4,6},{5,7},{6,4},{7,5},{8,10},{9,11},{10,... | collective-permute-start | bytes 491528 | tf_op jit(solution)/shard_map/ppermute | solution.py:360

commit v5 on v4

--- a/solution.py
+++ b/solution.py
@@ -11,8 +11,6 @@
 SLICES = (5, 5)
 META = 8
 PIECE = 16
-ORDER = [("KV", 0), ("C", 0), ("KV", 1), ("Z", 0), ("Q", 0), ("Z", 1), ("Q", 1), ("H", 0), ("H", 1), ("B", 0), ("B", 1), ("P", 0), ("P", 1)]
-DEPTH_Y, DEPTH_Z = 3, 2
 F32 = jnp.float32
 BF16 = jnp.bfloat16
 I32 = jnp.int32
@@ -120,18 +118,25 @@
     return run(kernel, "pack", [*arrays, *notes], outs, scratch, copies, [me], where=HBM)
 
 
-def share_of(me, weight, gain, quarter):
+def pack_own(me, queries, weight, gain, quarter):
+    frames, toks, _ = queries.shape
+
     def kernel(scalars, ins, outs, scratch, sems):
         mine = scalars[0][0]
-        move([(i.at[:, lanes(mine, quarter, 0, quarter)], o) for i, o in zip(ins, outs)], sems)
-
-    outs = [rows((weight.shape[0], quarter)), rows((1, quarter), F32)]
-    return run(kernel, "share", [weight, gain], outs, [], 2, [me], where=HBM)
-
-
-def edges(me, near, far, size, first, width, lead):
-    pieces = size // PIECE + 1 if lead else 0
-
+        pairs = []
+        for k in range(2):
+            for f in range(frames):
+                where = lanes(mine ^ k, quarter, 0, quarter)
+                pairs.append((ins[0].at[f, :, where], outs[k].at[pl.ds(f * toks, toks)]))
+        for i in (1, 2):
+            pairs.append((ins[i].at[:, lanes(mine, quarter, 0, quarter)], outs[1 + i]))
+        move(pairs, sems)
+
+    outs = [rows((frames * toks, quarter))] * 2 + [rows((weight.shape[0], quarter)), rows((1, quarter), F32)]
+    return run(kernel, "pack_own", [queries, weight, gain], outs, [], 2 * frames + 2, [me], where=HBM)
+
+
+def edges(me, parts):
     def kernel(scalars, ins, outs, scratch, sems):
         mine = scalars[0][0]
         for out, owner in zip(outs, (GROUP - 1, 0)):
@@ -139,18 +144,10 @@
 
                 @pl.when((mine ^ k) == owner)
                 def _(out=out, k=k):
-                    if k >= 2:
-                        out[...] = ins[k][...]
-                    else:
-                        out[: 2 * size] = ins[k][: 2 * size, first : first + width]
-                        for i in range(pieces - 1):
-                            top, left = notes_at(i, width)
-                            top += 2 * size
-                            piece = read_note(ins[k], 3 * size, 0, ins[k].shape[1], i)
-                            out[top : top + PIECE, left : left + HEAD_DIM] = piece
-
-    shape = rows(far[0].shape)
-    return run(kernel, "edges", [*near, *far], [shape, shape], [], 0, [me], us=0.2)
+                    out[...] = ins[k][...]
+
+    shape = rows(parts[0].shape)
+    return run(kernel, "edges", parts, [shape, shape], [], 0, [me], us=0.2)
 
 
 def attend(jobs):
@@ -171,8 +168,8 @@
     return jnp.concatenate([ref[s, :, cols] for s in spots], axis=0)
 
 
-def hint_branch(me, near, pairs, queries, before, after, weight, gain, setting, spans, frames, first):
-    size, width = queries[0].shape
+def hint_branch(me, pairs, queries, before, after, weight, gain, setting, spans, frames, first):
+    size, width = queries[-1].shape
     toks = size // frames
     lead = setting is None
     total, wide = GROUP * frames, GROUP * frames + 2 * BAND
@@ -181,26 +178,19 @@
 
     def kernel(scalars, ins, outs, scratch, sems):
         mine = scalars[0][0]
-        kv, qs = ins[:GROUP], ins[GROUP : GROUP + 2]
-        prev, following, w_ref, g_ref = ins[GROUP + 2 : GROUP + 6]
+        sources, qs = [*ins[:GROUP], *ins[2 * GROUP : 2 * GROUP + 2]], ins[GROUP : 2 * GROUP]
+        w_ref, g_ref = ins[2 * GROUP + 2 : 2 * GROUP + 4]
         mixed, up, down, keys_out = outs[:4]
         q_s, k_s, c_s = scratch[:3]
         pieces, per = size // PIECE, toks // PIECE
 
         def taken(k, j, f):
-            if k < 2:
-                top = j * size + f * toks
-                return ins[k][top : top + toks, own_lanes]
-            if j == 2:
-                return qs[k - 2][f * toks : (f + 1) * toks]
-            src = kv[k] if k < GROUP else (prev, following)[k - GROUP]
-            return src[j * size + f * toks : j * size + (f + 1) * toks]
+            if j < 2:
+                return sources[k][j * size + f * toks : j * size + (f + 1) * toks]
+            return qs[k][f * toks : (f + 1) * toks, own_lanes if k < 2 else slice(None)]
 
         def note(k, i):
-            if k < 2:
-                return read_note(ins[k], 3 * size, 0, ins[k].shape[1], i)
-            src = kv[k] if k < GROUP else (prev, following)[k - GROUP]
-            return read_note(src, 2 * size, 0, width, i)
+            return read_note(sources[k], 2 * size, 0, width, i)
 
         if lead:
             pose_out, meta_out = outs[4:]
@@ -231,20 +221,19 @@
                     q_s[k * frames + f] = (taken(k, 2, f).astype(F32) + own).astype(BF16)
         if lead:
             known.wait()
+        at, jobs = [], []
         for k in range(GROUP):
-            s = mine ^ k
-            at, jobs = [], []
             for r in range(frames):
+                s = mine ^ k
                 f = s * frames + r
                 spots = [BAND + f + meta[s, r, j] for j in range(spans)]
                 for cols in heads:
-                    at.append((r, meta[s, r, spans].astype(F32), cols))
+                    at.append((k, r, f, meta[s, r, spans].astype(F32), cols))
                     jobs.append((q_s[k * frames + r, :, cols], band(k_s, spots, cols), band(c_s, spots, cols)))
-            for (r, flag, cols), out in zip(at, attend(jobs)):
-                scale = g_ref[:, first + cols.start : first + cols.stop]
-                residual = (flag * scale * out.astype(F32)).astype(BF16)
-                plain = taken(k, 1, r)[:, cols].astype(F32)
-                mixed[s * frames + r, :, cols] = (plain + residual.astype(F32)).astype(BF16)
+        for (k, r, f, flag, cols), out in zip(at, attend(jobs)):
+            scale = g_ref[:, first + cols.start : first + cols.stop]
+            residual = (flag * scale * out.astype(F32)).astype(BF16)
+            mixed[f, :, cols] = (taken(k, 1, r)[:, cols].astype(F32) + residual.astype(F32)).astype(BF16)
         up[...] = mixed[total - BAND :]
         down[...] = mixed[:BAND]
 
@@ -254,7 +243,7 @@
         pltpu.VMEM((wide, toks, width), BF16),
         pltpu.VMEM((wide, toks, width), BF16),
     ]
-    ins = [*near, *pairs, *queries, before, after, weight, gain]
+    ins = [*pairs, *queries, before, after, weight, gain]
     scalars = [me]
     if lead:
         outs += [rows((wide, toks, HEAD_DIM)), rows((GROUP, META, HEAD_DIM), I32)]
@@ -265,10 +254,9 @@
     return run(kernel, "hint_branch", ins, outs, scratch, 1, scalars, us=0.5 + 0.8 * len(heads))
 
 
-def base_block(me, near, queries, keys, mixed, mixed_before, mixed_after, meta, spans, first):
+def base_block(me, queries, keys, mixed, mixed_before, mixed_after, meta, spans, first):
     total, toks, width = mixed.shape
     frames, wide = total // GROUP, total + 2 * BAND
-    size = frames * toks
     heads = [slice(h * HEAD_DIM, (h + 1) * HEAD_DIM) for h in range(width // HEAD_DIM)]
 
     def kernel(scalars, ins, outs, scratch, sems):
@@ -277,23 +265,20 @@
         m_s[BAND : BAND + total] = ins[GROUP + 1][...]
         m_s[:BAND] = ins[GROUP + 2][...]
         m_s[BAND + total :] = ins[GROUP + 3][...]
+        at, jobs = [], []
         for k in range(GROUP):
-            s = mine ^ k
-            at, jobs = [], []
             for r in range(frames):
+                s = mine ^ k
                 spots = [BAND + s * frames + r + meta[s, r, j] for j in range(spans)]
                 for cols in heads:
-                    at.append((r, cols))
-                    if k < 2:
-                        top = 2 * size + r * toks
-                        query = ins[k][top : top + toks, first + cols.start : first + cols.stop]
-                    else:
-                        query = ins[k][r * toks : (r + 1) * toks, cols]
+                    at.append((k, r, cols))
+                    left = first if k < 2 else 0
+                    query = ins[k][r * toks : (r + 1) * toks, left + cols.start : left + cols.stop]
                     jobs.append((query, band(k_ref, spots, cols), band(m_s, spots, cols)))
-            for (r, cols), out in zip(at, attend(jobs)):
-                outs[k][r, :, cols] = out
-
-    ins = [*near, *queries, keys, mixed, mixed_before, mixed_after]
+        for (k, r, cols), out in zip(at, attend(jobs)):
+            outs[k][r, :, cols] = out
+
+    ins = [*queries, keys, mixed, mixed_before, mixed_after]
     scratch = [pltpu.VMEM((wide, toks, width), BF16)]
     outs = [rows((frames, toks, width))] * GROUP
     return run(kernel, "base_block", ins, outs, scratch, 0, [me, meta], us=0.7 * len(heads))
@@ -346,64 +331,61 @@
             )
         ]
         cuts = [(sum(SLICES[:c]) * HEAD_DIM, n * HEAD_DIM) for c, n in enumerate(SLICES)]
-        wires = {"y": [], "z": []}
-
-        def after(values, wire, depth):
-            if len(wires[wire]) < depth:
-                return values
-            return lax.optimization_barrier((values, wires[wire][-depth]))[0]
-
-        def far_group(parts):
+        far_wire, side_wire = [], []
+
+        def after(values, *deps):
+            deps = [d for d in deps if d is not None]
+            return lax.optimization_barrier((values, deps))[0] if deps else values
+
+        def back(wire, depth):
+            return wire[-depth] if 0 < depth <= len(wire) else None
+
+        def far_group(parts, depth, gate=None):
             got = []
             for part, k in zip(parts, (3, 2)):
-                part = after(part, "y", DEPTH_Y)
+                part = after(part, back(far_wire, depth), gate)
                 got.append(lax.ppermute(part, "tm", across[k]))
-                wires["y"].append(got[-1])
+                far_wire.append(got[-1])
+                gate = None
             return [got[1], got[0]]
 
+        def near_group(parts):
+            return [parts[0], lax.ppermute(parts[1], "tm", across[1])]
+
         def along(last, start):
-            last, start = after([last, start], "z", DEPTH_Z)
+            last, start = after([last, start], back(side_wire, 2))
             got = (lax.ppermute(last, "tm", upward), lax.ppermute(start, "tm", downward))
-            wires["z"].append(got)
+            side_wire.append(got)
             return got
 
+        n = len(cuts)
         size = frames * queries.shape[1]
-        notes = [pose_depth, band_offsets, control_flags]
-        pairs, asked, sides, mixed, parts = {}, {}, {}, {}, {}
-        state = {"setting": None, "out": None}
-
-        def step(name, c):
-            first, width = cuts[c]
-            if name == "KV":
-                sent = pack(me, (3, 2), [key_states, value_states], notes if c == 0 else [], quarter, first, width)
-                pairs[c] = far_group(sent)
-            elif name == "C":
-                mine, other = pack(me, (0, 1), [key_states, value_states, queries], notes, quarter, 0, quarter)
-                state["near"] = [mine, lax.ppermute(other, "tm", across[1])]
-                state["shares"] = share_of(me, hint_weight, gain, quarter)
-            elif name == "Q":
-                asked[c] = far_group(pack(me, (3, 2), [queries], [], quarter, first, width))
-            elif name == "Z":
-                sides[c] = along(*edges(me, state["near"], pairs[c], size, first, width, c == 0))
-            elif name == "H":
-                got = hint_branch(
-                    me, state["near"], pairs[c], asked[c], *sides[c], *state["shares"], state["setting"], spans, frames, first
-                )
-                if state["setting"] is None:
-                    state["setting"] = got[4:]
-                mixed[c] = (got[3], got[0], *along(got[1], got[2]))
-            elif name == "B":
-                mine, other, *far = base_block(
-                    me, state["near"], asked[c], *mixed[c], state["setting"][1], spans, first
-                )
-                far = far_group(far[::-1])
-                parts[c] = [mine, lax.ppermute(other, "tm", across[1]), *far]
-            else:
-                state["out"] = place(me, parts[c], state["out"], model_width, quarter, first)
-
-        for name, c in ORDER:
-            step(name, c)
-        return state["out"]
+        pairs, asked, sides, mixed, edge = {}, {}, {}, {}, {}
+        for c, (first, width) in enumerate(cuts):
+            what = ([key_states, value_states], [pose_depth, band_offsets, control_flags] if c == 0 else [])
+            far = far_group(pack(me, (3, 2), *what, quarter, first, width), 4, edge.get(c - 1))
+            pairs[c] = [*near_group(pack(me, (0, 1), *what, quarter, first, width)), *far]
+            edge[c] = edges(me, pairs[c])
+            sides[c] = along(*edge[c])
+        *near, weight, share = pack_own(me, queries, hint_weight, gain, quarter)
+        near, shares = near_group(near), (weight, share)
+        for c, (first, width) in enumerate(cuts):
+            far = far_group(pack(me, (3, 2), [queries], [], quarter, first, width), 4, edge.get(n + c - 1))
+            asked[c] = [*near, *far]
+        setting = None
+        for c, (first, width) in enumerate(cuts):
+            got = hint_branch(me, pairs[c], asked[c], *sides[c], *shares, setting, spans, frames, first)
+            setting = got[4:] if setting is None else setting
+            mixed[c] = [got[3], got[0], *along(got[1], got[2])]
+        parts = []
+        for c, (first, width) in enumerate(cuts):
+            keys = after(mixed[c][0], mixed[n - 1][1]) if True and c < n - 1 else mixed[c][0]
+            got = base_block(me, asked[c], keys, *mixed[c][1:], setting[1], spans, first)
+            parts.append([*near_group(got[:2]), *far_group(got[:1:-1], 2)])
+        out = None
+        for c, (first, width) in enumerate(cuts):
+            out = place(me, parts[c], out, model_width, quarter, first)
+        return out
 
     return jax.shard_map(
         body,

time: 87.1 us -> 85.4 us (0.980)
  starting transfers between devices: 33.3 us -> 31.8 us
  waiting for transfers between devices: 27.6 us -> 28.6 us
    ppermute x12, starting transfers between devices: 17.9 us -> 13.6 us  [far_group(): got.append(lax.ppermute(part, 'tm', across[k]))]
    ppermute x3 -> x5, starting transfers between devices: 0.55 us -> 3.57 us  [near_group(): return [parts[0], lax.ppermute(parts[1], 'tm', across[1])]]
    ppermute x4, waiting for transfers between devices: 1.65 us -> 3.26 us  [along(): lax.ppermute(start, 'tm', downward)]
    ppermute x4, starting transfers between devices: 3.73 us -> 2.37 us  [along(): lax.ppermute(last, 'tm', upward)]
    ppermute x4, starting transfers between devices: 11.2 us -> 12.2 us  [along(): lax.ppermute(start, 'tm', downward)]
    ppermute x12, waiting for transfers between devices: 26 us -> 25 us  [far_group(): got.append(lax.ppermute(part, 'tm', across[k]))]
    pallas_call x14 -> x15, Pallas kernels: 24.9 us -> 24.1 us  [run(): pl.pallas_call(body, out_shape=list(outs), in_specs=[SMEM] * a + (where i...]
  transfers between devices with their start and end apart: 23 -> 25, of which waited for: 9 -> 11; matrix products, arithmetic and copies ran while one was open for 0% -> 0% of each run, Pallas kernels for 26% -> 26%
where the time goes in v5:
time: 85.4 us; the launch traced here: 84.6 us
  starting transfers between devices  31.8 us (37%)
  waiting for transfers between devices  28.6 us (33%)
  Pallas kernels  24.1 us (28%)
    ppermute x12, waiting for transfers between devices, far_group(): got.append(lax.ppermute(part, 'tm', across[k]))  25 us
    pallas_call x15, Pallas kernels, run(): pl.pallas_call(body, out_shape=list(outs), in_specs=[SMEM] * a + (where i...  24.1 us
    ppermute x12, starting transfers between devices, far_group(): got.append(lax.ppermute(part, 'tm', across[k]))  13.6 us
    ppermute x4, starting transfers between devices, along(): lax.ppermute(start, 'tm', downward)  12.2 us
    ppermute x5, starting transfers between devices, near_group(): return [parts[0], lax.ppermute(parts[1], 'tm', across[1])]  3.57 us
    ppermute x4, waiting for transfers between devices, along(): lax.ppermute(start, 'tm', downward)  3.26 us
    ppermute x4, starting transfers between devices, along(): lax.ppermute(last, 'tm', upward)  2.37 us
  transfers between devices with their start and end apart: 25, of which 11 were waited for; matrix products, arithmetic and copies ran while one was open for 0% of the time, Pallas kernels for 26%

profile of v5, /device:TPU:1, one launch (start us, length us, event | category | flops | bytes accessed | tf_op | source)
XLA Modules:
  0.0 84.6 jit_solution(1934621764074133862)
XLA Ops:
  0.0 1.3 %pack.7 = (bf16[288,640]{1,0:T(8,128)(2,1)S(1)}, bf16[288,640]{1,0:T(8,128)(2,1)S(1)}) custom-call(s32[1]{0:T(128)} %bitcast.refs_0_, bf16[2,64,5120]{2,1,0:T(8,128)(2,1)} %refs_1_.12, bf16[2,64,5120]{2,1,0:T(8,128)(2,1)} %refs_2_.9, bf16[2,64,128]{2,1,0:T(8,128)(2,1)} %refs_3_.3, s32[2,3]{1,0:T(2,128)} %refs_4_.3, s32[2]{0:T(128)} %refs_5_.3), custom_call_target="tpu_custom_call" | custom-call | flops 1 | bytes 3400000 | tf_op jit(solution)/shard_map/pack/pallas_call | solution.py:28
  1.3 2.1 %collective-permute-start.1 = (bf16[288,640]{1,0:T(8,128)(2,1)S(1)}, bf16[288,640]{1,0:T(8,128)(2,1)S(1)}, u32[]{:S(2)}, u32[]{:S(2)}) collective-permute-start(bf16[288,640]{1,0:T(8,128)(2,1)S(1)} %get-tuple-element.59), channel_id=1, source_target_pairs={{0,2},{1,3},{2,0},{3,1},{4,6},{5,7},{6,4},{7,5},{8,10},{9,11},{10,... | collective-permute-start | bytes 1105928 | tf_op jit(solution)/shard_map/ppermute | solution.py:347
  4.0 1.3 %pack.6 = (bf16[288,640]{1,0:T(8,128)(2,1)S(1)}, bf16[288,640]{1,0:T(8,128)(2,1)S(1)}) custom-call(s32[1]{0:T(128)} %bitcast.refs_0_, bf16[2,64,5120]{2,1,0:T(8,128)(2,1)} %refs_1_.12, bf16[2,64,5120]{2,1,0:T(8,128)(2,1)} %refs_2_.9, bf16[2,64,128]{2,1,0:T(8,128)(2,1)} %refs_3_.3, s32[2,3]{1,0:T(2,128)} %refs_4_.3, s32[2]{0:T(128)} %refs_5_.3), custom_call_target="tpu_custom_call" | custom-call | flops 1 | bytes 3400000 | tf_op jit(solution)/shard_map/pack/pallas_call | solution.py:28
  7.0 1.4 %collective-permute-start.6 = (bf16[256,640]{1,0:T(8,128)(2,1)S(1)}, bf16[256,640]{1,0:T(8,128)(2,1)S(1)}, u32[]{:S(2)}, u32[]{:S(2)}) collective-permute-start(bf16[256,640]{1,0:T(8,128)(2,1)S(1)} %get-tuple-element.68), channel_id=1, source_target_pairs={{0,2},{1,3},{2,0},{3,1},{4,6},{5,7},{6,4},{7,5},{8,10},{9,11},{10,... | collective-permute-start | bytes 983048 | tf_op jit(solution)/shard_map/ppermute | solution.py:347
  11.7 9.3 %collective-permute-done.2.refs_4_ = bf16[288,640]{1,0:T(8,128)(2,1)S(1)} collective-permute-done((bf16[288,640]{1,0:T(8,128)(2,1)S(1)}, bf16[288,640]{1,0:T(8,128)(2,1)S(1)}, u32[]{:S(2)}, u32[]{:S(2)}) %collective-permute-start.2) | collective-permute-done | bytes 368672 | tf_op jit(solution)/shard_map/ppermute | solution.py:347
  21.1 3.9 %collective-permute-start.10 = (bf16[288,640]{1,0:T(8,128)(2,1)S(1)}, bf16[288,640]{1,0:T(8,128)(2,1)S(1)}, u32[]{:S(2)}, u32[]{:S(2)}) collective-permute-start(bf16[288,640]{1,0:T(8,128)(2,1)S(1)} %get-tuple-element.71), channel_id=1, source_target_pairs={{0,12},{1,13},{2,14},{3,15},{4,0},{5,1},{6,2},{7,3},{8,4},{9,5},{1... | collective-permute-start | bytes 1105928 | tf_op jit(solution)/shard_map/ppermute | solution.py:357
  25.1 1.3 %pack_own.1 = (bf16[128,1280]{1,0:T(8,128)(2,1)S(1)}, bf16[128,1280]{1,0:T(8,128)(2,1)S(1)}, bf16[128,1280]{1,0:T(8,128)(2,1)S(1)}, f32[1,1280]{1,0:T(1,128)S(1)}) custom-call(s32[1]{0:T(128)} %bitcast.refs_0_, bf16[2,64,5120]{2,1,0:T(8,128)(2,1)} %refs_1_.13, bf16[128,5120]{1,0:T(8,128)(2,1)} %refs_2_.7, f32[1,5120]{1,0:T(1,128)} %bitcast.2), custom_call_target="tpu_custom_call" | custom-call | flops 1 | bytes 3400000 | tf_op jit(solution)/shard_map/pack_own/pallas_call | solution.py:28
  26.5 1.6 %collective-permute-start.3 = (bf16[128,1280]{1,0:T(8,128)(2,1)S(1)}, bf16[128,1280]{1,0:T(8,128)(2,1)S(1)}, u32[]{:S(2)}, u32[]{:S(2)}) collective-permute-start(bf16[128,1280]{1,0:T(8,128)(2,1)S(1)} %get-tuple-element.62), channel_id=1, source_target_pairs={{0,1},{1,0},{2,3},{3,2},{4,5},{5,4},{6,7},{7,6},{8,9},{9,8},{10,11... | collective-permute-start | bytes 983048 | tf_op jit(solution)/shard_map/ppermute | solution.py:353
  30.2 5.1 %collective-permute-done.7.refs_4_.refs_5_ = bf16[256,640]{1,0:T(8,128)(2,1)S(1)} collective-permute-done((bf16[256,640]{1,0:T(8,128)(2,1)S(1)}, bf16[256,640]{1,0:T(8,128)(2,1)S(1)}, u32[]{:S(2)}, u32[]{:S(2)}) %collective-permute-start.7) | collective-permute-done | bytes 327712 | tf_op jit(solution)/shard_map/ppermute | solution.py:347
  35.3 2.0 %collective-permute-start.13 = (bf16[256,640]{1,0:T(8,128)(2,1)S(1)}, bf16[256,640]{1,0:T(8,128)(2,1)S(1)}, u32[]{:S(2)}, u32[]{:S(2)}) collective-permute-start(bf16[256,640]{1,0:T(8,128)(2,1)S(1)} %get-tuple-element.73), channel_id=1, source_target_pairs={{0,4},{1,5},{2,6},{3,7},{4,8},{5,9},{6,10},{7,11},{8,12},{9,13},{1... | collective-permute-start | bytes 983048 | tf_op jit(solution)/shard_map/ppermute | solution.py:357
  37.3 2.1 %collective-permute-start.14 = (bf16[256,640]{1,0:T(8,128)(2,1)S(1)}, bf16[256,640]{1,0:T(8,128)(2,1)S(1)}, u32[]{:S(2)}, u32[]{:S(2)}) collective-permute-start(bf16[256,640]{1,0:T(8,128)(2,1)S(1)} %get-tuple-element.74), channel_id=1, source_target_pairs={{0,12},{1,13},{2,14},{3,15},{4,0},{5,1},{6,2},{7,3},{8,4},{9,5},{1... | collective-permute-start | bytes 983048 | tf_op jit(solution)/shard_map/ppermute | solution.py:357
  42.0 1.8 %collective-permute-start.12 = (bf16[128,640]{1,0:T(8,128)(2,1)S(1)}, bf16[128,640]{1,0:T(8,128)(2,1)S(1)}, u32[]{:S(2)}, u32[]{:S(2)}) collective-permute-start(bf16[128,640]{1,0:T(8,128)(2,1)S(1)} %get-tuple-element.82), channel_id=1, source_target_pairs={{0,3},{1,2},{2,1},{3,0},{4,7},{5,6},{6,5},{7,4},{8,11},{9,10},{10,... | collective-permute-start | bytes 491528 | tf_op jit(solution)/shard_map/ppermute | solution.py:347
  43.8 2.3 %collective-permute-done.8.refs_8_.refs_5_ = bf16[128,640]{1,0:T(8,128)(2,1)S(1)} collective-permute-done((bf16[128,640]{1,0:T(8,128)(2,1)S(1)}, bf16[128,640]{1,0:T(8,128)(2,1)S(1)}, u32[]{:S(2)}, u32[]{:S(2)}) %collective-permute-start.8) | collective-permute-done | bytes 163872 | tf_op jit(solution)/shard_map/ppermute | solution.py:347
  46.2 3.9 %hint_branch.2 = (bf16[8,64,640]{2,1,0:T(8,128)(2,1)S(1)}, bf16[2,64,640]{2,1,0:T(8,128)(2,1)S(1)}, bf16[2,64,640]{2,1,0:T(8,128)(2,1)S(1)}, bf16[12,64,640]{2,1...) custom-call(s32[1]{0:T(128)} %bitcast.refs_0_, ...), custom_call_target="tpu_custom_call" | custom-call | flops 1 | bytes 15300000 | tf_op jit(solution)/shard_map/hint_branch/pallas_call | solution.py:28
  50.2 3.2 %collective-permute-start.19 = (bf16[2,64,640]{2,1,0:T(8,128)(2,1)S(1)}, bf16[2,64,640]{2,1,0:T(8,128)(2,1)S(1)}, u32[]{:S(2)}, u32[]{:S(2)}) collective-permute-start(bf16[2,64,640]{2,1,0:T(8,128)(2,1)S(1)} %get-tuple-element.99), channel_id=1, source_target_pairs={{0,12},{1,13},{2,14},{3,15},{4,0},{5,1},{6,2},{7,3},{8,4},{9,5},{1... | collective-permute-start | bytes 491528 | tf_op jit(solution)/shard_map/ppermute | solution.py:357
  53.4 2.9 %collective-permute-done.14.refs_11_ = bf16[256,640]{1,0:T(8,128)(2,1)S(1)} collective-permute-done((bf16[256,640]{1,0:T(8,128)(2,1)S(1)}, bf16[256,640]{1,0:T(8,128)(2,1)S(1)}, u32[]{:S(2)}, u32[]{:S(2)}) %collective-permute-start.14) | collective-permute-done | bytes 327712 | tf_op jit(solution)/shard_map/ppermute | solution.py:357
  56.4 3.9 %hint_branch.3 = (bf16[8,64,640]{2,1,0:T(8,128)(2,1)S(1)}, bf16[2,64,640]{2,1,0:T(8,128)(2,1)S(1)}, bf16[2,64,640]{2,1,0:T(8,128)(2,1)S(1)}, bf16[12,64,640]{2,1,0:T(8,128)(2,1)S(1)}) custom-call(s32[1]{0:T(128)} %bitcast.refs_0_, s32[4,8,128]{2,1,0:T(8,128)S(1)} %get-tuple-element.78.refs_1_, bf16[256,640]{1,0:T(8,128)(2,1)S(1)} %get-tuple-element.66.refs_1_.refs_2_, ...), custom_call_target="tpu_custom_call" | custom-call | flops 1 | bytes 15300000 | tf_op jit(solution)/shard_map/hint_branch/pallas_call | solution.py:28
  60.6 3.0 %collective-permute-start.16 = (bf16[2,64,640]{2,1,0:T(8,128)(2,1)S(1)}, bf16[2,64,640]{2,1,0:T(8,128)(2,1)S(1)}, u32[]{:S(2)}, u32[]{:S(2)}) collective-permute-start(bf16[2,64,640]{2,1,0:T(8,128)(2,1)S(1)} %get-tuple-element.89), channel_id=1, source_target_pairs={{0,12},{1,13},{2,14},{3,15},{4,0},{5,1},{6,2},{7,3},{8,4},{9,5},{1... | collective-permute-start | bytes 491528 | tf_op jit(solution)/shard_map/ppermute | solution.py:357
  63.5 3.0 %base_block.3 = (bf16[2,64,640]{2,1,0:T(8,128)(2,1)S(1)}, bf16[2,64,640]{2,1,0:T(8,128)(2,1)S(1)}, bf16[2,64,640]{2,1,0:T(8,128)(2,1)S(1)}, bf16[2,64,640]{2,1,0:T(8,128)(2,1)S(1)}) custom-call(s32[1]{0:T(128)} %bitcast.refs_0_, s32[4,8,128]{2,1,0:T(8,128)S(1)} %get-tuple-element.78.refs_1_, bf16[128,1280]{1,0:T(8,128)(2,1)S(1)} %get-tuple-element.61.refs_5_.refs_6_.refs_2_, ...), custom_call_target="tpu_custom_call" | custom-call | flops 1 | bytes 11900000 | tf_op jit(solution)/shard_map/base_block/pallas_call | solution.py:28
  66.6 1.7 %collective-permute-start.22 = (bf16[2,64,640]{2,1,0:T(8,128)(2,1)S(1)}, bf16[2,64,640]{2,1,0:T(8,128)(2,1)S(1)}, u32[]{:S(2)}, u32[]{:S(2)}) collective-permute-start(bf16[2,64,640]{2,1,0:T(8,128)(2,1)S(1)} %get-tuple-element.105), channel_id=1, source_target_pairs={{0,3},{1,2},{2,1},{3,0},{4,7},{5,6},{6,5},{7,4},{8,11},{9,10},{10,... | collective-permute-start | bytes 491528 | tf_op jit(solution)/shard_map/ppermute | solution.py:347
  69.3 3.0 %base_block.2 = (bf16[2,64,640]{2,1,0:T(8,128)(2,1)S(1)}, bf16[2,64,640]{2,1,0:T(8,128)(2,1)S(1)}, bf16[2,64,640]{2,1,0:T(8,128)(2,1)S(1)}, bf16[2,64,640]{2,1,0:T(8,128)(2,1)S(1)}) custom-call(s32[1]{0:T(128)} %bitcast.refs_0_, s32[4,8,128]{2,1,0:T(8,128)S(1)} %get-tuple-element.78.refs_1_, bf16[128,1280]{1,0:T(8,128)(2,1)S(1)} %get-tuple-element.61.refs_5_.refs_6_.refs_2_, ...), custom_call_target="tpu_custom_call" | custom-call | flops 1 | bytes 11900000 | tf_op jit(solution)/shard_map/base_block/pallas_call | solution.py:28
  73.1 1.7 %collective-permute-start.23 = (bf16[2,64,640]{2,1,0:T(8,128)(2,1)S(1)}, bf16[2,64,640]{2,1,0:T(8,128)(2,1)S(1)}, u32[]{:S(2)}, u32[]{:S(2)}) collective-permute-start(bf16[2,64,640]{2,1,0:T(8,128)(2,1)S(1)} %get-tuple-element.106), channel_id=1, source_target_pairs={{0,3},{1,2},{2,1},{3,0},{4,7},{5,6},{6,5},{7,4},{8,11},{9,10},{10,... | collective-permute-start | bytes 491528 | tf_op jit(solution)/shard_map/ppermute | solution.py:347
  74.8 2.2 %collective-permute-done.20.refs_3_ = bf16[2,64,640]{2,1,0:T(8,128)(2,1)S(1)} collective-permute-done((bf16[2,64,640]{2,1,0:T(8,128)(2,1)S(1)}, bf16[2,64,640]{2,1,0:T(8,128)(2,1)S(1)}, u32[]{:S(2)}, u32[]{:S(2)}) %collective-permute-start.20) | collective-permute-done | bytes 163872 | tf_op jit(solution)/shard_map/ppermute | solution.py:347
  80.1 3.6 %collective-permute-done.21.refs_3_ = bf16[2,64,640]{2,1,0:T(8,128)(2,1)S(1)} collective-permute-done((bf16[2,64,640]{2,1,0:T(8,128)(2,1)S(1)}, bf16[2,64,640]{2,1,0:T(8,128)(2,1)S(1)}, u32[]{:S(2)}, u32[]{:S(2)}) %collective-permute-start.21) | collective-permute-done | bytes 163872 | tf_op jit(solution)/shard_map/ppermute | solution.py:347
  (41 shorter events, 16.9 us)
Async XLA Ops:
  1.3 10.4 %collective-permute-start.1 = (bf16[288,640]{1,0:T(8,128)(2,1)S(1)}, bf16[288,640]{1,0:T(8,128)(2,1)S(1)}, u32[]{:S(2)}, u32[]{:S(2)}) collective-permute-start(bf16[288,640]{1,0:T(8,128)(2,1)S(1)} %get-tuple-element.59), channel_id=1, source_target_pairs={{0,2},{1,3},{2,0},{3,1},{4,6},{5,7},{6,4},{7,5},{8,10},{9,11},{10,... | collective-permute-start | bytes 1105928 | tf_op jit(solution)/shard_map/ppermute | solution.py:347
  3.4 17.6 %collective-permute-start.2 = (bf16[288,640]{1,0:T(8,128)(2,1)S(1)}, bf16[288,640]{1,0:T(8,128)(2,1)S(1)}, u32[]{:S(2)}, u32[]{:S(2)}) collective-permute-start(bf16[288,640]{1,0:T(8,128)(2,1)S(1)} %get-tuple-element.60), channel_id=1, source_target_pairs={{0,3},{1,2},{2,1},{3,0},{4,7},{5,6},{6,5},{7,4},{8,11},{9,10},{10,... | collective-permute-start | bytes 1105928 | tf_op jit(solution)/shard_map/ppermute | solution.py:347
  5.3 15.7 %collective-permute-start = (bf16[288,640]{1,0:T(8,128)(2,1)S(1)}, bf16[288,640]{1,0:T(8,128)(2,1)S(1)}, u32[]{:S(2)}, u32[]{:S(2)}) collective-permute-start(bf16[288,640]{1,0:T(8,128)(2,1)S(1)} %get-tuple-element.58), channel_id=1, source_target_pairs={{0,1},{1,0},{2,3},{3,2},{4,5},{5,4},{6,7},{7,6},{8,9},{9,8},{10,11... | collective-permute-start | bytes 1105928 | tf_op jit(solution)/shard_map/ppermute | solution.py:353
  7.0 21.1 %collective-permute-start.6 = (bf16[256,640]{1,0:T(8,128)(2,1)S(1)}, bf16[256,640]{1,0:T(8,128)(2,1)S(1)}, u32[]{:S(2)}, u32[]{:S(2)}) collective-permute-start(bf16[256,640]{1,0:T(8,128)(2,1)S(1)} %get-tuple-element.68), channel_id=1, source_target_pairs={{0,2},{1,3},{2,0},{3,1},{4,6},{5,7},{6,4},{7,5},{8,10},{9,11},{10,... | collective-permute-start | bytes 983048 | tf_op jit(solution)/shard_map/ppermute | solution.py:347
  9.6 19.5 %collective-permute-start.5 = (bf16[256,640]{1,0:T(8,128)(2,1)S(1)}, bf16[256,640]{1,0:T(8,128)(2,1)S(1)}, u32[]{:S(2)}, u32[]{:S(2)}) collective-permute-start(bf16[256,640]{1,0:T(8,128)(2,1)S(1)} %get-tuple-element.67), channel_id=1, source_target_pairs={{0,1},{1,0},{2,3},{3,2},{4,5},{5,4},{6,7},{7,6},{8,9},{9,8},{10,11... | collective-permute-start | bytes 983048 | tf_op jit(solution)/shard_map/ppermute | solution.py:353
  21.1 19.7 %collective-permute-start.10 = (bf16[288,640]{1,0:T(8,128)(2,1)S(1)}, bf16[288,640]{1,0:T(8,128)(2,1)S(1)}, u32[]{:S(2)}, u32[]{:S(2)}) collective-permute-start(bf16[288,640]{1,0:T(8,128)(2,1)S(1)} %get-tuple-element.71), channel_id=1, source_target_pairs={{0,12},{1,13},{2,14},{3,15},{4,0},{5,1},{6,2},{7,3},{8,4},{9,5},{1... | collective-permute-start | bytes 1105928 | tf_op jit(solution)/shard_map/ppermute | solution.py:357
  25.0 10.3 %collective-permute-start.7 = (bf16[256,640]{1,0:T(8,128)(2,1)S(1)}, bf16[256,640]{1,0:T(8,128)(2,1)S(1)}, u32[]{:S(2)}, u32[]{:S(2)}) collective-permute-start(bf16[256,640]{1,0:T(8,128)(2,1)S(1)} %get-tuple-element.72), channel_id=1, source_target_pairs={{0,3},{1,2},{2,1},{3,0},{4,7},{5,6},{6,5},{7,4},{8,11},{9,10},{10,... | collective-permute-start | bytes 983048 | tf_op jit(solution)/shard_map/ppermute | solution.py:347
  26.5 10.8 %collective-permute-start.3 = (bf16[128,1280]{1,0:T(8,128)(2,1)S(1)}, bf16[128,1280]{1,0:T(8,128)(2,1)S(1)}, u32[]{:S(2)}, u32[]{:S(2)}) collective-permute-start(bf16[128,1280]{1,0:T(8,128)(2,1)S(1)} %get-tuple-element.62), channel_id=1, source_target_pairs={{0,1},{1,0},{2,3},{3,2},{4,5},{5,4},{6,7},{7,6},{8,9},{9,8},{10,11... | collective-permute-start | bytes 983048 | tf_op jit(solution)/shard_map/ppermute | solution.py:353
  28.1 14.0 %collective-permute-start.9 = (bf16[288,640]{1,0:T(8,128)(2,1)S(1)}, bf16[288,640]{1,0:T(8,128)(2,1)S(1)}, u32[]{:S(2)}, u32[]{:S(2)}) collective-permute-start(bf16[288,640]{1,0:T(8,128)(2,1)S(1)} %get-tuple-element.70), channel_id=1, source_target_pairs={{0,4},{1,5},{2,6},{3,7},{4,8},{5,9},{6,10},{7,11},{8,12},{9,13},{1... | collective-permute-start | bytes 1105928 | tf_op jit(solution)/shard_map/ppermute | solution.py:357
  29.1 10.3 %collective-permute-start.4 = (bf16[128,640]{1,0:T(8,128)(2,1)S(1)}, bf16[128,640]{1,0:T(8,128)(2,1)S(1)}, u32[]{:S(2)}, u32[]{:S(2)}) collective-permute-start(bf16[128,640]{1,0:T(8,128)(2,1)S(1)} %get-tuple-element.64), channel_id=1, source_target_pairs={{0,2},{1,3},{2,0},{3,1},{4,6},{5,7},{6,4},{7,5},{8,10},{9,11},{10,... | collective-permute-start | bytes 491528 | tf_op jit(solution)/shard_map/ppermute | solution.py:347
  35.3 18.1 %collective-permute-start.13 = (bf16[256,640]{1,0:T(8,128)(2,1)S(1)}, bf16[256,640]{1,0:T(8,128)(2,1)S(1)}, u32[]{:S(2)}, u32[]{:S(2)}) collective-permute-start(bf16[256,640]{1,0:T(8,128)(2,1)S(1)} %get-tuple-element.73), channel_id=1, source_target_pairs={{0,4},{1,5},{2,6},{3,7},{4,8},{5,9},{6,10},{7,11},{8,12},{9,13},{1... | collective-permute-start | bytes 983048 | tf_op jit(solution)/shard_map/ppermute | solution.py:357
  37.3 19.1 %collective-permute-start.14 = (bf16[256,640]{1,0:T(8,128)(2,1)S(1)}, bf16[256,640]{1,0:T(8,128)(2,1)S(1)}, u32[]{:S(2)}, u32[]{:S(2)}) collective-permute-start(bf16[256,640]{1,0:T(8,128)(2,1)S(1)} %get-tuple-element.74), channel_id=1, source_target_pairs={{0,12},{1,13},{2,14},{3,15},{4,0},{5,1},{6,2},{7,3},{8,4},{9,5},{1... | collective-permute-start | bytes 983048 | tf_op jit(solution)/shard_map/ppermute | solution.py:357
  39.4 6.8 %collective-permute-start.8 = (bf16[128,640]{1,0:T(8,128)(2,1)S(1)}, bf16[128,640]{1,0:T(8,128)(2,1)S(1)}, u32[]{:S(2)}, u32[]{:S(2)}) collective-permute-start(bf16[128,640]{1,0:T(8,128)(2,1)S(1)} %get-tuple-element.75), channel_id=1, source_target_pairs={{0,3},{1,2},{2,1},{3,0},{4,7},{5,6},{6,5},{7,4},{8,11},{9,10},{10,... | collective-permute-start | bytes 491528 | tf_op jit(solution)/shard_map/ppermute | solution.py:347
  40.8 9.4 %collective-permute-start.11 = (bf16[128,640]{1,0:T(8,128)(2,1)S(1)}, bf16[128,640]{1,0:T(8,128)(2,1)S(1)}, u32[]{:S(2)}, u32[]{:S(2)}) collective-permute-start(bf16[128,640]{1,0:T(8,128)(2,1)S(1)} %get-tuple-element.80), channel_id=1, source_target_pairs={{0,2},{1,3},{2,0},{3,1},{4,6},{5,7},{6,4},{7,5},{8,10},{9,11},{10,... | collective-permute-start | bytes 491528 | tf_op jit(solution)/shard_map/ppermute | solution.py:347
  42.0 11.4 %collective-permute-start.12 = (bf16[128,640]{1,0:T(8,128)(2,1)S(1)}, bf16[128,640]{1,0:T(8,128)(2,1)S(1)}, u32[]{:S(2)}, u32[]{:S(2)}) collective-permute-start(bf16[128,640]{1,0:T(8,128)(2,1)S(1)} %get-tuple-element.82), channel_id=1, source_target_pairs={{0,3},{1,2},{2,1},{3,0},{4,7},{5,6},{6,5},{7,4},{8,11},{9,10},{10,... | collective-permute-start | bytes 491528 | tf_op jit(solution)/shard_map/ppermute | solution.py:347
  50.1 13.4 %collective-permute-start.18 = (bf16[2,64,640]{2,1,0:T(8,128)(2,1)S(1)}, bf16[2,64,640]{2,1,0:T(8,128)(2,1)S(1)}, u32[]{:S(2)}, u32[]{:S(2)}) collective-permute-start(bf16[2,64,640]{2,1,0:T(8,128)(2,1)S(1)} %get-tuple-element.98), channel_id=1, source_target_pairs={{0,4},{1,5},{2,6},{3,7},{4,8},{5,9},{6,10},{7,11},{8,12},{9,13},{1... | collective-permute-start | bytes 491528 | tf_op jit(solution)/shard_map/ppermute | solution.py:357
  50.2 13.4 %collective-permute-start.19 = (bf16[2,64,640]{2,1,0:T(8,128)(2,1)S(1)}, bf16[2,64,640]{2,1,0:T(8,128)(2,1)S(1)}, u32[]{:S(2)}, u32[]{:S(2)}) collective-permute-start(bf16[2,64,640]{2,1,0:T(8,128)(2,1)S(1)} %get-tuple-element.99), channel_id=1, source_target_pairs={{0,12},{1,13},{2,14},{3,15},{4,0},{5,1},{6,2},{7,3},{8,4},{9,5},{1... | collective-permute-start | bytes 491528 | tf_op jit(solution)/shard_map/ppermute | solution.py:357
  60.2 8.8 %collective-permute-start.15 = (bf16[2,64,640]{2,1,0:T(8,128)(2,1)S(1)}, bf16[2,64,640]{2,1,0:T(8,128)(2,1)S(1)}, u32[]{:S(2)}, u32[]{:S(2)}) collective-permute-start(bf16[2,64,640]{2,1,0:T(8,128)(2,1)S(1)} %get-tuple-element.88), channel_id=1, source_target_pairs={{0,4},{1,5},{2,6},{3,7},{4,8},{5,9},{6,10},{7,11},{8,12},{9,13},{1... | collective-permute-start | bytes 491528 | tf_op jit(solution)/shard_map/ppermute | solution.py:357
  60.6 8.8 %collective-permute-start.16 = (bf16[2,64,640]{2,1,0:T(8,128)(2,1)S(1)}, bf16[2,64,640]{2,1,0:T(8,128)(2,1)S(1)}, u32[]{:S(2)}, u32[]{:S(2)}) collective-permute-start(bf16[2,64,640]{2,1,0:T(8,128)(2,1)S(1)} %get-tuple-element.89), channel_id=1, source_target_pairs={{0,12},{1,13},{2,14},{3,15},{4,0},{5,1},{6,2},{7,3},{8,4},{9,5},{1... | collective-permute-start | bytes 491528 | tf_op jit(solution)/shard_map/ppermute | solution.py:357
  66.6 6.5 %collective-permute-start.22 = (bf16[2,64,640]{2,1,0:T(8,128)(2,1)S(1)}, bf16[2,64,640]{2,1,0:T(8,128)(2,1)S(1)}, u32[]{:S(2)}, u32[]{:S(2)}) collective-permute-start(bf16[2,64,640]{2,1,0:T(8,128)(2,1)S(1)} %get-tuple-element.105), channel_id=1, source_target_pairs={{0,3},{1,2},{2,1},{3,0},{4,7},{5,6},{6,5},{7,4},{8,11},{9,10},{10,... | collective-permute-start | bytes 491528 | tf_op jit(solution)/shard_map/ppermute | solution.py:347
  68.3 8.7 %collective-permute-start.20 = (bf16[2,64,640]{2,1,0:T(8,128)(2,1)S(1)}, bf16[2,64,640]{2,1,0:T(8,128)(2,1)S(1)}, u32[]{:S(2)}, u32[]{:S(2)}) collective-permute-start(bf16[2,64,640]{2,1,0:T(8,128)(2,1)S(1)} %get-tuple-element.101), channel_id=1, source_target_pairs={{0,2},{1,3},{2,0},{3,1},{4,6},{5,7},{6,4},{7,5},{8,10},{9,11},{10,... | collective-permute-start | bytes 491528 | tf_op jit(solution)/shard_map/ppermute | solution.py:347
  69.0 9.7 %collective-permute-start.24 = (bf16[2,64,640]{2,1,0:T(8,128)(2,1)S(1)}, bf16[2,64,640]{2,1,0:T(8,128)(2,1)S(1)}, u32[]{:S(2)}, u32[]{:S(2)}) collective-permute-start(bf16[2,64,640]{2,1,0:T(8,128)(2,1)S(1)} %get-tuple-element.108), channel_id=1, source_target_pairs={{0,1},{1,0},{2,3},{3,2},{4,5},{5,4},{6,7},{7,6},{8,9},{9,8},{10,11... | collective-permute-start | bytes 491528 | tf_op jit(solution)/shard_map/ppermute | solution.py:353
  73.1 7.0 %collective-permute-start.23 = (bf16[2,64,640]{2,1,0:T(8,128)(2,1)S(1)}, bf16[2,64,640]{2,1,0:T(8,128)(2,1)S(1)}, u32[]{:S(2)}, u32[]{:S(2)}) collective-permute-start(bf16[2,64,640]{2,1,0:T(8,128)(2,1)S(1)} %get-tuple-element.106), channel_id=1, source_target_pairs={{0,3},{1,2},{2,1},{3,0},{4,7},{5,6},{6,5},{7,4},{8,11},{9,10},{10,... | collective-permute-start | bytes 491528 | tf_op jit(solution)/shard_map/ppermute | solution.py:347
  77.0 6.8 %collective-permute-start.21 = (bf16[2,64,640]{2,1,0:T(8,128)(2,1)S(1)}, bf16[2,64,640]{2,1,0:T(8,128)(2,1)S(1)}, u32[]{:S(2)}, u32[]{:S(2)}) collective-permute-start(bf16[2,64,640]{2,1,0:T(8,128)(2,1)S(1)} %get-tuple-element.102), channel_id=1, source_target_pairs={{0,2},{1,3},{2,0},{3,1},{4,6},{5,7},{6,4},{7,5},{8,10},{9,11},{10,... | collective-permute-start | bytes 491528 | tf_op jit(solution)/shard_map/ppermute | solution.py:347
  (1 other events, 5.8 us)

commit v6 on v5

--- a/solution.py
+++ b/solution.py
@@ -363,14 +363,14 @@
         pairs, asked, sides, mixed, edge = {}, {}, {}, {}, {}
         for c, (first, width) in enumerate(cuts):
             what = ([key_states, value_states], [pose_depth, band_offsets, control_flags] if c == 0 else [])
-            far = far_group(pack(me, (3, 2), *what, quarter, first, width), 4, edge.get(c - 1))
+            far = far_group(pack(me, (3, 2), *what, quarter, first, width), 3, edge.get(c - 2))
             pairs[c] = [*near_group(pack(me, (0, 1), *what, quarter, first, width)), *far]
             edge[c] = edges(me, pairs[c])
             sides[c] = along(*edge[c])
         *near, weight, share = pack_own(me, queries, hint_weight, gain, quarter)
         near, shares = near_group(near), (weight, share)
         for c, (first, width) in enumerate(cuts):
-            far = far_group(pack(me, (3, 2), [queries], [], quarter, first, width), 4, edge.get(n + c - 1))
+            far = far_group(pack(me, (3, 2), [queries], [], quarter, first, width), 3, sides[0] if c == n - 1 else edge.get(n + c - 2))
             asked[c] = [*near, *far]
         setting = None
         for c, (first, width) in enumerate(cuts):

time: 85.4 us -> 85 us (level)
  starting transfers between devices: 31.8 us -> 28.6 us
  waiting for transfers between devices: 28.6 us -> 31.3 us
    ppermute x12, waiting for transfers between devices: 25 us -> 30 us  [far_group(): got.append(lax.ppermute(part, 'tm', across[k]))]
    ppermute x5, starting transfers between devices: 3.57 us -> 0.57 us  [near_group(): return [parts[0], lax.ppermute(parts[1], 'tm', across[1])]]
    ppermute x4, waiting for transfers between devices: 3.26 us -> 1.22 us  [along(): lax.ppermute(start, 'tm', downward)]
    ppermute x4, starting transfers between devices: 12.2 us -> 10.7 us  [along(): lax.ppermute(start, 'tm', downward)]
where the time goes in v6:
time: 85 us; the launch traced here: 84.2 us
  waiting for transfers between devices  31.3 us (37%)
  starting transfers between devices  28.6 us (34%)
  Pallas kernels  24.1 us (28%)
    ppermute x12, waiting for transfers between devices, far_group(): got.append(lax.ppermute(part, 'tm', across[k]))  30 us
    pallas_call x15, Pallas kernels, run(): pl.pallas_call(body, out_shape=list(outs), in_specs=[SMEM] * a + (where i...  24.1 us
    ppermute x12, starting transfers between devices, far_group(): got.append(lax.ppermute(part, 'tm', across[k]))  14.4 us
    ppermute x4, starting transfers between devices, along(): lax.ppermute(start, 'tm', downward)  10.7 us
    ppermute x4, starting transfers between devices, along(): lax.ppermute(last, 'tm', upward)  2.98 us
  transfers between devices with their start and end apart: 25, of which 11 were waited for; matrix products, arithmetic and copies ran while one was open for 0% of the time, Pallas kernels for 26%

profile of v6, /device:TPU:1, one launch (start us, length us, event | category | flops | bytes accessed | tf_op | source)
XLA Modules:
  0.0 84.2 jit_solution(4800481262834405769)
XLA Ops:
  0.0 1.3 %pack.7 = (bf16[288,640]{1,0:T(8,128)(2,1)S(1)}, bf16[288,640]{1,0:T(8,128)(2,1)S(1)}) custom-call(s32[1]{0:T(128)} %bitcast.refs_0_, bf16[2,64,5120]{2,1,0:T(8,128)(2,1)} %refs_1_.13, bf16[2,64,5120]{2,1,0:T(8,128)(2,1)} %refs_2_.9, bf16[2,64,128]{2,1,0:T(8,128)(2,1)} %refs_3_.3, s32[2,3]{1,0:T(2,128)} %refs_4_.3, s32[2]{0:T(128)} %refs_5_.3), custom_call_target="tpu_custom_call" | custom-call | flops 1 | bytes 3400000 | tf_op jit(solution)/shard_map/pack/pallas_call | solution.py:28
  1.3 2.1 %collective-permute-start.1 = (bf16[288,640]{1,0:T(8,128)(2,1)S(1)}, bf16[288,640]{1,0:T(8,128)(2,1)S(1)}, u32[]{:S(2)}, u32[]{:S(2)}) collective-permute-start(bf16[288,640]{1,0:T(8,128)(2,1)S(1)} %get-tuple-element.59), channel_id=1, source_target_pairs={{0,2},{1,3},{2,0},{3,1},{4,6},{5,7},{6,4},{7,5},{8,10},{9,11},{10,... | collective-permute-start | bytes 1105928 | tf_op jit(solution)/shard_map/ppermute | solution.py:347
  4.0 1.3 %pack.6 = (bf16[288,640]{1,0:T(8,128)(2,1)S(1)}, bf16[288,640]{1,0:T(8,128)(2,1)S(1)}) custom-call(s32[1]{0:T(128)} %bitcast.refs_0_, bf16[2,64,5120]{2,1,0:T(8,128)(2,1)} %refs_1_.13, bf16[2,64,5120]{2,1,0:T(8,128)(2,1)} %refs_2_.9, bf16[2,64,128]{2,1,0:T(8,128)(2,1)} %refs_3_.3, s32[2,3]{1,0:T(2,128)} %refs_4_.3, s32[2]{0:T(128)} %refs_5_.3), custom_call_target="tpu_custom_call" | custom-call | flops 1 | bytes 3400000 | tf_op jit(solution)/shard_map/pack/pallas_call | solution.py:28
  7.0 1.8 %collective-permute-start.4 = (bf16[256,640]{1,0:T(8,128)(2,1)S(1)}, bf16[256,640]{1,0:T(8,128)(2,1)S(1)}, u32[]{:S(2)}, u32[]{:S(2)}) collective-permute-start(bf16[256,640]{1,0:T(8,128)(2,1)S(1)} %get-tuple-element.64), channel_id=1, source_target_pairs={{0,3},{1,2},{2,1},{3,0},{4,7},{5,6},{6,5},{7,4},{8,11},{9,10},{10,... | collective-permute-start | bytes 983048 | tf_op jit(solution)/shard_map/ppermute | solution.py:347
  10.1 1.6 %collective-permute-done.1.refs_3_ = bf16[288,640]{1,0:T(8,128)(2,1)S(1)} collective-permute-done((bf16[288,640]{1,0:T(8,128)(2,1)S(1)}, bf16[288,640]{1,0:T(8,128)(2,1)S(1)}, u32[]{:S(2)}, u32[]{:S(2)}) %collective-permute-start.1) | collective-permute-done | bytes 368672 | tf_op jit(solution)/shard_map/ppermute | solution.py:347
  11.7 9.6 %collective-permute-done.2.refs_4_ = bf16[288,640]{1,0:T(8,128)(2,1)S(1)} collective-permute-done((bf16[288,640]{1,0:T(8,128)(2,1)S(1)}, bf16[288,640]{1,0:T(8,128)(2,1)S(1)}, u32[]{:S(2)}, u32[]{:S(2)}) %collective-permute-start.2) | collective-permute-done | bytes 368672 | tf_op jit(solution)/shard_map/ppermute | solution.py:347
  21.4 1.9 %collective-permute-start.7 = (bf16[288,640]{1,0:T(8,128)(2,1)S(1)}, bf16[288,640]{1,0:T(8,128)(2,1)S(1)}, u32[]{:S(2)}, u32[]{:S(2)}) collective-permute-start(bf16[288,640]{1,0:T(8,128)(2,1)S(1)} %get-tuple-element.67), channel_id=1, source_target_pairs={{0,4},{1,5},{2,6},{3,7},{4,8},{5,9},{6,10},{7,11},{8,12},{9,13},{1... | collective-permute-start | bytes 1105928 | tf_op jit(solution)/shard_map/ppermute | solution.py:357
  23.3 2.1 %collective-permute-start.8 = (bf16[288,640]{1,0:T(8,128)(2,1)S(1)}, bf16[288,640]{1,0:T(8,128)(2,1)S(1)}, u32[]{:S(2)}, u32[]{:S(2)}) collective-permute-start(bf16[288,640]{1,0:T(8,128)(2,1)S(1)} %get-tuple-element.68), channel_id=1, source_target_pairs={{0,12},{1,13},{2,14},{3,15},{4,0},{5,1},{6,2},{7,3},{8,4},{9,5},{1... | collective-permute-start | bytes 1105928 | tf_op jit(solution)/shard_map/ppermute | solution.py:357
  27.7 1.4 %pack_own.1 = (bf16[128,1280]{1,0:T(8,128)(2,1)S(1)}, bf16[128,1280]{1,0:T(8,128)(2,1)S(1)}, bf16[128,1280]{1,0:T(8,128)(2,1)S(1)}, f32[1,1280]{1,0:T(1,128)S(1)}) custom-call(s32[1]{0:T(128)} %bitcast.refs_0_, bf16[2,64,5120]{2,1,0:T(8,128)(2,1)} %refs_1_.12, bf16[128,5120]{1,0:T(8,128)(2,1)} %refs_2_.7, f32[1,5120]{1,0:T(1,128)} %bitcast.2), custom_call_target="tpu_custom_call" | custom-call | flops 1 | bytes 3400000 | tf_op jit(solution)/shard_map/pack_own/pallas_call | solution.py:28
  29.7 5.0 %collective-permute-done.10.refs_3_.refs_4_ = bf16[256,640]{1,0:T(8,128)(2,1)S(1)} collective-permute-done((bf16[256,640]{1,0:T(8,128)(2,1)S(1)}, bf16[256,640]{1,0:T(8,128)(2,1)S(1)}, u32[]{:S(2)}, u32[]{:S(2)}) %collective-permute-start.10) | collective-permute-done | bytes 327712 | tf_op jit(solution)/shard_map/ppermute | solution.py:347
  35.0 3.6 %collective-permute-done.6.refs_8_.refs_5_ = bf16[128,640]{1,0:T(8,128)(2,1)S(1)} collective-permute-done((bf16[128,640]{1,0:T(8,128)(2,1)S(1)}, bf16[128,640]{1,0:T(8,128)(2,1)S(1)}, u32[]{:S(2)}, u32[]{:S(2)}) %collective-permute-start.6) | collective-permute-done | bytes 163872 | tf_op jit(solution)/shard_map/ppermute | solution.py:347
  38.6 3.0 %collective-permute-start.14 = (bf16[256,640]{1,0:T(8,128)(2,1)S(1)}, bf16[256,640]{1,0:T(8,128)(2,1)S(1)}, u32[]{:S(2)}, u32[]{:S(2)}) collective-permute-start(bf16[256,640]{1,0:T(8,128)(2,1)S(1)} %get-tuple-element.82), channel_id=1, source_target_pairs={{0,12},{1,13},{2,14},{3,15},{4,0},{5,1},{6,2},{7,3},{8,4},{9,5},{1... | collective-permute-start | bytes 983048 | tf_op jit(solution)/shard_map/ppermute | solution.py:357
  45.4 2.2 %collective-permute-done.5.refs_7_.refs_4_ = bf16[128,640]{1,0:T(8,128)(2,1)S(1)} collective-permute-done((bf16[128,640]{1,0:T(8,128)(2,1)S(1)}, bf16[128,640]{1,0:T(8,128)(2,1)S(1)}, u32[]{:S(2)}, u32[]{:S(2)}) %collective-permute-start.5) | collective-permute-done | bytes 163872 | tf_op jit(solution)/shard_map/ppermute | solution.py:347
  47.6 3.9 %hint_branch.2 = (bf16[8,64,640]{2,1,0:T(8,128)(2,1)S(1)}, bf16[2,64,640]{2,1,0:T(8,128)(2,1)S(1)}, bf16[2,64,640]{2,1,0:T(8,128)(2,1)S(1)}, bf16[12,64,640]{2,1...) custom-call(s32[1]{0:T(128)} %bitcast.refs_0_, ...), custom_call_target="tpu_custom_call" | custom-call | flops 1 | bytes 15300000 | tf_op jit(solution)/shard_map/hint_branch/pallas_call | solution.py:28
  51.6 3.2 %collective-permute-start.19 = (bf16[2,64,640]{2,1,0:T(8,128)(2,1)S(1)}, bf16[2,64,640]{2,1,0:T(8,128)(2,1)S(1)}, u32[]{:S(2)}, u32[]{:S(2)}) collective-permute-start(bf16[2,64,640]{2,1,0:T(8,128)(2,1)S(1)} %get-tuple-element.99), channel_id=1, source_target_pairs={{0,12},{1,13},{2,14},{3,15},{4,0},{5,1},{6,2},{7,3},{8,4},{9,5},{1... | collective-permute-start | bytes 491528 | tf_op jit(solution)/shard_map/ppermute | solution.py:357
  55.7 3.9 %hint_branch.3 = (bf16[8,64,640]{2,1,0:T(8,128)(2,1)S(1)}, bf16[2,64,640]{2,1,0:T(8,128)(2,1)S(1)}, bf16[2,64,640]{2,1,0:T(8,128)(2,1)S(1)}, bf16[12,64,640]{2,1,0:T(8,128)(2,1)S(1)}) custom-call(s32[1]{0:T(128)} %bitcast.refs_0_, s32[4,8,128]{2,1,0:T(8,128)S(1)} %get-tuple-element.72.refs_1_, bf16[256,640]{1,0:T(8,128)(2,1)S(1)} %get-tuple-element.79.refs_1_.refs_2_, ...), custom_call_target="tpu_custom_call" | custom-call | flops 1 | bytes 15300000 | tf_op jit(solution)/shard_map/hint_branch/pallas_call | solution.py:28
  60.4 2.4 %collective-permute-start.16 = (bf16[2,64,640]{2,1,0:T(8,128)(2,1)S(1)}, bf16[2,64,640]{2,1,0:T(8,128)(2,1)S(1)}, u32[]{:S(2)}, u32[]{:S(2)}) collective-permute-start(bf16[2,64,640]{2,1,0:T(8,128)(2,1)S(1)} %get-tuple-element.89), channel_id=1, source_target_pairs={{0,12},{1,13},{2,14},{3,15},{4,0},{5,1},{6,2},{7,3},{8,4},{9,5},{1... | collective-permute-start | bytes 491528 | tf_op jit(solution)/shard_map/ppermute | solution.py:357
  62.8 3.0 %base_block.3 = (bf16[2,64,640]{2,1,0:T(8,128)(2,1)S(1)}, bf16[2,64,640]{2,1,0:T(8,128)(2,1)S(1)}, bf16[2,64,640]{2,1,0:T(8,128)(2,1)S(1)}, bf16[2,64,640]{2,1,0:T(8,128)(2,1)S(1)}) custom-call(s32[1]{0:T(128)} %bitcast.refs_0_, s32[4,8,128]{2,1,0:T(8,128)S(1)} %get-tuple-element.72.refs_1_, bf16[128,1280]{1,0:T(8,128)(2,1)S(1)} %get-tuple-element.61.refs_5_.refs_6_.refs_2_, ...), custom_call_target="tpu_custom_call" | custom-call | flops 1 | bytes 11900000 | tf_op jit(solution)/shard_map/base_block/pallas_call | solution.py:28
  65.9 2.1 %collective-permute-start.22 = (bf16[2,64,640]{2,1,0:T(8,128)(2,1)S(1)}, bf16[2,64,640]{2,1,0:T(8,128)(2,1)S(1)}, u32[]{:S(2)}, u32[]{:S(2)}) collective-permute-start(bf16[2,64,640]{2,1,0:T(8,128)(2,1)S(1)} %get-tuple-element.105), channel_id=1, source_target_pairs={{0,3},{1,2},{2,1},{3,0},{4,7},{5,6},{6,5},{7,4},{8,11},{9,10},{10,... | collective-permute-start | bytes 491528 | tf_op jit(solution)/shard_map/ppermute | solution.py:347
  69.0 3.0 %base_block.2 = (bf16[2,64,640]{2,1,0:T(8,128)(2,1)S(1)}, bf16[2,64,640]{2,1,0:T(8,128)(2,1)S(1)}, bf16[2,64,640]{2,1,0:T(8,128)(2,1)S(1)}, bf16[2,64,640]{2,1,0:T(8,128)(2,1)S(1)}) custom-call(s32[1]{0:T(128)} %bitcast.refs_0_, s32[4,8,128]{2,1,0:T(8,128)S(1)} %get-tuple-element.72.refs_1_, bf16[128,1280]{1,0:T(8,128)(2,1)S(1)} %get-tuple-element.61.refs_5_.refs_6_.refs_2_, ...), custom_call_target="tpu_custom_call" | custom-call | flops 1 | bytes 11900000 | tf_op jit(solution)/shard_map/base_block/pallas_call | solution.py:28
  72.7 1.7 %collective-permute-start.23 = (bf16[2,64,640]{2,1,0:T(8,128)(2,1)S(1)}, bf16[2,64,640]{2,1,0:T(8,128)(2,1)S(1)}, u32[]{:S(2)}, u32[]{:S(2)}) collective-permute-start(bf16[2,64,640]{2,1,0:T(8,128)(2,1)S(1)} %get-tuple-element.106), channel_id=1, source_target_pairs={{0,3},{1,2},{2,1},{3,0},{4,7},{5,6},{6,5},{7,4},{8,11},{9,10},{10,... | collective-permute-start | bytes 491528 | tf_op jit(solution)/shard_map/ppermute | solution.py:347
  74.4 2.2 %collective-permute-done.20.refs_3_ = bf16[2,64,640]{2,1,0:T(8,128)(2,1)S(1)} collective-permute-done((bf16[2,64,640]{2,1,0:T(8,128)(2,1)S(1)}, bf16[2,64,640]{2,1,0:T(8,128)(2,1)S(1)}, u32[]{:S(2)}, u32[]{:S(2)}) %collective-permute-start.20) | collective-permute-done | bytes 163872 | tf_op jit(solution)/shard_map/ppermute | solution.py:347
  78.2 1.5 %collective-permute-done.23.refs_4_ = bf16[2,64,640]{2,1,0:T(8,128)(2,1)S(1)} collective-permute-done((bf16[2,64,640]{2,1,0:T(8,128)(2,1)S(1)}, bf16[2,64,640]{2,1,0:T(8,128)(2,1)S(1)}, u32[]{:S(2)}, u32[]{:S(2)}) %collective-permute-start.23) | collective-permute-done | bytes 163872 | tf_op jit(solution)/shard_map/ppermute | solution.py:347
  79.7 3.6 %collective-permute-done.21.refs_3_ = bf16[2,64,640]{2,1,0:T(8,128)(2,1)S(1)} collective-permute-done((bf16[2,64,640]{2,1,0:T(8,128)(2,1)S(1)}, bf16[2,64,640]{2,1,0:T(8,128)(2,1)S(1)}, u32[]{:S(2)}, u32[]{:S(2)}) %collective-permute-start.21) | collective-permute-done | bytes 163872 | tf_op jit(solution)/shard_map/ppermute | solution.py:347
  (41 shorter events, 16.6 us)
Async XLA Ops:
  1.3 10.4 %collective-permute-start.1 = (bf16[288,640]{1,0:T(8,128)(2,1)S(1)}, bf16[288,640]{1,0:T(8,128)(2,1)S(1)}, u32[]{:S(2)}, u32[]{:S(2)}) collective-permute-start(bf16[288,640]{1,0:T(8,128)(2,1)S(1)} %get-tuple-element.59), channel_id=1, source_target_pairs={{0,2},{1,3},{2,0},{3,1},{4,6},{5,7},{6,4},{7,5},{8,10},{9,11},{10,... | collective-permute-start | bytes 1105928 | tf_op jit(solution)/shard_map/ppermute | solution.py:347
  3.4 17.9 %collective-permute-start.2 = (bf16[288,640]{1,0:T(8,128)(2,1)S(1)}, bf16[288,640]{1,0:T(8,128)(2,1)S(1)}, u32[]{:S(2)}, u32[]{:S(2)}) collective-permute-start(bf16[288,640]{1,0:T(8,128)(2,1)S(1)} %get-tuple-element.60), channel_id=1, source_target_pairs={{0,3},{1,2},{2,1},{3,0},{4,7},{5,6},{6,5},{7,4},{8,11},{9,10},{10,... | collective-permute-start | bytes 1105928 | tf_op jit(solution)/shard_map/ppermute | solution.py:347
  5.3 16.0 %collective-permute-start = (bf16[288,640]{1,0:T(8,128)(2,1)S(1)}, bf16[288,640]{1,0:T(8,128)(2,1)S(1)}, u32[]{:S(2)}, u32[]{:S(2)}) collective-permute-start(bf16[288,640]{1,0:T(8,128)(2,1)S(1)} %get-tuple-element.58), channel_id=1, source_target_pairs={{0,1},{1,0},{2,3},{3,2},{4,5},{5,4},{6,7},{7,6},{8,9},{9,8},{10,11... | collective-permute-start | bytes 1105928 | tf_op jit(solution)/shard_map/ppermute | solution.py:353
  7.0 22.1 %collective-permute-start.4 = (bf16[256,640]{1,0:T(8,128)(2,1)S(1)}, bf16[256,640]{1,0:T(8,128)(2,1)S(1)}, u32[]{:S(2)}, u32[]{:S(2)}) collective-permute-start(bf16[256,640]{1,0:T(8,128)(2,1)S(1)} %get-tuple-element.64), channel_id=1, source_target_pairs={{0,3},{1,2},{2,1},{3,0},{4,7},{5,6},{6,5},{7,4},{8,11},{9,10},{10,... | collective-permute-start | bytes 983048 | tf_op jit(solution)/shard_map/ppermute | solution.py:347
  10.0 19.1 %collective-permute-start.12 = (bf16[256,640]{1,0:T(8,128)(2,1)S(1)}, bf16[256,640]{1,0:T(8,128)(2,1)S(1)}, u32[]{:S(2)}, u32[]{:S(2)}) collective-permute-start(bf16[256,640]{1,0:T(8,128)(2,1)S(1)} %get-tuple-element.80), channel_id=1, source_target_pairs={{0,1},{1,0},{2,3},{3,2},{4,5},{5,4},{6,7},{7,6},{8,9},{9,8},{10,11... | collective-permute-start | bytes 983048 | tf_op jit(solution)/shard_map/ppermute | solution.py:353
  21.4 20.2 %collective-permute-start.7 = (bf16[288,640]{1,0:T(8,128)(2,1)S(1)}, bf16[288,640]{1,0:T(8,128)(2,1)S(1)}, u32[]{:S(2)}, u32[]{:S(2)}) collective-permute-start(bf16[288,640]{1,0:T(8,128)(2,1)S(1)} %get-tuple-element.67), channel_id=1, source_target_pairs={{0,4},{1,5},{2,6},{3,7},{4,8},{5,9},{6,10},{7,11},{8,12},{9,13},{1... | collective-permute-start | bytes 1105928 | tf_op jit(solution)/shard_map/ppermute | solution.py:357
  23.3 20.4 %collective-permute-start.8 = (bf16[288,640]{1,0:T(8,128)(2,1)S(1)}, bf16[288,640]{1,0:T(8,128)(2,1)S(1)}, u32[]{:S(2)}, u32[]{:S(2)}) collective-permute-start(bf16[288,640]{1,0:T(8,128)(2,1)S(1)} %get-tuple-element.68), channel_id=1, source_target_pairs={{0,12},{1,13},{2,14},{3,15},{4,0},{5,1},{6,2},{7,3},{8,4},{9,5},{1... | collective-permute-start | bytes 1105928 | tf_op jit(solution)/shard_map/ppermute | solution.py:357
  25.4 9.4 %collective-permute-start.10 = (bf16[256,640]{1,0:T(8,128)(2,1)S(1)}, bf16[256,640]{1,0:T(8,128)(2,1)S(1)}, u32[]{:S(2)}, u32[]{:S(2)}) collective-permute-start(bf16[256,640]{1,0:T(8,128)(2,1)S(1)} %get-tuple-element.77), channel_id=1, source_target_pairs={{0,2},{1,3},{2,0},{3,1},{4,6},{5,7},{6,4},{7,5},{8,10},{9,11},{10,... | collective-permute-start | bytes 983048 | tf_op jit(solution)/shard_map/ppermute | solution.py:347
  29.0 15.1 %collective-permute-start.3 = (bf16[128,1280]{1,0:T(8,128)(2,1)S(1)}, bf16[128,1280]{1,0:T(8,128)(2,1)S(1)}, u32[]{:S(2)}, u32[]{:S(2)}) collective-permute-start(bf16[128,1280]{1,0:T(8,128)(2,1)S(1)} %get-tuple-element.62), channel_id=1, source_target_pairs={{0,1},{1,0},{2,3},{3,2},{4,5},{5,4},{6,7},{7,6},{8,9},{9,8},{10,11... | collective-permute-start | bytes 983048 | tf_op jit(solution)/shard_map/ppermute | solution.py:353
  29.1 9.5 %collective-permute-start.6 = (bf16[128,640]{1,0:T(8,128)(2,1)S(1)}, bf16[128,640]{1,0:T(8,128)(2,1)S(1)}, u32[]{:S(2)}, u32[]{:S(2)}) collective-permute-start(bf16[128,640]{1,0:T(8,128)(2,1)S(1)} %get-tuple-element.69), channel_id=1, source_target_pairs={{0,3},{1,2},{2,1},{3,0},{4,7},{5,6},{6,5},{7,4},{8,11},{9,10},{10,... | collective-permute-start | bytes 491528 | tf_op jit(solution)/shard_map/ppermute | solution.py:347
  34.8 20.0 %collective-permute-start.13 = (bf16[256,640]{1,0:T(8,128)(2,1)S(1)}, bf16[256,640]{1,0:T(8,128)(2,1)S(1)}, u32[]{:S(2)}, u32[]{:S(2)}) collective-permute-start(bf16[256,640]{1,0:T(8,128)(2,1)S(1)} %get-tuple-element.81), channel_id=1, source_target_pairs={{0,4},{1,5},{2,6},{3,7},{4,8},{5,9},{6,10},{7,11},{8,12},{9,13},{1... | collective-permute-start | bytes 983048 | tf_op jit(solution)/shard_map/ppermute | solution.py:357
  38.6 17.0 %collective-permute-start.14 = (bf16[256,640]{1,0:T(8,128)(2,1)S(1)}, bf16[256,640]{1,0:T(8,128)(2,1)S(1)}, u32[]{:S(2)}, u32[]{:S(2)}) collective-permute-start(bf16[256,640]{1,0:T(8,128)(2,1)S(1)} %get-tuple-element.82), channel_id=1, source_target_pairs={{0,12},{1,13},{2,14},{3,15},{4,0},{5,1},{6,2},{7,3},{8,4},{9,5},{1... | collective-permute-start | bytes 983048 | tf_op jit(solution)/shard_map/ppermute | solution.py:357
  41.6 6.0 %collective-permute-start.5 = (bf16[128,640]{1,0:T(8,128)(2,1)S(1)}, bf16[128,640]{1,0:T(8,128)(2,1)S(1)}, u32[]{:S(2)}, u32[]{:S(2)}) collective-permute-start(bf16[128,640]{1,0:T(8,128)(2,1)S(1)} %get-tuple-element.65), channel_id=1, source_target_pairs={{0,2},{1,3},{2,0},{3,1},{4,6},{5,7},{6,4},{7,5},{8,10},{9,11},{10,... | collective-permute-start | bytes 491528 | tf_op jit(solution)/shard_map/ppermute | solution.py:347
  43.7 7.9 %collective-permute-start.9 = (bf16[128,640]{1,0:T(8,128)(2,1)S(1)}, bf16[128,640]{1,0:T(8,128)(2,1)S(1)}, u32[]{:S(2)}, u32[]{:S(2)}) collective-permute-start(bf16[128,640]{1,0:T(8,128)(2,1)S(1)} %get-tuple-element.74), channel_id=1, source_target_pairs={{0,2},{1,3},{2,0},{3,1},{4,6},{5,7},{6,4},{7,5},{8,10},{9,11},{10,... | collective-permute-start | bytes 491528 | tf_op jit(solution)/shard_map/ppermute | solution.py:347
  44.2 10.7 %collective-permute-start.11 = (bf16[128,640]{1,0:T(8,128)(2,1)S(1)}, bf16[128,640]{1,0:T(8,128)(2,1)S(1)}, u32[]{:S(2)}, u32[]{:S(2)}) collective-permute-start(bf16[128,640]{1,0:T(8,128)(2,1)S(1)} %get-tuple-element.78), channel_id=1, source_target_pairs={{0,3},{1,2},{2,1},{3,0},{4,7},{5,6},{6,5},{7,4},{8,11},{9,10},{10,... | collective-permute-start | bytes 491528 | tf_op jit(solution)/shard_map/ppermute | solution.py:347
  51.5 11.3 %collective-permute-start.18 = (bf16[2,64,640]{2,1,0:T(8,128)(2,1)S(1)}, bf16[2,64,640]{2,1,0:T(8,128)(2,1)S(1)}, u32[]{:S(2)}, u32[]{:S(2)}) collective-permute-start(bf16[2,64,640]{2,1,0:T(8,128)(2,1)S(1)} %get-tuple-element.98), channel_id=1, source_target_pairs={{0,4},{1,5},{2,6},{3,7},{4,8},{5,9},{6,10},{7,11},{8,12},{9,13},{1... | collective-permute-start | bytes 491528 | tf_op jit(solution)/shard_map/ppermute | solution.py:357
  51.6 11.2 %collective-permute-start.19 = (bf16[2,64,640]{2,1,0:T(8,128)(2,1)S(1)}, bf16[2,64,640]{2,1,0:T(8,128)(2,1)S(1)}, u32[]{:S(2)}, u32[]{:S(2)}) collective-permute-start(bf16[2,64,640]{2,1,0:T(8,128)(2,1)S(1)} %get-tuple-element.99), channel_id=1, source_target_pairs={{0,12},{1,13},{2,14},{3,15},{4,0},{5,1},{6,2},{7,3},{8,4},{9,5},{1... | collective-permute-start | bytes 491528 | tf_op jit(solution)/shard_map/ppermute | solution.py:357
  59.5 9.1 %collective-permute-start.15 = (bf16[2,64,640]{2,1,0:T(8,128)(2,1)S(1)}, bf16[2,64,640]{2,1,0:T(8,128)(2,1)S(1)}, u32[]{:S(2)}, u32[]{:S(2)}) collective-permute-start(bf16[2,64,640]{2,1,0:T(8,128)(2,1)S(1)} %get-tuple-element.88), channel_id=1, source_target_pairs={{0,4},{1,5},{2,6},{3,7},{4,8},{5,9},{6,10},{7,11},{8,12},{9,13},{1... | collective-permute-start | bytes 491528 | tf_op jit(solution)/shard_map/ppermute | solution.py:357
  60.4 8.6 %collective-permute-start.16 = (bf16[2,64,640]{2,1,0:T(8,128)(2,1)S(1)}, bf16[2,64,640]{2,1,0:T(8,128)(2,1)S(1)}, u32[]{:S(2)}, u32[]{:S(2)}) collective-permute-start(bf16[2,64,640]{2,1,0:T(8,128)(2,1)S(1)} %get-tuple-element.89), channel_id=1, source_target_pairs={{0,12},{1,13},{2,14},{3,15},{4,0},{5,1},{6,2},{7,3},{8,4},{9,5},{1... | collective-permute-start | bytes 491528 | tf_op jit(solution)/shard_map/ppermute | solution.py:357
  65.9 6.8 %collective-permute-start.22 = (bf16[2,64,640]{2,1,0:T(8,128)(2,1)S(1)}, bf16[2,64,640]{2,1,0:T(8,128)(2,1)S(1)}, u32[]{:S(2)}, u32[]{:S(2)}) collective-permute-start(bf16[2,64,640]{2,1,0:T(8,128)(2,1)S(1)} %get-tuple-element.105), channel_id=1, source_target_pairs={{0,3},{1,2},{2,1},{3,0},{4,7},{5,6},{6,5},{7,4},{8,11},{9,10},{10,... | collective-permute-start | bytes 491528 | tf_op jit(solution)/shard_map/ppermute | solution.py:347
  68.0 8.6 %collective-permute-start.20 = (bf16[2,64,640]{2,1,0:T(8,128)(2,1)S(1)}, bf16[2,64,640]{2,1,0:T(8,128)(2,1)S(1)}, u32[]{:S(2)}, u32[]{:S(2)}) collective-permute-start(bf16[2,64,640]{2,1,0:T(8,128)(2,1)S(1)} %get-tuple-element.101), channel_id=1, source_target_pairs={{0,2},{1,3},{2,0},{3,1},{4,6},{5,7},{6,4},{7,5},{8,10},{9,11},{10,... | collective-permute-start | bytes 491528 | tf_op jit(solution)/shard_map/ppermute | solution.py:347
  68.6 8.8 %collective-permute-start.24 = (bf16[2,64,640]{2,1,0:T(8,128)(2,1)S(1)}, bf16[2,64,640]{2,1,0:T(8,128)(2,1)S(1)}, u32[]{:S(2)}, u32[]{:S(2)}) collective-permute-start(bf16[2,64,640]{2,1,0:T(8,128)(2,1)S(1)} %get-tuple-element.108), channel_id=1, source_target_pairs={{0,1},{1,0},{2,3},{3,2},{4,5},{5,4},{6,7},{7,6},{8,9},{9,8},{10,11... | collective-permute-start | bytes 491528 | tf_op jit(solution)/shard_map/ppermute | solution.py:353
  72.7 7.0 %collective-permute-start.23 = (bf16[2,64,640]{2,1,0:T(8,128)(2,1)S(1)}, bf16[2,64,640]{2,1,0:T(8,128)(2,1)S(1)}, u32[]{:S(2)}, u32[]{:S(2)}) collective-permute-start(bf16[2,64,640]{2,1,0:T(8,128)(2,1)S(1)} %get-tuple-element.106), channel_id=1, source_target_pairs={{0,3},{1,2},{2,1},{3,0},{4,7},{5,6},{6,5},{7,4},{8,11},{9,10},{10,... | collective-permute-start | bytes 491528 | tf_op jit(solution)/shard_map/ppermute | solution.py:347
  76.6 6.8 %collective-permute-start.21 = (bf16[2,64,640]{2,1,0:T(8,128)(2,1)S(1)}, bf16[2,64,640]{2,1,0:T(8,128)(2,1)S(1)}, u32[]{:S(2)}, u32[]{:S(2)}) collective-permute-start(bf16[2,64,640]{2,1,0:T(8,128)(2,1)S(1)} %get-tuple-element.102), channel_id=1, source_target_pairs={{0,2},{1,3},{2,0},{3,1},{4,6},{5,7},{6,4},{7,5},{8,10},{9,11},{10,... | collective-permute-start | bytes 491528 | tf_op jit(solution)/shard_map/ppermute | solution.py:347
  (1 other events, 6.0 us)

commit v7 on v6

--- a/solution.py
+++ b/solution.py
@@ -254,33 +254,33 @@
     return run(kernel, "hint_branch", ins, outs, scratch, 1, scalars, us=0.5 + 0.8 * len(heads))
 
 
-def base_block(me, queries, keys, mixed, mixed_before, mixed_after, meta, spans, first):
+def base_block(me, ks, queries, keys, mixed, mixed_before, mixed_after, meta, spans, first):
     total, toks, width = mixed.shape
     frames, wide = total // GROUP, total + 2 * BAND
     heads = [slice(h * HEAD_DIM, (h + 1) * HEAD_DIM) for h in range(width // HEAD_DIM)]
 
     def kernel(scalars, ins, outs, scratch, sems):
         mine, meta = scalars[0][0], scalars[1]
-        k_ref, m_s = ins[GROUP], scratch[0]
-        m_s[BAND : BAND + total] = ins[GROUP + 1][...]
-        m_s[:BAND] = ins[GROUP + 2][...]
-        m_s[BAND + total :] = ins[GROUP + 3][...]
+        k_ref, m_s = ins[len(ks)], scratch[0]
+        m_s[BAND : BAND + total] = ins[len(ks) + 1][...]
+        m_s[:BAND] = ins[len(ks) + 2][...]
+        m_s[BAND + total :] = ins[len(ks) + 3][...]
         at, jobs = [], []
-        for k in range(GROUP):
+        for i, k in enumerate(ks):
             for r in range(frames):
                 s = mine ^ k
                 spots = [BAND + s * frames + r + meta[s, r, j] for j in range(spans)]
                 for cols in heads:
-                    at.append((k, r, cols))
+                    at.append((i, r, cols))
                     left = first if k < 2 else 0
-                    query = ins[k][r * toks : (r + 1) * toks, left + cols.start : left + cols.stop]
+                    query = ins[i][r * toks : (r + 1) * toks, left + cols.start : left + cols.stop]
                     jobs.append((query, band(k_ref, spots, cols), band(m_s, spots, cols)))
-        for (k, r, cols), out in zip(at, attend(jobs)):
-            outs[k][r, :, cols] = out
+        for (i, r, cols), out in zip(at, attend(jobs)):
+            outs[i][r, :, cols] = out
 
     ins = [*queries, keys, mixed, mixed_before, mixed_after]
     scratch = [pltpu.VMEM((wide, toks, width), BF16)]
-    outs = [rows((frames, toks, width))] * GROUP
+    outs = [rows((frames, toks, width))] * len(ks)
     return run(kernel, "base_block", ins, outs, scratch, 0, [me, meta], us=0.7 * len(heads))
 
 
@@ -380,8 +380,11 @@
         parts = []
         for c, (first, width) in enumerate(cuts):
             keys = after(mixed[c][0], mixed[n - 1][1]) if True and c < n - 1 else mixed[c][0]
-            got = base_block(me, asked[c], keys, *mixed[c][1:], setting[1], spans, first)
-            parts.append([*near_group(got[:2]), *far_group(got[:1:-1], 2)])
+            rest = (keys, *mixed[c][1:], setting[1], spans, first)
+            sent = base_block(me, (3, 2), asked[c][:1:-1], *rest)
+            far = far_group(sent, 2)
+            got = base_block(after(me, sent[0]), (0, 1), asked[c][:2], *rest)
+            parts.append([*near_group(got), *far])
         out = None
         for c, (first, width) in enumerate(cuts):
             out = place(me, parts[c], out, model_width, quarter, first)

time: 85 us -> 84 us (0.988)
  waiting for transfers between devices: 31.3 us -> 28.1 us
  Pallas kernels: 24.1 us -> 26.2 us
    ppermute x12, waiting for transfers between devices: 30 us -> 27.3 us  [far_group(): got.append(lax.ppermute(part, 'tm', across[k]))]
    pallas_call x15 -> x17, Pallas kernels: 24.1 us -> 26.2 us  [run(): pl.pallas_call(body, out_shape=list(outs), in_specs=[SMEM] * a + (where i...]
  transfers between devices with their start and end apart: 25 -> 25, of which waited for: 11 -> 8; matrix products, arithmetic and copies ran while one was open for 0% -> 0% of each run, Pallas kernels for 26% -> 29%
where the time goes in v7:
time: 84 us; the launch traced here: 83.3 us
  starting transfers between devices  28.7 us (34%)
  waiting for transfers between devices  28.1 us (33%)
  Pallas kernels  26.2 us (31%)
    ppermute x12, waiting for transfers between devices, far_group(): got.append(lax.ppermute(part, 'tm', across[k]))  27.3 us
    pallas_call x17, Pallas kernels, run(): pl.pallas_call(body, out_shape=list(outs), in_specs=[SMEM] * a + (where i...  26.2 us
    ppermute x12, starting transfers between devices, far_group(): got.append(lax.ppermute(part, 'tm', across[k]))  14 us
    ppermute x4, starting transfers between devices, along(): lax.ppermute(start, 'tm', downward)  10.7 us
    ppermute x4, starting transfers between devices, along(): lax.ppermute(last, 'tm', upward)  2.98 us
  transfers between devices with their start and end apart: 25, of which 8 were waited for; matrix products, arithmetic and copies ran while one was open for 0% of the time, Pallas kernels for 29%

profile of v7, /device:TPU:1, one launch (start us, length us, event | category | flops | bytes accessed | tf_op | source)
XLA Modules:
  0.0 83.3 jit_solution(13633549692996267598)
XLA Ops:
  0.0 1.3 %pack.7 = (bf16[288,640]{1,0:T(8,128)(2,1)S(1)}, bf16[288,640]{1,0:T(8,128)(2,1)S(1)}) custom-call(s32[1]{0:T(128)} %bitcast.refs_0_, bf16[2,64,5120]{2,1,0:T(8,128)(2,1)} %refs_1_.13, bf16[2,64,5120]{2,1,0:T(8,128)(2,1)} %refs_2_.9, bf16[2,64,128]{2,1,0:T(8,128)(2,1)} %refs_3_.3, s32[2,3]{1,0:T(2,128)} %refs_4_.3, s32[2]{0:T(128)} %refs_5_.3), custom_call_target="tpu_custom_call" | custom-call | flops 1 | bytes 3400000 | tf_op jit(solution)/shard_map/pack/pallas_call | solution.py:28
  1.3 2.1 %collective-permute-start.1 = (bf16[288,640]{1,0:T(8,128)(2,1)S(1)}, bf16[288,640]{1,0:T(8,128)(2,1)S(1)}, u32[]{:S(2)}, u32[]{:S(2)}) collective-permute-start(bf16[288,640]{1,0:T(8,128)(2,1)S(1)} %get-tuple-element.61), channel_id=1, source_target_pairs={{0,2},{1,3},{2,0},{3,1},{4,6},{5,7},{6,4},{7,5},{8,10},{9,11},{10,... | collective-permute-start | bytes 1105928 | tf_op jit(solution)/shard_map/ppermute | solution.py:347
  7.0 1.8 %collective-permute-start.4 = (bf16[256,640]{1,0:T(8,128)(2,1)S(1)}, bf16[256,640]{1,0:T(8,128)(2,1)S(1)}, u32[]{:S(2)}, u32[]{:S(2)}) collective-permute-start(bf16[256,640]{1,0:T(8,128)(2,1)S(1)} %get-tuple-element.66), channel_id=1, source_target_pairs={{0,3},{1,2},{2,1},{3,0},{4,7},{5,6},{6,5},{7,4},{8,11},{9,10},{10,... | collective-permute-start | bytes 983048 | tf_op jit(solution)/shard_map/ppermute | solution.py:347
  10.1 1.6 %collective-permute-done.1.refs_3_ = bf16[288,640]{1,0:T(8,128)(2,1)S(1)} collective-permute-done((bf16[288,640]{1,0:T(8,128)(2,1)S(1)}, bf16[288,640]{1,0:T(8,128)(2,1)S(1)}, u32[]{:S(2)}, u32[]{:S(2)}) %collective-permute-start.1) | collective-permute-done | bytes 368672 | tf_op jit(solution)/shard_map/ppermute | solution.py:347
  11.7 9.6 %collective-permute-done.2.refs_4_ = bf16[288,640]{1,0:T(8,128)(2,1)S(1)} collective-permute-done((bf16[288,640]{1,0:T(8,128)(2,1)S(1)}, bf16[288,640]{1,0:T(8,128)(2,1)S(1)}, u32[]{:S(2)}, u32[]{:S(2)}) %collective-permute-start.2) | collective-permute-done | bytes 368672 | tf_op jit(solution)/shard_map/ppermute | solution.py:347
  21.4 1.9 %collective-permute-start.7 = (bf16[288,640]{1,0:T(8,128)(2,1)S(1)}, bf16[288,640]{1,0:T(8,128)(2,1)S(1)}, u32[]{:S(2)}, u32[]{:S(2)}) collective-permute-start(bf16[288,640]{1,0:T(8,128)(2,1)S(1)} %get-tuple-element.69), channel_id=1, source_target_pairs={{0,4},{1,5},{2,6},{3,7},{4,8},{5,9},{6,10},{7,11},{8,12},{9,13},{1... | collective-permute-start | bytes 1105928 | tf_op jit(solution)/shard_map/ppermute | solution.py:357
  23.3 2.1 %collective-permute-start.8 = (bf16[288,640]{1,0:T(8,128)(2,1)S(1)}, bf16[288,640]{1,0:T(8,128)(2,1)S(1)}, u32[]{:S(2)}, u32[]{:S(2)}) collective-permute-start(bf16[288,640]{1,0:T(8,128)(2,1)S(1)} %get-tuple-element.70), channel_id=1, source_target_pairs={{0,12},{1,13},{2,14},{3,15},{4,0},{5,1},{6,2},{7,3},{8,4},{9,5},{1... | collective-permute-start | bytes 1105928 | tf_op jit(solution)/shard_map/ppermute | solution.py:357
  27.7 1.4 %pack_own.1 = (bf16[128,1280]{1,0:T(8,128)(2,1)S(1)}, bf16[128,1280]{1,0:T(8,128)(2,1)S(1)}, bf16[128,1280]{1,0:T(8,128)(2,1)S(1)}, f32[1,1280]{1,0:T(1,128)S(1)}) custom-call(s32[1]{0:T(128)} %bitcast.refs_0_, bf16[2,64,5120]{2,1,0:T(8,128)(2,1)} %refs_1_.12, bf16[128,5120]{1,0:T(8,128)(2,1)} %refs_2_.7, f32[1,5120]{1,0:T(1,128)} %bitcast.2), custom_call_target="tpu_custom_call" | custom-call | flops 1 | bytes 3400000 | tf_op jit(solution)/shard_map/pack_own/pallas_call | solution.py:28
  29.7 5.0 %collective-permute-done.9.refs_3_.refs_4_ = bf16[256,640]{1,0:T(8,128)(2,1)S(1)} collective-permute-done((bf16[256,640]{1,0:T(8,128)(2,1)S(1)}, bf16[256,640]{1,0:T(8,128)(2,1)S(1)}, u32[]{:S(2)}, u32[]{:S(2)}) %collective-permute-start.9) | collective-permute-done | bytes 327712 | tf_op jit(solution)/shard_map/ppermute | solution.py:347
  35.0 3.6 %collective-permute-done.6.refs_8_.refs_2_ = bf16[128,640]{1,0:T(8,128)(2,1)S(1)} collective-permute-done((bf16[128,640]{1,0:T(8,128)(2,1)S(1)}, bf16[128,640]{1,0:T(8,128)(2,1)S(1)}, u32[]{:S(2)}, u32[]{:S(2)}) %collective-permute-start.6) | collective-permute-done | bytes 163872 | tf_op jit(solution)/shard_map/ppermute | solution.py:347
  38.6 3.0 %collective-permute-start.14 = (bf16[256,640]{1,0:T(8,128)(2,1)S(1)}, bf16[256,640]{1,0:T(8,128)(2,1)S(1)}, u32[]{:S(2)}, u32[]{:S(2)}) collective-permute-start(bf16[256,640]{1,0:T(8,128)(2,1)S(1)} %get-tuple-element.84), channel_id=1, source_target_pairs={{0,12},{1,13},{2,14},{3,15},{4,0},{5,1},{6,2},{7,3},{8,4},{9,5},{1... | collective-permute-start | bytes 983048 | tf_op jit(solution)/shard_map/ppermute | solution.py:357
  45.4 2.2 %collective-permute-done.5.refs_7_.refs_3_ = bf16[128,640]{1,0:T(8,128)(2,1)S(1)} collective-permute-done((bf16[128,640]{1,0:T(8,128)(2,1)S(1)}, bf16[128,640]{1,0:T(8,128)(2,1)S(1)}, u32[]{:S(2)}, u32[]{:S(2)}) %collective-permute-start.5) | collective-permute-done | bytes 163872 | tf_op jit(solution)/shard_map/ppermute | solution.py:347
  47.6 3.9 %hint_branch.2 = (bf16[8,64,640]{2,1,0:T(8,128)(2,1)S(1)}, bf16[2,64,640]{2,1,0:T(8,128)(2,1)S(1)}, bf16[2,64,640]{2,1,0:T(8,128)(2,1)S(1)}, bf16[12,64,640]{2,1...) custom-call(s32[1]{0:T(128)} %bitcast.refs_0_, ...), custom_call_target="tpu_custom_call" | custom-call | flops 1 | bytes 15300000 | tf_op jit(solution)/shard_map/hint_branch/pallas_call | solution.py:28
  51.6 3.2 %collective-permute-start.19 = (bf16[2,64,640]{2,1,0:T(8,128)(2,1)S(1)}, bf16[2,64,640]{2,1,0:T(8,128)(2,1)S(1)}, u32[]{:S(2)}, u32[]{:S(2)}) collective-permute-start(bf16[2,64,640]{2,1,0:T(8,128)(2,1)S(1)} %get-tuple-element.103), channel_id=1, source_target_pairs={{0,12},{1,13},{2,14},{3,15},{4,0},{5,1},{6,2},{7,3},{8,4},{9,5},{1... | collective-permute-start | bytes 491528 | tf_op jit(solution)/shard_map/ppermute | solution.py:357
  55.7 3.9 %hint_branch.3 = (bf16[8,64,640]{2,1,0:T(8,128)(2,1)S(1)}, bf16[2,64,640]{2,1,0:T(8,128)(2,1)S(1)}, bf16[2,64,640]{2,1,0:T(8,128)(2,1)S(1)}, bf16[12,64,640]{2,1,0:T(8,128)(2,1)S(1)}) custom-call(s32[1]{0:T(128)} %bitcast.refs_0_, s32[4,8,128]{2,1,0:T(8,128)S(1)} %get-tuple-element.74.refs_1_, bf16[256,640]{1,0:T(8,128)(2,1)S(1)} %get-tuple-element.81.refs_1_.refs_2_, ...), custom_call_target="tpu_custom_call" | custom-call | flops 1 | bytes 15300000 | tf_op jit(solution)/shard_map/hint_branch/pallas_call | solution.py:28
  60.4 2.4 %collective-permute-start.16 = (bf16[2,64,640]{2,1,0:T(8,128)(2,1)S(1)}, bf16[2,64,640]{2,1,0:T(8,128)(2,1)S(1)}, u32[]{:S(2)}, u32[]{:S(2)}) collective-permute-start(bf16[2,64,640]{2,1,0:T(8,128)(2,1)S(1)} %get-tuple-element.91), channel_id=1, source_target_pairs={{0,12},{1,13},{2,14},{3,15},{4,0},{5,1},{6,2},{7,3},{8,4},{9,5},{1... | collective-permute-start | bytes 491528 | tf_op jit(solution)/shard_map/ppermute | solution.py:357
  62.9 2.0 %base_block.6 = (bf16[2,64,640]{2,1,0:T(8,128)(2,1)S(1)}, bf16[2,64,640]{2,1,0:T(8,128)(2,1)S(1)}) custom-call(s32[1]{0:T(128)} %bitcast.refs_0_, s32[4,8,128]{2,1,0:T(8,128)S(1)} %get-tuple-element.74.refs_1_, bf16[128,640]{1,0:T(8,128)(2,1)S(1)} %collective-permute-done.6.refs_8_.refs_2_, bf16[128,640]{1,0:T(8,128)(2,1)S(1)} %collective-permute-done.5.refs_7_.refs_3_, ...), custom_call_target="tpu_custom_call" | custom-call | flops 1 | bytes 11900000 | tf_op jit(solution)/shard_map/base_block/pallas_call | solution.py:28
  64.9 2.1 %collective-permute-start.22 = (bf16[2,64,640]{2,1,0:T(8,128)(2,1)S(1)}, bf16[2,64,640]{2,1,0:T(8,128)(2,1)S(1)}, u32[]{:S(2)}, u32[]{:S(2)}) collective-permute-start(bf16[2,64,640]{2,1,0:T(8,128)(2,1)S(1)} %get-tuple-element.108), channel_id=1, source_target_pairs={{0,3},{1,2},{2,1},{3,0},{4,7},{5,6},{6,5},{7,4},{8,11},{9,10},{10,... | collective-permute-start | bytes 491528 | tf_op jit(solution)/shard_map/ppermute | solution.py:347
  67.6 2.0 %base_block.7 = (bf16[2,64,640]{2,1,0:T(8,128)(2,1)S(1)}, bf16[2,64,640]{2,1,0:T(8,128)(2,1)S(1)}) custom-call(s32[1]{0:T(128)} %bitcast.refs_0_, s32[4,8,128]{2,1,0:T(8,128)S(1)} %get-tuple-element.74.refs_1_, bf16[128,1280]{1,0:T(8,128)(2,1)S(1)} %get-tuple-element.63.refs_5_.refs_6_.refs_2_, ...), custom_call_target="tpu_custom_call" | custom-call | flops 1 | bytes 11900000 | tf_op jit(solution)/shard_map/base_block/pallas_call | solution.py:28
  69.8 2.0 %base_block.4 = (bf16[2,64,640]{2,1,0:T(8,128)(2,1)S(1)}, bf16[2,64,640]{2,1,0:T(8,128)(2,1)S(1)}) custom-call(s32[1]{0:T(128)} %bitcast.refs_0_, s32[4,8,128]{2,1,0:T(8,128)S(1)} %get-tuple-element.74.refs_1_, bf16[128,640]{1,0:T(8,128)(2,1)S(1)} %collective-permute-done.10.refs_9_.refs_2_, bf16[128,640]{1,0:T(8,128)(2,1)S(1)} %collective-permute-done.11.refs_8_.refs_3_, ...), custom_call_target="tpu_custom_call" | custom-call | flops 1 | bytes 11900000 | tf_op jit(solution)/shard_map/base_block/pallas_call | solution.py:28
  71.8 1.6 %collective-permute-start.23 = (bf16[2,64,640]{2,1,0:T(8,128)(2,1)S(1)}, bf16[2,64,640]{2,1,0:T(8,128)(2,1)S(1)}, u32[]{:S(2)}, u32[]{:S(2)}) collective-permute-start(bf16[2,64,640]{2,1,0:T(8,128)(2,1)S(1)} %get-tuple-element.109), channel_id=1, source_target_pairs={{0,3},{1,2},{2,1},{3,0},{4,7},{5,6},{6,5},{7,4},{8,11},{9,10},{10,... | collective-permute-start | bytes 491528 | tf_op jit(solution)/shard_map/ppermute | solution.py:347
  73.4 2.2 %collective-permute-done.20.refs_3_ = bf16[2,64,640]{2,1,0:T(8,128)(2,1)S(1)} collective-permute-done((bf16[2,64,640]{2,1,0:T(8,128)(2,1)S(1)}, bf16[2,64,640]{2,1,0:T(8,128)(2,1)S(1)}, u32[]{:S(2)}, u32[]{:S(2)}) %collective-permute-start.20) | collective-permute-done | bytes 163872 | tf_op jit(solution)/shard_map/ppermute | solution.py:347
  76.0 2.0 %base_block.5 = (bf16[2,64,640]{2,1,0:T(8,128)(2,1)S(1)}, bf16[2,64,640]{2,1,0:T(8,128)(2,1)S(1)}) custom-call(s32[1]{0:T(128)} %bitcast.refs_0_, s32[4,8,128]{2,1,0:T(8,128)S(1)} %get-tuple-element.74.refs_1_, bf16[128,1280]{1,0:T(8,128)(2,1)S(1)} %get-tuple-element.63.refs_5_.refs_6_.refs_2_, ...), custom_call_target="tpu_custom_call" | custom-call | flops 1 | bytes 11900000 | tf_op jit(solution)/shard_map/base_block/pallas_call | solution.py:28
  79.4 3.0 %collective-permute-done.21.refs_3_ = bf16[2,64,640]{2,1,0:T(8,128)(2,1)S(1)} collective-permute-done((bf16[2,64,640]{2,1,0:T(8,128)(2,1)S(1)}, bf16[2,64,640]{2,1,0:T(8,128)(2,1)S(1)}, u32[]{:S(2)}, u32[]{:S(2)}) %collective-permute-start.21) | collective-permute-done | bytes 163872 | tf_op jit(solution)/shard_map/ppermute | solution.py:347
  (43 shorter events, 16.9 us)
Async XLA Ops:
  1.3 10.4 %collective-permute-start.1 = (bf16[288,640]{1,0:T(8,128)(2,1)S(1)}, bf16[288,640]{1,0:T(8,128)(2,1)S(1)}, u32[]{:S(2)}, u32[]{:S(2)}) collective-permute-start(bf16[288,640]{1,0:T(8,128)(2,1)S(1)} %get-tuple-element.61), channel_id=1, source_target_pairs={{0,2},{1,3},{2,0},{3,1},{4,6},{5,7},{6,4},{7,5},{8,10},{9,11},{10,... | collective-permute-start | bytes 1105928 | tf_op jit(solution)/shard_map/ppermute | solution.py:347
  3.4 17.9 %collective-permute-start.2 = (bf16[288,640]{1,0:T(8,128)(2,1)S(1)}, bf16[288,640]{1,0:T(8,128)(2,1)S(1)}, u32[]{:S(2)}, u32[]{:S(2)}) collective-permute-start(bf16[288,640]{1,0:T(8,128)(2,1)S(1)} %get-tuple-element.62), channel_id=1, source_target_pairs={{0,3},{1,2},{2,1},{3,0},{4,7},{5,6},{6,5},{7,4},{8,11},{9,10},{10,... | collective-permute-start | bytes 1105928 | tf_op jit(solution)/shard_map/ppermute | solution.py:347
  5.3 16.0 %collective-permute-start = (bf16[288,640]{1,0:T(8,128)(2,1)S(1)}, bf16[288,640]{1,0:T(8,128)(2,1)S(1)}, u32[]{:S(2)}, u32[]{:S(2)}) collective-permute-start(bf16[288,640]{1,0:T(8,128)(2,1)S(1)} %get-tuple-element.60), channel_id=1, source_target_pairs={{0,1},{1,0},{2,3},{3,2},{4,5},{5,4},{6,7},{7,6},{8,9},{9,8},{10,11... | collective-permute-start | bytes 1105928 | tf_op jit(solution)/shard_map/ppermute | solution.py:353
  7.0 22.1 %collective-permute-start.4 = (bf16[256,640]{1,0:T(8,128)(2,1)S(1)}, bf16[256,640]{1,0:T(8,128)(2,1)S(1)}, u32[]{:S(2)}, u32[]{:S(2)}) collective-permute-start(bf16[256,640]{1,0:T(8,128)(2,1)S(1)} %get-tuple-element.66), channel_id=1, source_target_pairs={{0,3},{1,2},{2,1},{3,0},{4,7},{5,6},{6,5},{7,4},{8,11},{9,10},{10,... | collective-permute-start | bytes 983048 | tf_op jit(solution)/shard_map/ppermute | solution.py:347
  10.0 19.1 %collective-permute-start.12 = (bf16[256,640]{1,0:T(8,128)(2,1)S(1)}, bf16[256,640]{1,0:T(8,128)(2,1)S(1)}, u32[]{:S(2)}, u32[]{:S(2)}) collective-permute-start(bf16[256,640]{1,0:T(8,128)(2,1)S(1)} %get-tuple-element.82), channel_id=1, source_target_pairs={{0,1},{1,0},{2,3},{3,2},{4,5},{5,4},{6,7},{7,6},{8,9},{9,8},{10,11... | collective-permute-start | bytes 983048 | tf_op jit(solution)/shard_map/ppermute | solution.py:353
  21.4 20.2 %collective-permute-start.7 = (bf16[288,640]{1,0:T(8,128)(2,1)S(1)}, bf16[288,640]{1,0:T(8,128)(2,1)S(1)}, u32[]{:S(2)}, u32[]{:S(2)}) collective-permute-start(bf16[288,640]{1,0:T(8,128)(2,1)S(1)} %get-tuple-element.69), channel_id=1, source_target_pairs={{0,4},{1,5},{2,6},{3,7},{4,8},{5,9},{6,10},{7,11},{8,12},{9,13},{1... | collective-permute-start | bytes 1105928 | tf_op jit(solution)/shard_map/ppermute | solution.py:357
  23.3 20.4 %collective-permute-start.8 = (bf16[288,640]{1,0:T(8,128)(2,1)S(1)}, bf16[288,640]{1,0:T(8,128)(2,1)S(1)}, u32[]{:S(2)}, u32[]{:S(2)}) collective-permute-start(bf16[288,640]{1,0:T(8,128)(2,1)S(1)} %get-tuple-element.70), channel_id=1, source_target_pairs={{0,12},{1,13},{2,14},{3,15},{4,0},{5,1},{6,2},{7,3},{8,4},{9,5},{1... | collective-permute-start | bytes 1105928 | tf_op jit(solution)/shard_map/ppermute | solution.py:357
  25.4 9.4 %collective-permute-start.9 = (bf16[256,640]{1,0:T(8,128)(2,1)S(1)}, bf16[256,640]{1,0:T(8,128)(2,1)S(1)}, u32[]{:S(2)}, u32[]{:S(2)}) collective-permute-start(bf16[256,640]{1,0:T(8,128)(2,1)S(1)} %get-tuple-element.77), channel_id=1, source_target_pairs={{0,2},{1,3},{2,0},{3,1},{4,6},{5,7},{6,4},{7,5},{8,10},{9,11},{10,... | collective-permute-start | bytes 983048 | tf_op jit(solution)/shard_map/ppermute | solution.py:347
  29.0 15.1 %collective-permute-start.3 = (bf16[128,1280]{1,0:T(8,128)(2,1)S(1)}, bf16[128,1280]{1,0:T(8,128)(2,1)S(1)}, u32[]{:S(2)}, u32[]{:S(2)}) collective-permute-start(bf16[128,1280]{1,0:T(8,128)(2,1)S(1)} %get-tuple-element.64), channel_id=1, source_target_pairs={{0,1},{1,0},{2,3},{3,2},{4,5},{5,4},{6,7},{7,6},{8,9},{9,8},{10,11... | collective-permute-start | bytes 983048 | tf_op jit(solution)/shard_map/ppermute | solution.py:353
  29.1 9.5 %collective-permute-start.6 = (bf16[128,640]{1,0:T(8,128)(2,1)S(1)}, bf16[128,640]{1,0:T(8,128)(2,1)S(1)}, u32[]{:S(2)}, u32[]{:S(2)}) collective-permute-start(bf16[128,640]{1,0:T(8,128)(2,1)S(1)} %get-tuple-element.71), channel_id=1, source_target_pairs={{0,3},{1,2},{2,1},{3,0},{4,7},{5,6},{6,5},{7,4},{8,11},{9,10},{10,... | collective-permute-start | bytes 491528 | tf_op jit(solution)/shard_map/ppermute | solution.py:347
  34.8 20.0 %collective-permute-start.13 = (bf16[256,640]{1,0:T(8,128)(2,1)S(1)}, bf16[256,640]{1,0:T(8,128)(2,1)S(1)}, u32[]{:S(2)}, u32[]{:S(2)}) collective-permute-start(bf16[256,640]{1,0:T(8,128)(2,1)S(1)} %get-tuple-element.83), channel_id=1, source_target_pairs={{0,4},{1,5},{2,6},{3,7},{4,8},{5,9},{6,10},{7,11},{8,12},{9,13},{1... | collective-permute-start | bytes 983048 | tf_op jit(solution)/shard_map/ppermute | solution.py:357
  38.6 17.0 %collective-permute-start.14 = (bf16[256,640]{1,0:T(8,128)(2,1)S(1)}, bf16[256,640]{1,0:T(8,128)(2,1)S(1)}, u32[]{:S(2)}, u32[]{:S(2)}) collective-permute-start(bf16[256,640]{1,0:T(8,128)(2,1)S(1)} %get-tuple-element.84), channel_id=1, source_target_pairs={{0,12},{1,13},{2,14},{3,15},{4,0},{5,1},{6,2},{7,3},{8,4},{9,5},{1... | collective-permute-start | bytes 983048 | tf_op jit(solution)/shard_map/ppermute | solution.py:357
  41.6 6.0 %collective-permute-start.5 = (bf16[128,640]{1,0:T(8,128)(2,1)S(1)}, bf16[128,640]{1,0:T(8,128)(2,1)S(1)}, u32[]{:S(2)}, u32[]{:S(2)}) collective-permute-start(bf16[128,640]{1,0:T(8,128)(2,1)S(1)} %get-tuple-element.67), channel_id=1, source_target_pairs={{0,2},{1,3},{2,0},{3,1},{4,6},{5,7},{6,4},{7,5},{8,10},{9,11},{10,... | collective-permute-start | bytes 491528 | tf_op jit(solution)/shard_map/ppermute | solution.py:347
  43.7 7.9 %collective-permute-start.11 = (bf16[128,640]{1,0:T(8,128)(2,1)S(1)}, bf16[128,640]{1,0:T(8,128)(2,1)S(1)}, u32[]{:S(2)}, u32[]{:S(2)}) collective-permute-start(bf16[128,640]{1,0:T(8,128)(2,1)S(1)} %get-tuple-element.80), channel_id=1, source_target_pairs={{0,2},{1,3},{2,0},{3,1},{4,6},{5,7},{6,4},{7,5},{8,10},{9,11},{10,... | collective-permute-start | bytes 491528 | tf_op jit(solution)/shard_map/ppermute | solution.py:347
  44.2 10.7 %collective-permute-start.10 = (bf16[128,640]{1,0:T(8,128)(2,1)S(1)}, bf16[128,640]{1,0:T(8,128)(2,1)S(1)}, u32[]{:S(2)}, u32[]{:S(2)}) collective-permute-start(bf16[128,640]{1,0:T(8,128)(2,1)S(1)} %get-tuple-element.78), channel_id=1, source_target_pairs={{0,3},{1,2},{2,1},{3,0},{4,7},{5,6},{6,5},{7,4},{8,11},{9,10},{10,... | collective-permute-start | bytes 491528 | tf_op jit(solution)/shard_map/ppermute | solution.py:347
  51.5 11.3 %collective-permute-start.18 = (bf16[2,64,640]{2,1,0:T(8,128)(2,1)S(1)}, bf16[2,64,640]{2,1,0:T(8,128)(2,1)S(1)}, u32[]{:S(2)}, u32[]{:S(2)}) collective-permute-start(bf16[2,64,640]{2,1,0:T(8,128)(2,1)S(1)} %get-tuple-element.102), channel_id=1, source_target_pairs={{0,4},{1,5},{2,6},{3,7},{4,8},{5,9},{6,10},{7,11},{8,12},{9,13},{1... | collective-permute-start | bytes 491528 | tf_op jit(solution)/shard_map/ppermute | solution.py:357
  51.6 11.2 %collective-permute-start.19 = (bf16[2,64,640]{2,1,0:T(8,128)(2,1)S(1)}, bf16[2,64,640]{2,1,0:T(8,128)(2,1)S(1)}, u32[]{:S(2)}, u32[]{:S(2)}) collective-permute-start(bf16[2,64,640]{2,1,0:T(8,128)(2,1)S(1)} %get-tuple-element.103), channel_id=1, source_target_pairs={{0,12},{1,13},{2,14},{3,15},{4,0},{5,1},{6,2},{7,3},{8,4},{9,5},{1... | collective-permute-start | bytes 491528 | tf_op jit(solution)/shard_map/ppermute | solution.py:357
  59.5 10.2 %collective-permute-start.15 = (bf16[2,64,640]{2,1,0:T(8,128)(2,1)S(1)}, bf16[2,64,640]{2,1,0:T(8,128)(2,1)S(1)}, u32[]{:S(2)}, u32[]{:S(2)}) collective-permute-start(bf16[2,64,640]{2,1,0:T(8,128)(2,1)S(1)} %get-tuple-element.90), channel_id=1, source_target_pairs={{0,4},{1,5},{2,6},{3,7},{4,8},{5,9},{6,10},{7,11},{8,12},{9,13},{1... | collective-permute-start | bytes 491528 | tf_op jit(solution)/shard_map/ppermute | solution.py:357
  60.4 9.3 %collective-permute-start.16 = (bf16[2,64,640]{2,1,0:T(8,128)(2,1)S(1)}, bf16[2,64,640]{2,1,0:T(8,128)(2,1)S(1)}, u32[]{:S(2)}, u32[]{:S(2)}) collective-permute-start(bf16[2,64,640]{2,1,0:T(8,128)(2,1)S(1)} %get-tuple-element.91), channel_id=1, source_target_pairs={{0,12},{1,13},{2,14},{3,15},{4,0},{5,1},{6,2},{7,3},{8,4},{9,5},{1... | collective-permute-start | bytes 491528 | tf_op jit(solution)/shard_map/ppermute | solution.py:357
  64.9 6.9 %collective-permute-start.22 = (bf16[2,64,640]{2,1,0:T(8,128)(2,1)S(1)}, bf16[2,64,640]{2,1,0:T(8,128)(2,1)S(1)}, u32[]{:S(2)}, u32[]{:S(2)}) collective-permute-start(bf16[2,64,640]{2,1,0:T(8,128)(2,1)S(1)} %get-tuple-element.108), channel_id=1, source_target_pairs={{0,3},{1,2},{2,1},{3,0},{4,7},{5,6},{6,5},{7,4},{8,11},{9,10},{10,... | collective-permute-start | bytes 491528 | tf_op jit(solution)/shard_map/ppermute | solution.py:347
  67.0 8.6 %collective-permute-start.20 = (bf16[2,64,640]{2,1,0:T(8,128)(2,1)S(1)}, bf16[2,64,640]{2,1,0:T(8,128)(2,1)S(1)}, u32[]{:S(2)}, u32[]{:S(2)}) collective-permute-start(bf16[2,64,640]{2,1,0:T(8,128)(2,1)S(1)} %get-tuple-element.105), channel_id=1, source_target_pairs={{0,2},{1,3},{2,0},{3,1},{4,6},{5,7},{6,4},{7,5},{8,10},{9,11},{10,... | collective-permute-start | bytes 491528 | tf_op jit(solution)/shard_map/ppermute | solution.py:347
  69.7 8.8 %collective-permute-start.24 = (bf16[2,64,640]{2,1,0:T(8,128)(2,1)S(1)}, bf16[2,64,640]{2,1,0:T(8,128)(2,1)S(1)}, u32[]{:S(2)}, u32[]{:S(2)}) collective-permute-start(bf16[2,64,640]{2,1,0:T(8,128)(2,1)S(1)} %get-tuple-element.112), channel_id=1, source_target_pairs={{0,1},{1,0},{2,3},{3,2},{4,5},{5,4},{6,7},{7,6},{8,9},{9,8},{10,11... | collective-permute-start | bytes 491528 | tf_op jit(solution)/shard_map/ppermute | solution.py:353
  71.8 7.5 %collective-permute-start.23 = (bf16[2,64,640]{2,1,0:T(8,128)(2,1)S(1)}, bf16[2,64,640]{2,1,0:T(8,128)(2,1)S(1)}, u32[]{:S(2)}, u32[]{:S(2)}) collective-permute-start(bf16[2,64,640]{2,1,0:T(8,128)(2,1)S(1)} %get-tuple-element.109), channel_id=1, source_target_pairs={{0,3},{1,2},{2,1},{3,0},{4,7},{5,6},{6,5},{7,4},{8,11},{9,10},{10,... | collective-permute-start | bytes 491528 | tf_op jit(solution)/shard_map/ppermute | solution.py:347
  75.6 6.8 %collective-permute-start.21 = (bf16[2,64,640]{2,1,0:T(8,128)(2,1)S(1)}, bf16[2,64,640]{2,1,0:T(8,128)(2,1)S(1)}, u32[]{:S(2)}, u32[]{:S(2)}) collective-permute-start(bf16[2,64,640]{2,1,0:T(8,128)(2,1)S(1)} %get-tuple-element.106), channel_id=1, source_target_pairs={{0,2},{1,3},{2,0},{3,1},{4,6},{5,7},{6,4},{7,5},{8,10},{9,11},{10,... | collective-permute-start | bytes 491528 | tf_op jit(solution)/shard_map/ppermute | solution.py:347
  (1 other events, 4.3 us)
